TPU v7x, 32 devices: a whole 2x2x4 slice. The times are simulated.
32 devices in a mesh: row: 4 (over x, core), col: 8 (over z, y).
Axes of the slice: x: 2, y: 2, z: 4, core: 2. Of those that a mesh axis runs over, the one named last changes fastest.
Arguments:
- pixels: bfloat16 [16, 256, 6, 1536], P('row', 'col'), may hold values from -6 to 6
- timestamps: int32 [4, 8, 6], P('row', 'col'), may hold values from 0 to 365
- frame_count: int32 [4, 8], P('row', 'col'), may hold values from 1 to 6
- visible: int32 [16, 256, 6], P('row', 'col'), may hold values 0 or 1
- halo_reach: int32 [4, 8], P('row', 'col'), may hold values from 1 to 2
- w_patch: bfloat16 [1536, 768], replicated, may hold values from -0.15625 to 0.15625
- b_patch: bfloat16 [768], replicated, may hold values from -3 to 3
- gain_one: bfloat16 [768], replicated, may hold values from 0.099609375 to 1.8984375
- shift_one: bfloat16 [768], replicated, may hold values from -3 to 3
- w_qkv: bfloat16 [768, 2304], replicated, may hold values from -0.3125 to 0.3125
- b_query: bfloat16 [768], replicated, may hold values from -3 to 3
- b_value: bfloat16 [768], replicated, may hold values from -3 to 3
- w_out: bfloat16 [768, 768], replicated, may hold values from -1.75 to 1.75
- b_out: bfloat16 [768], replicated, may hold values from -3 to 3
- gain_two: bfloat16 [768], replicated, may hold values from 0.099609375 to 1.8984375
- shift_two: bfloat16 [768], replicated, may hold values from -3 to 3
- w_up: bfloat16 [768, 3072], replicated, may hold values from -0.21875 to 0.21875
- b_up: bfloat16 [3072], replicated, may hold values from -3 to 3
- w_down: bfloat16 [3072, 768], replicated, may hold values from -0.21875 to 0.21875
- b_down: bfloat16 [768], replicated, may hold values from -3 to 3
- w_dec: bfloat16 [768, 512], replicated, may hold values from -0.21875 to 0.21875
- b_dec: bfloat16 [512], replicated, may hold values from -3 to 3
- w_pix: bfloat16 [512, 1536], replicated, may hold values from -0.25 to 0.25
- b_pix: bfloat16 [1536], replicated, may hold values from -3 to 3
- cotangent: bfloat16 [16, 256, 6, 1536], P('row', 'col'), may hold values from -6 to 6
Outputs:
- pixel_out: bfloat16 [16, 256, 6, 1536], P('row', 'col')
- pixel_grad: bfloat16 [16, 256, 6, 1536], P('row', 'col')
- grad_w_patch: float32 [1536, 768], P('row')
- grad_b_patch: float32 [768], P('row')
- grad_gain_one: float32 [768], P('row')
- grad_shift_one: float32 [768], P('row')
- grad_w_qkv: float32 [768, 2304], P('row')
- grad_b_query: float32 [768], P('row')
- grad_b_value: float32 [768], P('row')
- grad_w_out: float32 [768, 768], P('row')
- grad_b_out: float32 [768], P('row')
- grad_gain_two: float32 [768], P('row')
- grad_shift_two: float32 [768], P('row')
- grad_w_up: float32 [768, 3072], P('row')
- grad_b_up: float32 [3072], P('row')
- grad_w_down: float32 [3072, 768], P('row')
- grad_b_down: float32 [768], P('row')
- grad_w_dec: float32 [768, 512], P('row')
- grad_b_dec: float32 [512], P('row')
- grad_w_pix: float32 [512, 1536], P('row')
- grad_b_pix: float32 [1536], P('row')
All inputs are finite; a program needn't handle non-finite values. No bound on the sum of `visible` on one device may be relied on, other than what follows from the above.
Results may differ from a plain program's by a relative error of at most 0.02.
Values may be sent and summed in bfloat16 or wider, within the bound.
No kernel may reach another device: no remote copies, remote signals or barrier semaphores. Data moves between devices by JAX's collectives and lax.ppermute only.
A program may use at most 192 MiB of HBM per device.

v0:
```python
import math

import jax
import jax.numpy as jnp
from jax import lax
from jax.sharding import PartitionSpec as P

HEAD_WIDTH = 64
HALO = 2


EPS = 1e-06
NEG_FILL = -1e30


def extended(cells, sides, width):
    for axis, dim in sides:
        count = lax.axis_size(axis)
        head = lax.slice_in_dim(cells, 0, width, axis=dim)
        tail = lax.slice_in_dim(cells, cells.shape[dim] - width, cells.shape[dim], axis=dim)
        cells = jnp.concatenate(
            [
                lax.ppermute(tail, axis, [(i, (i + 1) % count) for i in range(count)]),
                cells,
                lax.ppermute(head, axis, [((i + 1) % count, i) for i in range(count)]),
            ],
            axis=dim,
        )
    return cells


def shifted(value, axis, steps):
    count = lax.axis_size(axis)
    pairs = [(source, (source + steps) % count) for source in range(count)]
    return lax.ppermute(value, axis, pairs)


def sin_cos(places, width_part):
    half_width = width_part // 2
    frequency = 1.0 / 10000.0 ** (jnp.arange(half_width, dtype=jnp.float32) / half_width)
    angles = places[..., None] * frequency
    return jnp.concatenate([jnp.sin(angles), jnp.cos(angles)], -1)


def layer_norm(values, norm_gain, norm_shift):
    centre = values - jnp.mean(values, -1, keepdims=True)
    spread = jnp.mean(centre * centre, -1, keepdims=True)
    return centre * lax.rsqrt(spread + EPS) * norm_gain + norm_shift


def norm_backward(values, norm_gain, norm_shift, upstream):
    _, pull_back = jax.vjp(
        layer_norm, values, norm_gain.astype(jnp.float32), norm_shift.astype(jnp.float32)
    )
    return pull_back(upstream)


def gelu_exact(values):
    return jax.nn.gelu(values, approximate=False)


def mat_low(left_side, right_side):
    return jnp.dot(left_side, right_side, preferred_element_type=jnp.float32)


def outer_sum(left_side, right_side):
    return jnp.einsum("nd,ne->de", left_side, right_side, preferred_element_type=jnp.float32)


def times_transposed(left_side, right_side):
    return jnp.einsum("ne,de->nd", left_side, right_side, preferred_element_type=jnp.float32)


def column_sum(values):
    return jnp.sum(values, 0, dtype=jnp.float32)


def strip_distance(row_count, col_count, frame_total, halo_size):
    near_index = jnp.arange(halo_size, dtype=jnp.int32)
    upper_dist = jnp.broadcast_to(
        (halo_size - near_index)[:, None, None], (halo_size, col_count, frame_total)
    ).reshape(-1)
    lower_dist = jnp.broadcast_to(
        (near_index + 1)[:, None, None], (halo_size, col_count, frame_total)
    ).reshape(-1)
    left_dist = jnp.broadcast_to(
        (halo_size - near_index)[None, :, None], (row_count, halo_size, frame_total)
    ).reshape(-1)
    right_dist = jnp.broadcast_to(
        (near_index + 1)[None, :, None], (row_count, halo_size, frame_total)
    ).reshape(-1)
    return jnp.concatenate([upper_dist, lower_dist, left_dist, right_dist])


def cut_strips(padded, row_count, col_count):
    upper_strip = padded[:HALO, HALO : HALO + col_count]
    lower_strip = padded[HALO + row_count :, HALO : HALO + col_count]
    left_strip = padded[HALO : HALO + row_count, :HALO]
    right_strip = padded[HALO : HALO + row_count, HALO + col_count :]
    trailing = padded.shape[3:]
    return jnp.concatenate(
        [
            strip_piece.reshape((-1,) + trailing)
            for strip_piece in (upper_strip, lower_strip, left_strip, right_strip)
        ],
        0,
    )


def split_heads(array, group_count, head_group):
    row_count = array.shape[0]
    return jnp.moveaxis(array.reshape(row_count, group_count, head_group, HEAD_WIDTH), 1, 0)


def join_heads(array):
    moved = jnp.moveaxis(array, 0, 1)
    return moved.reshape(moved.shape[0], -1)


def group_forward(packed, allowed, score_scale):
    query_portion, key_portion, value_portion = packed
    attention_scores = (
        jnp.einsum("rex,sex->ers", query_portion, key_portion, preferred_element_type=jnp.float32)
        * score_scale
    )
    attention_scores = jnp.where(allowed[None], attention_scores, NEG_FILL)
    top_score = jnp.max(attention_scores, -1, keepdims=True)
    exp_scores = jnp.exp(attention_scores - top_score)
    totals = jnp.sum(exp_scores, -1, keepdims=True)
    reduced_probabilities = (exp_scores / totals).astype(jnp.bfloat16)
    mixed_heads_output = jnp.einsum(
        "bfq,qbp->fbp", reduced_probabilities, value_portion, preferred_element_type=jnp.float32
    )
    return (mixed_heads_output.astype(jnp.bfloat16), top_score[..., 0] + jnp.log(totals[..., 0]))


def group_backward(packed, allowed, score_scale):
    query_portion, key_portion, value_portion, partial_gradient, log_total = packed
    attention_scores = (
        jnp.einsum("rex,sex->ers", query_portion, key_portion, preferred_element_type=jnp.float32)
        * score_scale
    )
    attention_scores = jnp.where(allowed[None], attention_scores, NEG_FILL)
    attention_probabilities = jnp.exp(attention_scores - log_total[..., None])
    grad_probs = jnp.einsum(
        "rex,sex->ers", partial_gradient, value_portion, preferred_element_type=jnp.float32
    )
    row_delta = jnp.sum(attention_probabilities * grad_probs, -1, keepdims=True)
    score_gradient = (attention_probabilities * (grad_probs - row_delta)).astype(jnp.bfloat16)
    grad_query = (
        jnp.einsum("bfq,qbp->fbp", score_gradient, key_portion, preferred_element_type=jnp.float32)
        * score_scale
    )
    grad_key = (
        jnp.einsum(
            "tfo,ftc->otc", score_gradient, query_portion, preferred_element_type=jnp.float32
        )
        * score_scale
    )
    grad_value = jnp.einsum(
        "tfo,ftc->otc",
        attention_probabilities.astype(jnp.bfloat16),
        partial_gradient,
        preferred_element_type=jnp.float32,
    )
    return (
        grad_query.astype(jnp.bfloat16),
        grad_key.astype(jnp.bfloat16),
        grad_value.astype(jnp.bfloat16),
    )


def per_device(
    pixels,
    timestamps,
    frame_count,
    visible,
    halo_reach,
    w_patch,
    b_patch,
    gain_one,
    shift_one,
    w_qkv,
    b_query,
    b_value,
    w_out,
    b_out,
    gain_two,
    shift_two,
    w_up,
    b_up,
    w_down,
    b_down,
    w_dec,
    b_dec,
    w_pix,
    b_pix,
    cotangent,
):
    tile_rows, tile_cols, frames, pix_width = pixels.shape
    model_width = w_patch.shape[1]
    tokens = tile_rows * tile_cols * frames
    head_count = model_width // HEAD_WIDTH
    head_group = math.gcd(head_count, 2)
    group_count = head_count // head_group
    score_scale = HEAD_WIDTH ** (-0.5)
    row_places = (
        lax.axis_index("row") * tile_rows + jnp.arange(tile_rows, dtype=jnp.int32)
    ).astype(jnp.float32)
    col_places = (
        lax.axis_index("col") * tile_cols + jnp.arange(tile_cols, dtype=jnp.int32)
    ).astype(jnp.float32)
    time_part = sin_cos(timestamps[0, 0].astype(jnp.float32), model_width // 16 * 4)
    row_part = sin_cos(row_places, model_width // 16 * 6)
    col_part = sin_cos(col_places, model_width // 16 * 6)
    position = jnp.concatenate(
        [
            jnp.broadcast_to(
                time_part[None, None], (tile_rows, tile_cols, frames, time_part.shape[-1])
            ),
            jnp.broadcast_to(
                row_part[:, None, None], (tile_rows, tile_cols, frames, row_part.shape[-1])
            ),
            jnp.broadcast_to(
                col_part[None, :, None], (tile_rows, tile_cols, frames, col_part.shape[-1])
            ),
        ],
        -1,
    ).reshape(tokens, model_width)
    frame_index = jnp.arange(frames, dtype=jnp.int32)
    own_ok = ((frame_index[None, None, :] < frame_count[0, 0]) & (visible == 1)).astype(
        jnp.bfloat16
    )
    flat_pixels = pixels.reshape(tokens, pix_width)
    stream_one = mat_low(flat_pixels, w_patch) + b_patch.astype(jnp.float32) + position
    normed_one = layer_norm(
        stream_one, gain_one.astype(jnp.float32), shift_one.astype(jnp.float32)
    ).astype(jnp.bfloat16)
    grid_one = normed_one.reshape(tile_rows, tile_cols, frames, model_width)
    padded_rows, padded_ok = (
        extended(grid_one, (("row", 0), ("col", 1)), HALO),
        extended(own_ok, (("row", 0), ("col", 1)), HALO),
    )
    strip_rows = cut_strips(padded_rows, tile_rows, tile_cols)
    strip_ok = cut_strips(padded_ok, tile_rows, tile_cols)
    reach_ok = halo_reach[0, 0] >= strip_distance(tile_rows, tile_cols, frames, HALO)
    key_ok = jnp.concatenate([own_ok.reshape(-1) > 0.5, (strip_ok > 0.5) & reach_ok])
    key_count = key_ok.shape[0]
    allowed = key_ok[None, :] | (jnp.arange(key_count)[None, :] == jnp.arange(tokens)[:, None])
    qkv_own = mat_low(normed_one, w_qkv)
    kv_strip = mat_low(strip_rows, w_qkv[:, model_width:])
    query_rows = (qkv_own[:, :model_width] + b_query.astype(jnp.float32)).astype(jnp.bfloat16)
    key_rows = jnp.concatenate(
        [qkv_own[:, model_width : 2 * model_width], kv_strip[:, :model_width]], 0
    ).astype(jnp.bfloat16)
    value_rows = (
        jnp.concatenate([qkv_own[:, 2 * model_width :], kv_strip[:, model_width:]], 0)
        + b_value.astype(jnp.float32)
    ).astype(jnp.bfloat16)
    query_groups = split_heads(query_rows, group_count, head_group)
    key_groups = split_heads(key_rows, group_count, head_group)
    value_groups = split_heads(value_rows, group_count, head_group)
    mixed_groups, log_totals = lax.map(
        lambda packed: group_forward(packed, allowed, score_scale),
        (query_groups, key_groups, value_groups),
    )
    attended = join_heads(mixed_groups)
    stream_two = stream_one + mat_low(attended, w_out) + b_out.astype(jnp.float32)
    normed_two = layer_norm(
        stream_two, gain_two.astype(jnp.float32), shift_two.astype(jnp.float32)
    ).astype(jnp.bfloat16)
    hidden_pre = mat_low(normed_two, w_up) + b_up.astype(jnp.float32)
    hidden_act = gelu_exact(hidden_pre).astype(jnp.bfloat16)
    stream_out = stream_two + mat_low(hidden_act, w_down) + b_down.astype(jnp.float32)
    stream_low = stream_out.astype(jnp.bfloat16)
    decoded = (mat_low(stream_low, w_dec) + b_dec.astype(jnp.float32)).astype(jnp.bfloat16)
    pixel_out = (mat_low(decoded, w_pix) + b_pix.astype(jnp.float32)).astype(jnp.bfloat16)
    grad_pixels_out = cotangent.reshape(tokens, pix_width)
    grad_w_pix = outer_sum(decoded, grad_pixels_out)
    grad_b_pix = column_sum(grad_pixels_out)
    grad_dec = times_transposed(grad_pixels_out, w_pix).astype(jnp.bfloat16)
    grad_w_dec = outer_sum(stream_low, grad_dec)
    grad_b_dec = column_sum(grad_dec)
    grad_stream = times_transposed(grad_dec, w_dec)
    grad_mlp = grad_stream.astype(jnp.bfloat16)
    grad_w_down = outer_sum(hidden_act, grad_mlp)
    grad_b_down = column_sum(grad_mlp)
    grad_act = times_transposed(grad_mlp, w_down)
    _, gelu_pull = jax.vjp(gelu_exact, hidden_pre)
    grad_pre = gelu_pull(grad_act)[0].astype(jnp.bfloat16)
    grad_w_up = outer_sum(normed_two, grad_pre)
    grad_b_up = column_sum(grad_pre)
    grad_normed_two = times_transposed(grad_pre, w_up)
    back_two, grad_gain_two, grad_shift_two = norm_backward(
        stream_two, gain_two, shift_two, grad_normed_two
    )
    grad_stream_two = grad_stream + back_two
    grad_att = grad_stream_two.astype(jnp.bfloat16)
    grad_w_out = outer_sum(attended, grad_att)
    grad_b_out = column_sum(grad_att)
    grad_attended = times_transposed(grad_att, w_out).astype(jnp.bfloat16)
    grad_q_groups, grad_k_groups, grad_v_groups = lax.map(
        lambda packed: group_backward(packed, allowed, score_scale),
        (
            query_groups,
            key_groups,
            value_groups,
            split_heads(grad_attended, group_count, head_group),
            log_totals,
        ),
    )
    grad_query = join_heads(grad_q_groups)
    grad_keys = join_heads(grad_k_groups)
    grad_values = join_heads(grad_v_groups)
    grad_b_query = column_sum(grad_query)
    grad_b_value = column_sum(grad_values)
    own_grad = jnp.concatenate([grad_query, grad_keys[:tokens], grad_values[:tokens]], 1)
    strip_grad = jnp.concatenate([grad_keys[tokens:], grad_values[tokens:]], 1)
    grad_w_qkv = outer_sum(normed_one, own_grad)
    grad_w_qkv = grad_w_qkv.at[:, model_width:].add(outer_sum(strip_rows, strip_grad))
    grad_normed_one = times_transposed(own_grad, w_qkv)
    grad_strip = times_transposed(strip_grad, w_qkv[:, model_width:])
    upper_size = HALO * tile_cols * frames
    side_size = tile_rows * HALO * frames
    upper_back = grad_strip[:upper_size].reshape(HALO, tile_cols, frames, model_width)
    lower_back = grad_strip[upper_size : 2 * upper_size].reshape(
        HALO, tile_cols, frames, model_width
    )
    left_back = grad_strip[2 * upper_size : 2 * upper_size + side_size].reshape(
        tile_rows, HALO, frames, model_width
    )
    right_back = grad_strip[2 * upper_size + side_size :].reshape(
        tile_rows, HALO, frames, model_width
    )
    from_below = shifted(upper_back.astype(jnp.bfloat16), "row", -1).astype(upper_back.dtype)
    from_above = shifted(lower_back.astype(jnp.bfloat16), "row", 1).astype(lower_back.dtype)
    from_right = shifted(left_back.astype(jnp.bfloat16), "col", -1).astype(left_back.dtype)
    from_left = shifted(right_back.astype(jnp.bfloat16), "col", 1).astype(right_back.dtype)
    grad_grid = grad_normed_one.reshape(tile_rows, tile_cols, frames, model_width)
    grad_grid = grad_grid.at[tile_rows - HALO :].add(from_below)
    grad_grid = grad_grid.at[:HALO].add(from_above)
    grad_grid = grad_grid.at[:, tile_cols - HALO :].add(from_right)
    grad_grid = grad_grid.at[:, :HALO].add(from_left)
    back_one, grad_gain_one, grad_shift_one = norm_backward(
        stream_one, gain_one, shift_one, grad_grid.reshape(tokens, model_width)
    )
    grad_stream_one = grad_stream_two + back_one
    grad_b_patch = jnp.sum(grad_stream_one, 0)
    grad_emb = grad_stream_one.astype(jnp.bfloat16)
    grad_w_patch = outer_sum(flat_pixels, grad_emb)
    pixel_grad = (
        times_transposed(grad_emb, w_patch)
        .astype(jnp.bfloat16)
        .reshape(tile_rows, tile_cols, frames, pix_width)
    )
    (
        sum_w_patch,
        sum_b_patch,
        sum_gain_one,
        sum_shift_one,
        sum_w_qkv,
        sum_b_query,
        sum_b_value,
        sum_w_out,
        sum_b_out,
        sum_gain_two,
        sum_shift_two,
        sum_w_up,
        sum_b_up,
        sum_w_down,
        sum_b_down,
        sum_w_dec,
        sum_b_dec,
        sum_w_pix,
        sum_b_pix,
    ) = (
        lax.psum(grad_w_patch.astype(jnp.bfloat16), "col").astype(jnp.float32),
        lax.psum(grad_b_patch.astype(jnp.bfloat16), "col").astype(jnp.float32),
        lax.psum(grad_gain_one.astype(jnp.bfloat16), "col").astype(jnp.float32),
        lax.psum(grad_shift_one.astype(jnp.bfloat16), "col").astype(jnp.float32),
        lax.psum(grad_w_qkv.astype(jnp.bfloat16), "col").astype(jnp.float32),
        lax.psum(grad_b_query.astype(jnp.bfloat16), "col").astype(jnp.float32),
        lax.psum(grad_b_value.astype(jnp.bfloat16), "col").astype(jnp.float32),
        lax.psum(grad_w_out.astype(jnp.bfloat16), "col").astype(jnp.float32),
        lax.psum(grad_b_out.astype(jnp.bfloat16), "col").astype(jnp.float32),
        lax.psum(grad_gain_two.astype(jnp.bfloat16), "col").astype(jnp.float32),
        lax.psum(grad_shift_two.astype(jnp.bfloat16), "col").astype(jnp.float32),
        lax.psum(grad_w_up.astype(jnp.bfloat16), "col").astype(jnp.float32),
        lax.psum(grad_b_up.astype(jnp.bfloat16), "col").astype(jnp.float32),
        lax.psum(grad_w_down.astype(jnp.bfloat16), "col").astype(jnp.float32),
        lax.psum(grad_b_down.astype(jnp.bfloat16), "col").astype(jnp.float32),
        lax.psum(grad_w_dec.astype(jnp.bfloat16), "col").astype(jnp.float32),
        lax.psum(grad_b_dec.astype(jnp.bfloat16), "col").astype(jnp.float32),
        lax.psum(grad_w_pix.astype(jnp.bfloat16), "col").astype(jnp.float32),
        lax.psum(grad_b_pix.astype(jnp.bfloat16), "col").astype(jnp.float32),
    )
    shares = (
        lax.psum_scatter(
            sum_w_patch.astype(jnp.bfloat16), "row", scatter_dimension=0, tiled=True
        ).astype(jnp.float32),
        lax.psum_scatter(
            sum_b_patch.astype(jnp.bfloat16), "row", scatter_dimension=0, tiled=True
        ).astype(jnp.float32),
        lax.psum_scatter(
            sum_gain_one.astype(jnp.bfloat16), "row", scatter_dimension=0, tiled=True
        ).astype(jnp.float32),
        lax.psum_scatter(
            sum_shift_one.astype(jnp.bfloat16), "row", scatter_dimension=0, tiled=True
        ).astype(jnp.float32),
        lax.psum_scatter(
            sum_w_qkv.astype(jnp.bfloat16), "row", scatter_dimension=0, tiled=True
        ).astype(jnp.float32),
        lax.psum_scatter(
            sum_b_query.astype(jnp.bfloat16), "row", scatter_dimension=0, tiled=True
        ).astype(jnp.float32),
        lax.psum_scatter(
            sum_b_value.astype(jnp.bfloat16), "row", scatter_dimension=0, tiled=True
        ).astype(jnp.float32),
        lax.psum_scatter(
            sum_w_out.astype(jnp.bfloat16), "row", scatter_dimension=0, tiled=True
        ).astype(jnp.float32),
        lax.psum_scatter(
            sum_b_out.astype(jnp.bfloat16), "row", scatter_dimension=0, tiled=True
        ).astype(jnp.float32),
        lax.psum_scatter(
            sum_gain_two.astype(jnp.bfloat16), "row", scatter_dimension=0, tiled=True
        ).astype(jnp.float32),
        lax.psum_scatter(
            sum_shift_two.astype(jnp.bfloat16), "row", scatter_dimension=0, tiled=True
        ).astype(jnp.float32),
        lax.psum_scatter(
            sum_w_up.astype(jnp.bfloat16), "row", scatter_dimension=0, tiled=True
        ).astype(jnp.float32),
        lax.psum_scatter(
            sum_b_up.astype(jnp.bfloat16), "row", scatter_dimension=0, tiled=True
        ).astype(jnp.float32),
        lax.psum_scatter(
            sum_w_down.astype(jnp.bfloat16), "row", scatter_dimension=0, tiled=True
        ).astype(jnp.float32),
        lax.psum_scatter(
            sum_b_down.astype(jnp.bfloat16), "row", scatter_dimension=0, tiled=True
        ).astype(jnp.float32),
        lax.psum_scatter(
            sum_w_dec.astype(jnp.bfloat16), "row", scatter_dimension=0, tiled=True
        ).astype(jnp.float32),
        lax.psum_scatter(
            sum_b_dec.astype(jnp.bfloat16), "row", scatter_dimension=0, tiled=True
        ).astype(jnp.float32),
        lax.psum_scatter(
            sum_w_pix.astype(jnp.bfloat16), "row", scatter_dimension=0, tiled=True
        ).astype(jnp.float32),
        lax.psum_scatter(
            sum_b_pix.astype(jnp.bfloat16), "row", scatter_dimension=0, tiled=True
        ).astype(jnp.float32),
    )
    return (pixel_out.reshape(tile_rows, tile_cols, frames, pix_width), pixel_grad) + tuple(shares)


def solution(mesh):
    return jax.shard_map(
        per_device,
        mesh=mesh,
        in_specs=(
            P("row", "col", None, None),
            P("row", "col", None),
            P("row", "col"),
            P("row", "col", None),
            P("row", "col"),
            P(),
            P(),
            P(),
            P(),
            P(),
            P(),
            P(),
            P(),
            P(),
            P(),
            P(),
            P(),
            P(),
            P(),
            P(),
            P(),
            P(),
            P(),
            P(),
            P("row", "col", None, None),
        ),
        out_specs=(
            P("row", "col", None, None),
            P("row", "col", None, None),
            P("row", None),
            P("row"),
            P("row"),
            P("row"),
            P("row", None),
            P("row"),
            P("row"),
            P("row", None),
            P("row"),
            P("row"),
            P("row"),
            P("row", None),
            P("row"),
            P("row", None),
            P("row"),
            P("row", None),
            P("row"),
            P("row", None),
            P("row"),
        ),
        check_vma=False,
    )
```

profile of v0, /device:TPU:0, one launch (start us, length us, event | category | flops | bytes accessed | tf_op | source)
XLA Modules:
  0.0 1026.6 jit_solution(14599556640518600437)
XLA Ops:
  27.3 5.0 reshape.461
  54.4 5.0 reshape.479
  59.5 5.1 fusion.114
  110.8 5.1 collective-permute-start.3
  152.9 75.8 %while.33 = (s32[]{:T(128)}, bf16[6,768,2,64]{1,3,2,0:T(8,128)(2,1)}, f32[6,2,768]{2,1,0:T(2,128)}, bf16[6,1632,2,64]{1,3,2,0:T(8,128)(2,1)}, bf16[6,768,2,64]{1...) while((s32[]{:T(128)}, ...), condition=%wide.region_5.6_spmd.clone, body=%wide.region_2.5_spmd.clone.sunk | while | flops 674413056 | bytes 36392640 | solution.py:263
  159.9 5.1 fusion.178
  172.5 5.1 fusion.178
  185.1 5.1 fusion.178
  197.6 5.1 fusion.178
  210.2 5.1 fusion.178
  222.8 5.1 fusion.178
  233.3 28.1 %multiply_convert_fusion.1 = (bf16[768,3072]{1,0:T(8,128)(2,1)}, f32[768,3072]{1,0:T(8,128)}, f32[768,3072]{1,0:T(8,128)}) fusion(f32[3072]{0:T(1024)S(1)} %copy-done.60, bf16[768,3072]{1,0:T(8,128)(2,1)S(1)} %bitcast.200, f32[768,768]{1,0:T(8,128)S(1)} %get-tuple-element.395, f32[768]{0:T(1024)S(1)} %copy-done.65, f32[768]{0:T(1024)S(1)} %copy-done.56, ...), kind=kOutput, calls=%fused_computation.67 | convolution fusion | flops 3782541312 | bytes 30695424 | tf_op jit(solution)/shard_map/dot_general | solution.py:63
  261.4 13.8 %fusion.112 = (bf16[3072]{0:T(1024)(128)(2,1)}, bf16[768,3072]{1,0:T(8,128)(2,1)}) fusion(f32[768,3072]{1,0:T(8,128)} %get-tuple-element.360, bf16[3072,768]{1,0:T(8,128)(2,1)} %param.57, f32[768,768]{1,0:T(8,128)S(1)} %copy-done.8, f32[768,3072]{1,0:T(8,128)} %get-tuple-element.396, f32[3072]{0:T(1024)S(1)} %copy-done.60), kind=kOutput, calls=%fused_computation.201 | convolution fusion | flops 3662214144 | bytes 30689280 | tf_op jit(solution)/shard_map/ne,de->nd/dot_general | solution.py:71
  275.1 8.6 multiply_reduce_fusion.1
  290.0 203.0 %while.34 = (s32[]{:T(128)}, bf16[6,768,2,64]{1,3,2,0:T(8,128)(2,1)}, bf16[6,1632,2,64]{1,3,2,0:T(8,128)(2,1)}, bf16[6,1632,2,64]{1,3,2,0:T(8,128)(2,1)}, bf16[6...) while((s32[]{:T(128)}, ...), condition=%wide.region_12.13_spmd.clone, body=%wide.region_10.12_spmd.clone.sunk | while | flops 1630210560 | bytes 141021968 | solution.py:302
  294.8 7.1 multiply_reduce_fusion.8
  301.9 10.4 %multiply_convert_fusion.3 = bf16[2,768,1632]{1,2,0:T(8,128)(2,1)} fusion(f32[2,768,1632]{1,2,0:T(8,128)} %get-tuple-element.514, f32[2,768,1632]{1,2,0:T(8,128)} %copy-done.1, f32[2,768]{1,0:T(2,128)S(1)} %get-tuple-element.515), kind=kLoop, calls=%fused_computation.25.clone.1 | loop fusion | flops 7520256 | bytes 25073664 | tf_op jit(solution)/shard_map/while/body/eval_jaxpr/convert_element_type | solution.py:149
  312.3 6.5 fusion.191
  328.6 7.1 multiply_reduce_fusion.8
  335.7 10.4 %multiply_convert_fusion.3 = bf16[2,768,1632]{1,2,0:T(8,128)(2,1)} fusion(f32[2,768,1632]{1,2,0:T(8,128)} %get-tuple-element.514, f32[2,768,1632]{1,2,0:T(8,128)} %copy-done.1, f32[2,768]{1,0:T(2,128)S(1)} %get-tuple-element.515), kind=kLoop, calls=%fused_computation.25.clone.1 | loop fusion | flops 7520256 | bytes 25073664 | tf_op jit(solution)/shard_map/while/body/eval_jaxpr/convert_element_type | solution.py:149
  346.1 6.5 fusion.191
  362.4 7.1 multiply_reduce_fusion.8
  369.5 10.4 %multiply_convert_fusion.3 = bf16[2,768,1632]{1,2,0:T(8,128)(2,1)} fusion(f32[2,768,1632]{1,2,0:T(8,128)} %get-tuple-element.514, f32[2,768,1632]{1,2,0:T(8,128)} %copy-done.1, f32[2,768]{1,0:T(2,128)S(1)} %get-tuple-element.515), kind=kLoop, calls=%fused_computation.25.clone.1 | loop fusion | flops 7520256 | bytes 25073664 | tf_op jit(solution)/shard_map/while/body/eval_jaxpr/convert_element_type | solution.py:149
  379.9 6.5 fusion.191
  396.2 7.1 multiply_reduce_fusion.8
  403.3 10.4 %multiply_convert_fusion.3 = bf16[2,768,1632]{1,2,0:T(8,128)(2,1)} fusion(f32[2,768,1632]{1,2,0:T(8,128)} %get-tuple-element.514, f32[2,768,1632]{1,2,0:T(8,128)} %copy-done.1, f32[2,768]{1,0:T(2,128)S(1)} %get-tuple-element.515), kind=kLoop, calls=%fused_computation.25.clone.1 | loop fusion | flops 7520256 | bytes 25073664 | tf_op jit(solution)/shard_map/while/body/eval_jaxpr/convert_element_type | solution.py:149
  413.7 6.5 fusion.191
  429.9 7.1 multiply_reduce_fusion.8
  437.1 10.4 %multiply_convert_fusion.3 = bf16[2,768,1632]{1,2,0:T(8,128)(2,1)} fusion(f32[2,768,1632]{1,2,0:T(8,128)} %get-tuple-element.514, f32[2,768,1632]{1,2,0:T(8,128)} %copy-done.1, f32[2,768]{1,0:T(2,128)S(1)} %get-tuple-element.515), kind=kLoop, calls=%fused_computation.25.clone.1 | loop fusion | flops 7520256 | bytes 25073664 | tf_op jit(solution)/shard_map/while/body/eval_jaxpr/convert_element_type | solution.py:149
  447.5 6.5 fusion.191
  463.8 7.1 multiply_reduce_fusion.8
  470.9 10.4 %multiply_convert_fusion.3 = bf16[2,768,1632]{1,2,0:T(8,128)(2,1)} fusion(f32[2,768,1632]{1,2,0:T(8,128)} %get-tuple-element.514, f32[2,768,1632]{1,2,0:T(8,128)} %copy-done.1, f32[2,768]{1,0:T(2,128)S(1)} %get-tuple-element.515), kind=kLoop, calls=%fused_computation.25.clone.1 | loop fusion | flops 7520256 | bytes 25073664 | tf_op jit(solution)/shard_map/while/body/eval_jaxpr/convert_element_type | solution.py:149
  481.3 6.5 fusion.191
  513.2 5.6 fusion.80
  565.1 8.3 add_convert_fusion.2
  585.7 5.1 fusion.79
  596.7 9.2 convolution_convert_fusion
  606.6 9.7 convolution_convert_fusion.1
  618.7 7.1 reduce-scatter.18.cloned.1.call-done
  625.8 28.9 %reduce-scatter.12.cloned.1.call-done = bf16[192,768]{1,0:T(8,128)(2,1)} async-done(((bf16[768,768]{1,0:T(8,128)(2,1)}), bf16[192,768]{1,0:T(8,128)(2,1)}) %reduce-scatter.12.cloned.1.call-update) | async-done | bytes 294928 | tf_op jit(solution)/shard_map/reduce_scatter | solution.py:419
  654.7 31.3 %reduce-scatter.20.cloned.1.call-done = bf16[128,1536]{1,0:T(8,128)(2,1)} async-done(((bf16[512,1536]{1,0:T(8,128)(2,1)}), bf16[128,1536]{1,0:T(8,128)(2,1)}) %reduce-scatter.20.cloned.1.call-update) | async-done | bytes 393232 | tf_op jit(solution)/shard_map/reduce_scatter | solution.py:449
  686.0 42.9 %reduce-scatter.10.cloned.1.call-done = bf16[192,2304]{1,0:T(8,128)(2,1)} async-done(((bf16[768,2304]{1,0:T(8,128)(2,1)}), bf16[192,2304]{1,0:T(8,128)(2,1)}) %reduce-scatter.10.cloned.1.call-update) | async-done | bytes 884752 | tf_op jit(solution)/shard_map/reduce_scatter | solution.py:410
  728.9 50.4 %reduce-scatter.16.cloned.1.call-done = bf16[768,768]{1,0:T(8,128)(2,1)} async-done(((bf16[3072,768]{1,0:T(8,128)(2,1)}), bf16[768,768]{1,0:T(8,128)(2,1)}) %reduce-scatter.16.cloned.1.call-update) | async-done | bytes 1179664 | tf_op jit(solution)/shard_map/reduce_scatter | solution.py:437
  779.3 50.4 %reduce-scatter.14.cloned.1.call-done = bf16[192,3072]{1,0:T(8,128)(2,1)} async-done(((bf16[768,3072]{1,0:T(8,128)(2,1)}), bf16[192,3072]{1,0:T(8,128)(2,1)}) %reduce-scatter.14.cloned.1.call-update) | async-done | bytes 1179664 | tf_op jit(solution)/shard_map/reduce_scatter | solution.py:431
  840.0 5.0 reshape.478
  853.5 12.2 %all-reduce.14 = (bf16[768]{0:T(1024)(128)(2,1)}, bf16[768]{0:T(1024)(128)(2,1)}, bf16[768]{0:T(1024)(128)(2,1)}, bf16[768]{0:T(1024)(128)(2,1)}, bf16[768]{0:T(...) all-reduce(bf16[768]{0:T(1024)(128)(2,1)} %get-tuple-element.353, ...), channel_id=3, replica_groups=mesh['row'=4,'col'=8] {'row'}, use_global_device_ids=true, to_apply=%region_19.20.clone | all-reduce | flops 12032 | bytes 48128
  879.9 23.1 %all-reduce.12 = (bf16[192]{0:T(256)(128)(2,1)}, bf16[192]{0:T(256)(128)(2,1)}, bf16[192]{0:T(256)(128)(2,1)}, bf16[192]{0:T(256)(128)(2,1)}, bf16[192]{0:T(256)...) all-reduce(bf16[192]{0:T(256)(128)(2,1)} %dynamic-slice.41, ...), channel_id=1, replica_groups=mesh['row'=4,'col'=8] {'col'}, use_global_device_ids=true, to_apply=%region_18.19 | all-reduce | flops 3008 | bytes 12032 | tf_op jit(solution)/shard_map/psum | solution.py:378
  928.7 79.4 %all-reduce.17.cloned.1.call-done = (bf16[384,768]{0,1:T(8,128)(2,1)}, bf16[192,2304]{1,0:T(8,128)(2,1)}, bf16[192,768]{1,0:T(8,128)(2,1)}, bf16[192,3072]{1,0:T...) async-done(((bf16[384,768]{0,1:T(8,128)(2,1)}, bf16[192,2304]{1,0:T(8,128)(2,1)}, bf16[192,768]{1,0:T(8,128)(2,1)}, ...) | async-done | bytes 4718608 | tf_op jit(solution)/shard_map/psum | solution.py:377
  (474 shorter events, 393.2 us)
Async XLA Ops:
  7.2 25.1 %copy-start = (bf16[1536,768]{1,0:T(8,128)(2,1)S(1)}, bf16[1536,768]{1,0:T(8,128)(2,1)}, u32[]{:S(2)}) copy-start(bf16[1536,768]{1,0:T(8,128)(2,1)} %param.44) | copy-start | bytes 7077892
  7.2 609.4 %reduce-scatter.22.cloned.1.call-start = ((), (), s32[]{:S(2)}) async-start(), calls=%async_computation.13 | async-start | bytes 2949120
  10.0 81.5 %collective-permute-start.4 = (bf16[2,32,6]{1,0,2:T(2,128)(2,1)S(1)}, bf16[2,32,6]{1,0,2:T(2,128)(2,1)}, u32[]{:S(2)}, u32[]{:S(2)}) collective-permute-start(bf16[2,32,6]{1,0,2:T(2,128)(2,1)S(1)} %get-tuple-element.384), channel_id=1, source_target_pairs={{0,8},{8,16},{16,24},{24,0},{1,9},{9,17},{17,25},{25,1},{2,10},{10... | collective-permute-start | bytes 2312 | tf_op jit(solution)/shard_map/ppermute | solution.py:23
  10.5 82.5 %collective-permute-start.5 = (bf16[2,32,6]{1,0,2:T(2,128)(2,1)}, bf16[2,32,6]{1,0,2:T(2,128)(2,1)}, u32[]{:S(2)}, u32[]{:S(2)}) collective-permute-start(bf16[2,32,6]{1,0,2:T(2,128)(2,1)} %get-tuple-element.385), channel_id=1, source_target_pairs={{8,0},{16,8},{24,16},{0,24},{9,1},{17,9},{25,17},{1,25},{10,2},{18... | collective-permute-start | bytes 2312 | tf_op jit(solution)/shard_map/ppermute | solution.py:25
  13.8 24.3 %copy-start.46 = (f32[768]{0:T(1024)}, f32[768]{0:T(1024)S(1)}, u32[]{:S(2)}) copy-start(f32[768]{0:T(1024)S(1)} %convert_element_type.325) | copy-start | bytes 9220
  38.6 34.2 %copy-start.11 = (bf16[768,768]{1,0:T(8,128)(2,1)}, bf16[768,768]{1,0:T(8,128)(2,1)S(1)}, u32[]{:S(2)}) copy-start(bf16[768,768]{1,0:T(8,128)(2,1)S(1)} %add_convert_fusion.4) | copy-start | bytes 3538948
  41.9 7.9 copy-start.70
  44.0 63.7 %collective-permute-start.1 = (bf16[2,32,6,768]{3,1,2,0:T(8,128)(2,1)}, bf16[2,32,6,768]{3,1,2,0:T(8,128)(2,1)}, u32[]{:S(2)}, u32[]{:S(2)}) collective-permute-start(bf16[2,32,6,768]{3,1,2,0:T(8,128)(2,1)} %copy.77), channel_id=1, source_target_pairs={{8,0},{16,8},{24,16},{0,24},{9,1},{17,9},{25,17},{1,25},{10,2},{18... | collective-permute-start | bytes 1769480 | tf_op jit(solution)/shard_map/ppermute | solution.py:25
  48.8 56.5 %collective-permute-start = (bf16[2,32,6,768]{3,1,2,0:T(8,128)(2,1)}, bf16[2,32,6,768]{3,1,2,0:T(8,128)(2,1)}, u32[]{:S(2)}, u32[]{:S(2)}) collective-permute-start(bf16[2,32,6,768]{3,1,2,0:T(8,128)(2,1)} %copy.75), channel_id=1, source_target_pairs={{0,8},{8,16},{16,24},{24,0},{1,9},{9,17},{17,25},{25,1},{2,10},{10... | collective-permute-start | bytes 1769480 | tf_op jit(solution)/shard_map/ppermute | solution.py:23
  72.8 8.7 copy-start.63
  74.2 6.7 copy-start.75
  94.4 7.2 collective-permute-start.6
  98.0 4.7 collective-permute-start.7
  110.8 13.2 %collective-permute-start.3 = (bf16[8,2,6,768]{3,2,1,0:T(8,128)(2,1)}, bf16[8,2,6,768]{3,2,1,0:T(8,128)(2,1)}, u32[]{:S(2)}, u32[]{:S(2)}) collective-permute-start(bf16[8,2,6,768]{3,2,1,0:T(8,128)(2,1)} %get-tuple-element.369), channel_id=1, source_target_pairs={{1,0},{2,1},{3,2},{4,3},{5,4},{6,5},{7,6},{0,7},{9,8},{10,9},{11,1... | collective-permute-start | bytes 442376 | tf_op jit(solution)/shard_map/ppermute | solution.py:25
  115.9 11.2 %collective-permute-start.2 = (bf16[8,2,6,768]{3,2,1,0:T(8,128)(2,1)}, bf16[8,2,6,768]{3,2,1,0:T(8,128)(2,1)}, u32[]{:S(2)}, u32[]{:S(2)}) collective-permute-start(bf16[8,2,6,768]{3,2,1,0:T(8,128)(2,1)} %get-tuple-element.370), channel_id=1, source_target_pairs={{0,1},{1,2},{2,3},{3,4},{4,5},{5,6},{6,7},{7,0},{8,9},{9,10},{10,1... | collective-permute-start | bytes 442376 | tf_op jit(solution)/shard_map/ppermute | solution.py:23
  142.9 6.8 copy-start.55
  152.9 75.8 %copy-start.67 = (f32[768]{0:T(1024)S(1)}, f32[768]{0:T(1024)}, u32[]{:S(2)}) copy-start(f32[768]{0:T(1024)} %convert_element_type.332) | copy-start | bytes 9220
  232.5 51.3 %copy-start.14 = (f32[768,768]{1,0:T(8,128)}, f32[768,768]{1,0:T(8,128)S(1)}, u32[]{:S(2)}) copy-start(f32[768,768]{1,0:T(8,128)S(1)} %get-tuple-element.395) | copy-start | bytes 7077892
  232.5 51.2 %copy-start.51 = (f32[768]{0:T(1024)}, f32[768]{0:T(1024)S(1)}, u32[]{:S(2)}) copy-start(f32[768]{0:T(1024)S(1)} %broadcast_multiply_fusion) | copy-start | bytes 9220
  233.3 50.5 %copy-start.58 = (f32[768]{0:T(1024)}, f32[768]{0:T(1024)S(1)}, u32[]{:S(2)}) copy-start(f32[768]{0:T(1024)S(1)} %fusion.87) | copy-start | bytes 9220
  233.3 28.1 %copy-start.8 = (f32[768,768]{1,0:T(8,128)S(1)}, f32[768,768]{1,0:T(8,128)}, u32[]{:S(2)}) copy-start(f32[768,768]{1,0:T(8,128)} %fusion.115) | copy-start | bytes 7077892
  294.8 7.1 copy-start.1
  312.3 6.5 copy-start.2
  328.5 7.1 copy-start.1
  346.1 6.5 copy-start.2
  362.4 7.1 copy-start.1
  379.9 6.5 copy-start.2
  396.2 7.1 copy-start.1
  429.9 7.1 copy-start.1
  447.5 6.5 copy-start.2
  463.8 7.1 copy-start.1
  481.3 6.5 copy-start.2
  505.2 8.0 copy-start.21
  507.4 30.4 %collective-permute-start.9 = (bf16[2,32,6,768]{3,1,2,0:T(8,128)(2,1)}, bf16[2,32,6,768]{3,1,2,0:T(8,128)(2,1)}, u32[]{:S(2)}, u32[]{:S(2)}) collective-permute-start(bf16[2,32,6,768]{3,1,2,0:T(8,128)(2,1)} %copy.94), channel_id=1, source_target_pairs={{0,8},{8,16},{16,24},{24,0},{1,9},{9,17},{17,25},{25,1},{2,10},{10... | collective-permute-start | bytes 1769480 | tf_op jit(solution)/shard_map/ppermute | solution.py:35
  511.5 23.2 %collective-permute-start.8 = (bf16[2,32,6,768]{3,1,2,0:T(8,128)(2,1)}, bf16[2,32,6,768]{3,1,2,0:T(8,128)(2,1)}, u32[]{:S(2)}, u32[]{:S(2)}) collective-permute-start(bf16[2,32,6,768]{3,1,2,0:T(8,128)(2,1)} %copy.92), channel_id=1, source_target_pairs={{0,24},{8,0},{16,8},{24,16},{1,25},{9,1},{17,9},{25,17},{2,26},{10... | collective-permute-start | bytes 1769480 | tf_op jit(solution)/shard_map/ppermute | solution.py:35
  520.3 13.1 %slice-start = ((f32[768,768]{1,0:T(8,128)}), f32[384,768]{1,0:T(8,128)S(1)}, s32[]{:S(2)}) async-start(f32[768,768]{1,0:T(8,128)} %copy-done.19), calls=%async_computation.15 | async-start | bytes 2359296 | tf_op jit(solution)/shard_map/slice.158
  528.7 12.3 %collective-permute-start.10 = (bf16[4,2,6,768]{3,2,1,0:T(8,128)(2,1)}, bf16[4,2,6,768]{3,2,1,0:T(8,128)(2,1)}, u32[]{:S(2)}, u32[]{:S(2)}) collective-permute-start(bf16[4,2,6,768]{3,2,1,0:T(8,128)(2,1)} %convert_element_type.353), channel_id=1, source_target_pairs={{0,7},{1,0},{2,1},{3,2},{4,3},{5,4},{6,5},{7,6},{8,15},{9,8},{10,9... | collective-permute-start | bytes 221192 | tf_op jit(solution)/shard_map/ppermute | solution.py:35
  533.4 9.3 collective-permute-start.11
  564.5 61.4 %reduce-scatter.18.cloned.1.call-start = ((), (), s32[]{:S(2)}) async-start(), calls=%async_computation.11 | async-start | bytes 983040 | tf_op jit(solution)/shard_map/reduce_scatter | solution.py:443
  565.1 9.3 copy-start.41
  576.2 78.6 %reduce-scatter.12.cloned.1.call-start = ((), (), s32[]{:S(2)}) async-start(), calls=%async_computation.8 | async-start | bytes 1474560 | tf_op jit(solution)/shard_map/reduce_scatter | solution.py:419
  579.6 106.4 %reduce-scatter.20.cloned.1.call-start = ((), (), s32[]{:S(2)}) async-start(), calls=%async_computation.12 | async-start | bytes 1966080 | tf_op jit(solution)/shard_map/reduce_scatter | solution.py:449
  585.6 143.3 %reduce-scatter.10.cloned.1.call-start = ((), (), s32[]{:S(2)}) async-start(), calls=%async_computation.7 | async-start | bytes 4423680 | tf_op jit(solution)/shard_map/reduce_scatter | solution.py:410
  596.2 183.1 %reduce-scatter.16.cloned.1.call-start = ((), (), s32[]{:S(2)}) async-start(), calls=%async_computation.10 | async-start | bytes 5898240 | tf_op jit(solution)/shard_map/reduce_scatter | solution.py:437
  606.0 223.8 %reduce-scatter.14.cloned.1.call-start = ((), (), s32[]{:S(2)}) async-start(), calls=%async_computation.9 | async-start | bytes 5898240 | tf_op jit(solution)/shard_map/reduce_scatter | solution.py:431
  616.3 391.7 %all-reduce.17.cloned.1.call-start = ((), (), s32[]{:S(2)}) async-start(), calls=%async_computation.14 | async-start | bytes 9437184 | tf_op jit(solution)/shard_map/psum | solution.py:377
  850.6 65.7 %copy-start.34 = (bf16[768,768]{1,0:T(8,128)(2,1)S(1)}, bf16[768,768]{1,0:T(8,128)(2,1)}, u32[]{:S(2)}) copy-start(bf16[768,768]{1,0:T(8,128)(2,1)} %copy-done.33) | copy-start | bytes 3538948
  1008.0 6.9 copy-start.36
  (67 other events, 200.0 us)
Sparse Core Ops, SparseCore 0:
  564.6 34.6 reduce-scatter.21
  602.5 23.2 reduce-scatter.17
  629.0 25.7 reduce-scatter.11
  657.9 28.1 reduce-scatter.19
  688.5 40.4 reduce-scatter.9
  731.5 47.8 reduce-scatter.15
  781.9 47.8 reduce-scatter.13
  835.5 172.5 all-reduce.16
where the time goes:
time: 1040 us; the launch traced here: 1030 us
  matrix products  317 us (30%)
  waiting for transfers between devices  291 us (28%)
  local copies, waits for them, and re-layouts  177 us (17%)
  other arithmetic  165 us (16%)
  blocking collectives  35.3 us (3%)
  starting transfers between devices  21.6 us (2%)
  between operations  19.3 us (2%)
    psum x1, waiting for transfers between devices, per_device(): lax.psum(grad_w_patch.astype(jnp.bfloat16), 'col').astype(jnp.float32)  79.4 us
    unnamed x189, local copies, waits for them, and re-layouts  62.8 us
    convert_element_type x6, other arithmetic, group_backward(): (attention_probabilities * (grad_probs - row_delta)).astype(jnp.bfloat16)  62.3 us
    dot_general x8, matrix products, mat_low(): return jnp.dot(left_side, right_side, preferred_element_type=jnp.float32)  60.6 us
    reduce_scatter x1, waiting for transfers between devices, per_device(): lax.psum_scatter(sum_w_down.astype(jnp.bfloat16), 'row', scatter_dimensio...  50.4 us
    reduce_scatter x1, waiting for transfers between devices, per_device(): lax.psum_scatter(sum_w_up.astype(jnp.bfloat16), 'row', scatter_dimension=...  50.4 us
    reduce_scatter x1, waiting for transfers between devices, per_device(): lax.psum_scatter(sum_w_qkv.astype(jnp.bfloat16), 'row', scatter_dimension...  42.9 us
    dot_general x6, matrix products, group_backward(): jnp.einsum('rex,sex->ers', query_portion, key_portion, preferred_element_...  42.8 us
  transfers between devices with their start and end apart: 20, of which 9 were waited for; matrix products, arithmetic and copies ran while one was open for 23% of the time, Pallas kernels for 0%

commit v1 on v0

v1 whole, which is shorter than its diff:
```python
import functools
import math

import jax
import jax.numpy as jnp
from jax import lax
from jax.experimental import pallas as pl
from jax.experimental.pallas import tpu as pltpu
from jax.sharding import PartitionSpec as P

HEAD_WIDTH = 64
HALO = 2
EPS = 1e-06
NEG_FILL = -1e30
BLOCK = 256
LANES = 128
SCALE = HEAD_WIDTH**-0.5
LOG_SCALE = SCALE * math.log2(math.e)
F32 = jnp.float32
BF16 = jnp.bfloat16


def sin_cos(places, width_part):
    half_width = width_part // 2
    frequency = 1.0 / 10000.0 ** (jnp.arange(half_width, dtype=F32) / half_width)
    angles = places[..., None] * frequency
    return jnp.concatenate([jnp.sin(angles), jnp.cos(angles)], -1)


def layer_norm(values, norm_gain, norm_shift):
    centre = values - jnp.mean(values, -1, keepdims=True)
    spread = jnp.mean(centre * centre, -1, keepdims=True)
    return centre * lax.rsqrt(spread + EPS) * norm_gain + norm_shift


def norm_backward(values, norm_gain, norm_shift, upstream):
    _, pull_back = jax.vjp(layer_norm, values, norm_gain.astype(F32), norm_shift.astype(F32))
    return pull_back(upstream)


def gelu_exact(values):
    return jax.nn.gelu(values, approximate=False)


def mat_low(left_side, right_side):
    return jnp.dot(left_side, right_side, preferred_element_type=F32)


def outer_sum(left_side, right_side):
    return jnp.einsum("nd,ne->de", left_side, right_side, preferred_element_type=F32)


def times_transposed(left_side, right_side):
    return jnp.einsum("ne,de->nd", left_side, right_side, preferred_element_type=F32)


def column_sum(values):
    return jnp.sum(values, 0, dtype=F32)


def dot_last(a, b):
    return lax.dot_general(a, b, (((1,), (1,)), ((), ())), preferred_element_type=F32)


def dot_plain(a, b):
    return lax.dot_general(a, b, (((1,), (0,)), ((), ())), preferred_element_type=F32)


def one_head(pair, head):
    lane = lax.broadcasted_iota(jnp.int32, pair.shape, 1)
    keep = (lane < HEAD_WIDTH) if head == 0 else (lane >= HEAD_WIDTH)
    return jnp.where(keep, pair, jnp.zeros_like(pair))


def diagonal(size):
    rows = lax.broadcasted_iota(jnp.int32, (size, size), 0)
    return rows == lax.broadcasted_iota(jnp.int32, (size, size), 1)


def attend_kernel(q_ref, k_ref, v_ref, bias_ref, out_ref, log_ref, s_ref):
    tokens = q_ref.shape[0]
    eye = diagonal(BLOCK)
    lane = lax.broadcasted_iota(jnp.int32, (BLOCK, LANES), 1)

    def step(i, carry):
        at = pl.multiple_of(i * BLOCK, BLOCK)
        q = q_ref[pl.ds(at, BLOCK), :]
        mixed = []
        for head in range(2):
            q_head = one_head(q, head)
            s_ref[head] = dot_last(q_head, k_ref[...]) + bias_ref[...]
            own = dot_last(q_head, k_ref[pl.ds(at, BLOCK), :])
            s_ref[head, :, pl.ds(at, BLOCK)] = jnp.where(
                eye, own, own + bias_ref[:, pl.ds(at, BLOCK)]
            )
            scores = s_ref[head]
            top = jnp.max(scores, axis=1, keepdims=True)
            weights = jnp.exp2(scores * LOG_SCALE - top * LOG_SCALE)
            total = jnp.sum(weights, axis=1, keepdims=True)
            mixed.append(dot_plain(weights.astype(BF16), v_ref[...]) / total)
            log_ref[0, head, pl.ds(at, BLOCK)] = (top * LOG_SCALE + jnp.log2(total))[:, 0]
        out_ref[pl.ds(at, BLOCK), :] = jnp.where(lane < HEAD_WIDTH, mixed[0], mixed[1]).astype(
            out_ref.dtype
        )
        return carry

    lax.fori_loop(0, tokens // BLOCK, step, 0)


def attend(q, k, v, bias):
    tokens, width = q.shape
    keys = k.shape[0]
    pairs = width // LANES
    return pl.pallas_call(
        attend_kernel,
        grid=(pairs,),
        in_specs=[
            pl.BlockSpec((tokens, LANES), lambda p: (0, p)),
            pl.BlockSpec((keys, LANES), lambda p: (0, p)),
            pl.BlockSpec((keys, LANES), lambda p: (0, p)),
            pl.BlockSpec((1, keys), lambda p: (0, 0)),
        ],
        out_specs=[
            pl.BlockSpec((tokens, LANES), lambda p: (0, p)),
            pl.BlockSpec((1, 2, tokens), lambda p: (p, 0, 0)),
        ],
        out_shape=[
            jax.ShapeDtypeStruct((tokens, width), BF16),
            jax.ShapeDtypeStruct((pairs, 2, tokens), F32),
        ],
        scratch_shapes=[pltpu.VMEM((2, BLOCK, keys), F32)],
        compiler_params=pltpu.CompilerParams(vmem_limit_bytes=48 << 20),
        cost_estimate=pl.CostEstimate(
            flops=16 * tokens * keys * width, bytes_accessed=8 << 20, transcendentals=0
        ),
        name="attend",
    )(q, k, v, bias)


def attend_back_kernel(
    q_ref, k_ref, v_ref, do_ref, o_ref, log_ref, bias_ref, dq_ref, dk_ref, dv_ref, kt_ref, dk_sum, dv_sum
):
    tokens = q_ref.shape[0]
    kt_ref[...] = k_ref[...].T
    eye = diagonal(BLOCK)
    dk_sum[...] = jnp.zeros_like(dk_sum)
    dv_sum[...] = jnp.zeros_like(dv_sum)

    def step(i, carry):
        at = pl.multiple_of(i * BLOCK, BLOCK)
        q = q_ref[pl.ds(at, BLOCK), :]
        do = do_ref[pl.ds(at, BLOCK), :]
        product = (do.astype(F32) * o_ref[pl.ds(at, BLOCK), :].astype(F32)).T
        parts = []
        for head in range(2):
            delta = jnp.sum(
                product[head * HEAD_WIDTH : (head + 1) * HEAD_WIDTH], axis=0, keepdims=True
            )
            q_head = one_head(q, head)
            do_head = one_head(do, head)
            log_total = log_ref[0, pl.ds(head, 1), pl.ds(at, BLOCK)]
            scores = dot_last(k_ref[...], q_head) + bias_ref[...]
            weights = jnp.exp2(scores * LOG_SCALE - log_total)
            back = dot_last(v_ref[...], do_head)
            grad = (weights * (back - delta)).astype(BF16)
            own_scores = dot_last(k_ref[pl.ds(at, BLOCK), :], q_head)
            own = jnp.where(
                eye & (bias_ref[pl.ds(at, BLOCK), :] < 0),
                jnp.exp2(own_scores * LOG_SCALE - log_total),
                0.0,
            )
            own_back = dot_last(v_ref[pl.ds(at, BLOCK), :], do_head)
            own_grad = (own * (own_back - delta)).astype(BF16)
            dv_sum[...] += dot_plain(weights.astype(BF16), do_head)
            dv_sum[pl.ds(at, BLOCK), :] += dot_plain(own.astype(BF16), do_head)
            dk_sum[...] += dot_plain(grad, q_head)
            dk_sum[pl.ds(at, BLOCK), :] += dot_plain(own_grad, q_head)
            parts.append(
                dot_plain(kt_ref[...], grad) + dot_plain(kt_ref[:, pl.ds(at, BLOCK)], own_grad)
            )
        joined = jnp.concatenate([parts[0][:HEAD_WIDTH], parts[1][HEAD_WIDTH:]], axis=0)
        dq_ref[pl.ds(at, BLOCK), :] = (joined.T * SCALE).astype(BF16)
        return carry

    lax.fori_loop(0, tokens // BLOCK, step, 0)
    dk_ref[...] = (dk_sum[...] * SCALE).astype(BF16)
    dv_ref[...] = dv_sum[...].astype(BF16)


def attend_back(q, k, v, do, o, log_total, bias):
    tokens, width = q.shape
    keys = k.shape[0]
    pairs = width // LANES
    own = pl.BlockSpec((tokens, LANES), lambda p: (0, p))
    wide = pl.BlockSpec((keys, LANES), lambda p: (0, p))
    return pl.pallas_call(
        attend_back_kernel,
        grid=(pairs,),
        in_specs=[
            own,
            wide,
            wide,
            own,
            own,
            pl.BlockSpec((1, 2, tokens), lambda p: (p, 0, 0)),
            pl.BlockSpec((keys, 1), lambda p: (0, 0)),
        ],
        out_specs=[own, wide, wide],
        out_shape=[
            jax.ShapeDtypeStruct((tokens, width), BF16),
            jax.ShapeDtypeStruct((keys, width), BF16),
            jax.ShapeDtypeStruct((keys, width), BF16),
        ],
        scratch_shapes=[
            pltpu.VMEM((LANES, keys), BF16),
            pltpu.VMEM((keys, LANES), F32),
            pltpu.VMEM((keys, LANES), F32),
        ],
        compiler_params=pltpu.CompilerParams(vmem_limit_bytes=48 << 20),
        cost_estimate=pl.CostEstimate(
            flops=24 * tokens * keys * width, bytes_accessed=16 << 20, transcendentals=0
        ),
        name="attend_back",
    )(q, k, v, do, o, log_total, bias)


def swap(value, axis, stride):
    count = lax.axis_size(axis)
    return lax.ppermute(value, axis, [(i, i ^ stride) for i in range(count)])


def rotate(value, axis, steps):
    count = lax.axis_size(axis)
    return lax.ppermute(value, axis, [(i, (i + steps) % count) for i in range(count)])


def pick(values, index):
    return lax.dynamic_index_in_dim(values, index, 0, keepdims=False)


def add(a, b):
    return (a.astype(F32) + b.astype(F32)).astype(BF16)


def reduce_quarters(quarters):
    row_total = lax.axis_size("row")
    col_total = lax.axis_size("col")
    rows, width = quarters.shape[1:]
    granule = 8 * col_total
    padded = -(-rows // granule) * granule
    if padded != rows:
        quarters = jnp.pad(quarters, ((0, 0), (0, padded - rows), (0, 0)))
    row_at = lax.axis_index("row")
    held = quarters
    stride = 1
    while stride < row_total:
        count = held.shape[0]
        bit = (row_at // stride) % 2
        split = held.reshape((count // 2, 2) + held.shape[1:])
        sent = lax.dynamic_index_in_dim(split, 1 - bit, 1, keepdims=False)
        kept = lax.dynamic_index_in_dim(split, bit, 1, keepdims=False)
        held = add(kept, swap(sent, "row", stride))
        stride *= 2
    part = held[0]
    col_at = lax.axis_index("col")
    stride = 1
    while stride < col_total:
        bit = (col_at // stride) % 2
        split = part.reshape(2, part.shape[0] // 2, width)
        part = add(pick(split, bit), swap(pick(split, 1 - bit), "col", stride))
        stride *= 2
    while stride > 1:
        stride //= 2
        bit = (col_at // stride) % 2
        other = swap(part, "col", stride)
        first = jnp.where(bit == 0, part, other)
        second = jnp.where(bit == 0, other, part)
        part = jnp.concatenate([first, second], 0)
    return part[:rows]


def pack_columns(grad, width):
    rows, cols = grad.shape
    quarter = grad.astype(BF16).reshape(4, rows // 4, cols)
    return jnp.concatenate(
        [quarter[:, :, at : at + width] for at in range(0, cols, width)], 1
    )


def unpack_columns(packed, cols):
    width = packed.shape[1]
    count = cols // width
    rows = packed.shape[0] // count
    return jnp.concatenate([packed[i * rows : (i + 1) * rows] for i in range(count)], 1)


def per_device(
    pixels,
    timestamps,
    frame_count,
    visible,
    halo_reach,
    w_patch,
    b_patch,
    gain_one,
    shift_one,
    w_qkv,
    b_query,
    b_value,
    w_out,
    b_out,
    gain_two,
    shift_two,
    w_up,
    b_up,
    w_down,
    b_down,
    w_dec,
    b_dec,
    w_pix,
    b_pix,
    cotangent,
):
    tile_rows, tile_cols, frames, pix_width = pixels.shape
    model_width = w_patch.shape[1]
    tokens = tile_rows * tile_cols * frames
    row_places = (
        lax.axis_index("row") * tile_rows + jnp.arange(tile_rows, dtype=jnp.int32)
    ).astype(F32)
    col_places = (
        lax.axis_index("col") * tile_cols + jnp.arange(tile_cols, dtype=jnp.int32)
    ).astype(F32)
    time_part = sin_cos(timestamps[0, 0].astype(F32), model_width // 16 * 4)
    row_part = sin_cos(row_places, model_width // 16 * 6)
    col_part = sin_cos(col_places, model_width // 16 * 6)
    grid_shape = (tile_rows, frames, tile_cols)
    position = jnp.concatenate(
        [
            jnp.broadcast_to(time_part[None, :, None], grid_shape + (time_part.shape[-1],)),
            jnp.broadcast_to(row_part[:, None, None], grid_shape + (row_part.shape[-1],)),
            jnp.broadcast_to(col_part[None, None], grid_shape + (col_part.shape[-1],)),
        ],
        -1,
    ).reshape(tokens, model_width)
    frame_index = jnp.arange(frames, dtype=jnp.int32)
    own_ok = (
        (frame_index[None, :, None] < frame_count[0, 0]) & (visible.transpose(0, 2, 1) == 1)
    ).astype(BF16)
    flat_pixels = pixels.transpose(0, 2, 1, 3).reshape(tokens, pix_width)
    grad_pixels_out = cotangent.transpose(0, 2, 1, 3).reshape(tokens, pix_width)
    stream_one = mat_low(flat_pixels, w_patch) + b_patch.astype(F32) + position
    normed_one = layer_norm(stream_one, gain_one.astype(F32), shift_one.astype(F32)).astype(BF16)

    grid_one = normed_one.reshape(grid_shape + (model_width,))
    side = tile_rows * frames * HALO
    band = HALO * frames * tile_cols

    def with_flags(rows, flags):
        line = jnp.zeros((8 * model_width,), BF16).at[: flags.size].set(flags.reshape(-1))
        return jnp.concatenate([rows.reshape(-1, model_width), line.reshape(8, model_width)], 0)

    upper = rotate(with_flags(grid_one[tile_rows - HALO :], own_ok[tile_rows - HALO :]), "row", 1)
    lower = rotate(with_flags(grid_one[:HALO], own_ok[:HALO]), "row", -1)
    left = rotate(
        with_flags(grid_one[:, :, tile_cols - HALO :], own_ok[:, :, tile_cols - HALO :]), "col", 1
    )
    right = rotate(with_flags(grid_one[:, :, :HALO], own_ok[:, :, :HALO]), "col", -1)

    def flags_of(strip, count):
        return strip[-8:].reshape(-1)[:count]

    near = jnp.arange(HALO, dtype=jnp.int32)
    reach = halo_reach[0, 0]
    band_shape = (HALO, frames, tile_cols)
    side_shape = (tile_rows, frames, HALO)
    far_first = reach >= HALO - near
    near_first = reach >= near + 1
    keys = tokens + 2 * band + 2 * side
    key_total = -(-keys // LANES) * LANES
    spare = key_total - keys
    strip_ok = jnp.concatenate(
        [
            (flags_of(upper, band) > 0.5)
            & jnp.broadcast_to(far_first[:, None, None], band_shape).reshape(-1),
            (flags_of(lower, band) > 0.5)
            & jnp.broadcast_to(near_first[:, None, None], band_shape).reshape(-1),
            (flags_of(left, side) > 0.5)
            & jnp.broadcast_to(far_first[None, None, :], side_shape).reshape(-1),
            (flags_of(right, side) > 0.5)
            & jnp.broadcast_to(near_first[None, None, :], side_shape).reshape(-1),
            jnp.zeros((spare,), bool),
        ]
    )
    bias = jnp.where(
        jnp.concatenate([own_ok.reshape(-1) > 0.5, strip_ok]), 0.0, NEG_FILL
    ).astype(F32)
    strip_rows = jnp.concatenate(
        [
            upper[:band],
            lower[:band],
            left[:side],
            right[:side],
            jnp.zeros((spare, model_width), BF16),
        ],
        0,
    )

    qkv_own = mat_low(normed_one, w_qkv)
    kv_strip = mat_low(strip_rows, w_qkv[:, model_width:])
    query_rows = (qkv_own[:, :model_width] + b_query.astype(F32)).astype(BF16)
    key_rows = jnp.concatenate(
        [qkv_own[:, model_width : 2 * model_width], kv_strip[:, :model_width]], 0
    ).astype(BF16)
    value_rows = (
        jnp.concatenate([qkv_own[:, 2 * model_width :], kv_strip[:, model_width:]], 0)
        + b_value.astype(F32)
    ).astype(BF16)
    attended, log_total = attend(query_rows, key_rows, value_rows, bias[None, :])

    stream_two = stream_one + mat_low(attended, w_out) + b_out.astype(F32)
    normed_two = layer_norm(stream_two, gain_two.astype(F32), shift_two.astype(F32)).astype(BF16)
    hidden_pre = mat_low(normed_two, w_up) + b_up.astype(F32)
    hidden_act = gelu_exact(hidden_pre).astype(BF16)
    stream_out = stream_two + mat_low(hidden_act, w_down) + b_down.astype(F32)
    stream_low = stream_out.astype(BF16)
    decoded = (mat_low(stream_low, w_dec) + b_dec.astype(F32)).astype(BF16)
    pixel_out = (mat_low(decoded, w_pix) + b_pix.astype(F32)).astype(BF16)

    grad_w_pix = outer_sum(decoded, grad_pixels_out)
    grad_b_pix = column_sum(grad_pixels_out)
    grad_dec = times_transposed(grad_pixels_out, w_pix).astype(BF16)
    grad_w_dec = outer_sum(stream_low, grad_dec)
    grad_b_dec = column_sum(grad_dec)
    grad_stream = times_transposed(grad_dec, w_dec)
    grad_mlp = grad_stream.astype(BF16)
    grad_w_down = outer_sum(hidden_act, grad_mlp)
    grad_b_down = column_sum(grad_mlp)
    grad_act = times_transposed(grad_mlp, w_down)
    _, gelu_pull = jax.vjp(gelu_exact, hidden_pre)
    grad_pre = gelu_pull(grad_act)[0].astype(BF16)
    grad_w_up = outer_sum(normed_two, grad_pre)
    grad_b_up = column_sum(grad_pre)

    early = reduce_quarters(
        jnp.concatenate(
            [
                pack_columns(grad_w_down, model_width),
                pack_columns(grad_w_up, model_width),
                pack_columns(grad_w_pix, model_width),
            ],
            1,
        )
    )
    early_dec = reduce_quarters(pack_columns(grad_w_dec, grad_w_dec.shape[1]))

    grad_normed_two = times_transposed(grad_pre, w_up)
    back_two, grad_gain_two, grad_shift_two = norm_backward(
        stream_two, gain_two, shift_two, grad_normed_two
    )
    grad_stream_two = grad_stream + back_two
    grad_att = grad_stream_two.astype(BF16)
    grad_w_out = outer_sum(attended, grad_att)
    grad_b_out = column_sum(grad_att)
    grad_attended = times_transposed(grad_att, w_out).astype(BF16)
    grad_query, grad_keys, grad_values = attend_back(
        query_rows, key_rows, value_rows, grad_attended, attended, log_total, bias[:, None]
    )
    grad_b_query = column_sum(grad_query)
    grad_b_value = column_sum(grad_values)
    own_grad = jnp.concatenate([grad_query, grad_keys[:tokens], grad_values[:tokens]], 1)
    strip_grad = jnp.concatenate([grad_keys[tokens:], grad_values[tokens:]], 1)
    grad_strip = times_transposed(strip_grad, w_qkv[:, model_width:]).astype(BF16)
    from_below = rotate(grad_strip[:band], "row", -1)
    from_above = rotate(grad_strip[band : 2 * band], "row", 1)
    from_right = rotate(grad_strip[2 * band : 2 * band + side], "col", -1)
    from_left = rotate(grad_strip[2 * band + side : 2 * band + 2 * side], "col", 1)

    grad_w_qkv = outer_sum(normed_one, own_grad)
    grad_w_qkv = grad_w_qkv.at[:, model_width:].add(outer_sum(strip_rows, strip_grad))
    middle = reduce_quarters(
        jnp.concatenate(
            [pack_columns(grad_w_qkv, model_width), pack_columns(grad_w_out, model_width)], 1
        )
    )

    grad_normed_one = times_transposed(own_grad, w_qkv)
    grad_grid = grad_normed_one + jnp.concatenate([from_above, from_below], 0).astype(F32)
    sides = jnp.concatenate(
        [
            from_left.reshape(side_shape + (model_width,)),
            jnp.zeros((tile_rows, frames, tile_cols - 2 * HALO, model_width), BF16),
            from_right.reshape(side_shape + (model_width,)),
        ],
        2,
    ).reshape(tokens, model_width)
    grad_grid = grad_grid + sides.astype(F32)
    back_one, grad_gain_one, grad_shift_one = norm_backward(
        stream_one, gain_one, shift_one, grad_grid
    )
    grad_stream_one = grad_stream_two + back_one
    grad_b_patch = jnp.sum(grad_stream_one, 0)
    grad_emb = grad_stream_one.astype(BF16)
    grad_w_patch = outer_sum(flat_pixels, grad_emb)
    vectors = [
        grad_b_patch,
        grad_gain_one,
        grad_shift_one,
        grad_b_query,
        grad_b_value,
        grad_b_out,
        grad_gain_two,
        grad_shift_two,
        grad_b_up,
        grad_b_down,
        grad_b_dec,
        grad_b_pix,
    ]
    flat_vectors = jnp.concatenate([item.astype(BF16).reshape(4, -1) for item in vectors], 1)
    lines = -(-flat_vectors.shape[1] // model_width)
    flat_vectors = jnp.pad(
        flat_vectors, ((0, 0), (0, lines * model_width - flat_vectors.shape[1]))
    ).reshape(4, lines, model_width)
    patch_rows = pix_width // 4
    last = reduce_quarters(
        jnp.concatenate([pack_columns(grad_w_patch, model_width), flat_vectors], 1)
    )
    pixel_grad = times_transposed(grad_emb, w_patch).astype(BF16)

    sums = last[patch_rows : patch_rows + lines].reshape(-1).astype(F32)
    pieces = []
    at = 0
    for item in vectors:
        pieces.append(sums[at : at + item.size // 4])
        at += item.size // 4
    ff = w_up.shape[1]
    quarter = model_width // 4
    down_rows = ff // 4
    up_rows = quarter * (ff // model_width)
    share_patch = last[:patch_rows].astype(F32)
    qkv_rows = 3 * quarter
    share_qkv = unpack_columns(middle[:qkv_rows], 3 * model_width).astype(F32)
    share_out = middle[qkv_rows:].astype(F32)
    share_down = early[:down_rows].astype(F32)
    share_up = unpack_columns(early[down_rows : down_rows + up_rows], ff).astype(F32)
    share_pix = unpack_columns(early[down_rows + up_rows :], pix_width).astype(F32)
    share_dec = early_dec.astype(F32)

    def to_scene(flat):
        return flat.reshape(grid_shape + (pix_width,)).transpose(0, 2, 1, 3)

    return (
        to_scene(pixel_out),
        to_scene(pixel_grad),
        share_patch,
        pieces[0],
        pieces[1],
        pieces[2],
        share_qkv,
        pieces[3],
        pieces[4],
        share_out,
        pieces[5],
        pieces[6],
        pieces[7],
        share_up,
        pieces[8],
        share_down,
        pieces[9],
        share_dec,
        pieces[10],
        share_pix,
        pieces[11],
    )


def solution(mesh):
    tiles = P("row", "col", None, None)
    return jax.shard_map(
        per_device,
        mesh=mesh,
        in_specs=(
            tiles,
            P("row", "col", None),
            P("row", "col"),
            P("row", "col", None),
            P("row", "col"),
        )
        + (P(),) * 19
        + (tiles,),
        out_specs=(
            tiles,
            tiles,
            P("row", None),
            P("row"),
            P("row"),
            P("row"),
            P("row", None),
            P("row"),
            P("row"),
            P("row", None),
            P("row"),
            P("row"),
            P("row"),
            P("row", None),
            P("row"),
            P("row", None),
            P("row"),
            P("row", None),
            P("row"),
            P("row", None),
            P("row"),
        ),
        check_vma=False,
    )
```

time: 1040 us -> 654 us (0.63)
  matrix products: 317 us -> 116 us
  Pallas kernels: 0 us -> 94.3 us
  waiting for transfers between devices: 291 us -> 199 us
  other arithmetic: 165 us -> 82.6 us
  local copies, waits for them, and re-layouts: 177 us -> 105 us
  blocking collectives: 35.3 us -> 0 us
  starting transfers between devices: 21.6 us -> 46.4 us
  between operations: 19.3 us -> 3.9 us
    reduce_scatter x6 -> x0, waiting for transfers between devices: 211 us -> none  [the longest x1 50.4 us: per_device(): lax.psum_scatter(sum_w_down.astype(jnp.bfloat16), 'row', scatter_dimensio...]
    dot_general x66 -> x24, matrix products: 317 us -> 116 us  [the longest x8 48.3 us: mat_low(): return jnp.dot(left_side, right_side, preferred_element_type=F32)]
    ppermute x12 -> x40, waiting for transfers between devices: 0.71 us -> 199 us  [the longest x32 199 us: swap(): return lax.ppermute(value, axis, [(i, i ^ stride) for i in range(count)])]
    pallas_call x0 -> x2, Pallas kernels: none -> 94.3 us  [the longest x1 55.1 us: attend_back(): pl.pallas_call(attend_back_kernel, grid=(pairs,), in_specs=[own, wide, wi...]
    psum x1 -> x0, waiting for transfers between devices: 79.4 us -> none  [per_device(): lax.psum(grad_w_patch.astype(jnp.bfloat16), 'col').astype(jnp.float32)]
    convert_element_type x39 -> x44, other arithmetic: 94.6 us -> 38.5 us  [the longest x20 14.1 us: add(): return (a.astype(F32) + b.astype(F32)).astype(BF16)]
    unnamed x189 -> x192, local copies, waits for them, and re-layouts: 62.8 us -> 24.2 us
    ppermute x12 -> x40, starting transfers between devices: 20.5 us -> 46.4 us  [the longest x32 31.5 us: swap(): return lax.ppermute(value, axis, [(i, i ^ stride) for i in range(count)])]
  transfers between devices with their start and end apart: 20 -> 40, of which waited for: 9 -> 18; matrix products, arithmetic and copies ran while one was open for 23% -> 24% of each run, Pallas kernels for 0% -> 0%
where the time goes in v1:
time: 654 us; the launch traced here: 647 us
  waiting for transfers between devices  199 us (30%)
  matrix products  116 us (18%)
  local copies, waits for them, and re-layouts  105 us (16%)
  Pallas kernels  94.3 us (14%)
  other arithmetic  82.6 us (13%)
  starting transfers between devices  46.4 us (7%)
    ppermute x32, waiting for transfers between devices, swap(): return lax.ppermute(value, axis, [(i, i ^ stride) for i in range(count)])  199 us
    pallas_call x1, Pallas kernels, attend_back(): pl.pallas_call(attend_back_kernel, grid=(pairs,), in_specs=[own, wide, wi...  55.1 us
    dot_general x8, matrix products, mat_low(): return jnp.dot(left_side, right_side, preferred_element_type=F32)  48.3 us
    dot_general x8, matrix products, times_transposed(): jnp.einsum('ne,de->nd', left_side, right_side, preferred_element_type=F32)  42.8 us
    pallas_call x1, Pallas kernels, attend(): pl.pallas_call(attend_kernel, grid=(pairs,), in_specs=[pl.BlockSpec((toke...  39.2 us
    ppermute x32, starting transfers between devices, swap(): return lax.ppermute(value, axis, [(i, i ^ stride) for i in range(count)])  31.5 us
    dot_general x8, matrix products, outer_sum(): jnp.einsum('nd,ne->de', left_side, right_side, preferred_element_type=F32)  25 us
    unnamed x192, local copies, waits for them, and re-layouts  24.2 us
  transfers between devices with their start and end apart: 40, of which 18 were waited for; matrix products, arithmetic and copies ran while one was open for 24% of the time, Pallas kernels for 0%

profile of v1, /device:TPU:0, one launch (start us, length us, event | category | flops | bytes accessed | tf_op | source)
XLA Modules:
  0.0 647.2 jit_solution(17182298631360067299)
XLA Ops:
  17.8 3.0 collective-permute-start.2
  27.8 3.0 collective-permute-start.3
  41.2 5.1 fusion.88
  46.3 2.5 fusion.87
  56.6 2.8 slice.464
  90.1 4.5 fusion.19
  104.7 39.2 %attend.1 = (bf16[768,768]{1,0:T(8,128)(2,1)S(1)}, f32[6,2,768]{2,1,0:T(2,128)S(1)}) custom-call(bf16[768,768]{1,0:T(8,128)(2,1)S(1)} %get-tuple-element.110.q_ref, bf16[1664,768]{1,0:T(8,128)(2,1)S(1)} %pad_maximum_fusion.3.k_ref, bf16[1664,768]{1,0:T(8,128)(2,1)} %fusion.9.v_ref, f32[1,1664]{1,0:T(1,128)S(1)} %broadcast_select_fusion.25.bias_ref), custom_call_target="tpu_custom_call" | custom-call | flops 15703474176 | bytes 8388608 | tf_op jit(solution)/shard_map/attend/pallas_call | solution.py:114
  147.6 28.1 %multiply_convert_fusion = (bf16[768,3072]{1,0:T(8,128)(2,1)}, f32[768,3072]{1,0:T(8,128)}, f32[768,3072]{1,0:T(8,128)}) fusion(f32[3072]{0:T(1024)S(1)} %copy-done.63, bf16[768,3072]{1,0:T(8,128)(2,1)S(1)} %bitcast.239, f32[768,768]{1,0:T(8,128)S(1)} %get-tuple-element.188, f32[768]{0:T(1024)S(1)} %copy-done.69, f32[768]{0:T(1024)S(1)} %copy-done.60, ...), kind=kOutput, calls=%fused_computation.5 | convolution fusion | flops 3782541312 | bytes 30695424 | tf_op jit(solution)/shard_map/dot_general | solution.py:46
  175.7 13.8 %fusion.86 = (bf16[3072]{0:T(1024)(128)(2,1)}, bf16[768,3072]{1,0:T(8,128)(2,1)}) fusion(f32[768,3072]{1,0:T(8,128)} %get-tuple-element.106, bf16[3072,768]{1,0:T(8,128)(2,1)} %param.53, f32[768,768]{1,0:T(8,128)S(1)} %copy-done.15, f32[768,3072]{1,0:T(8,128)} %get-tuple-element.189, f32[3072]{0:T(1024)S(1)} %copy-done.63), kind=kOutput, calls=%fused_computation.260 | convolution fusion | flops 3662214144 | bytes 30689280 | tf_op jit(solution)/shard_map/ne,de->nd/dot_general | solution.py:54
  189.4 8.4 %multiply_reduce_fusion = (bf16[768]{0:T(1024)(128)(2,1)}, f32[768]{0:T(1024)S(1)}, bf16[768]{0:T(1024)(128)(2,1)}, f32[768,768]{1,0:T(8,128)S(1)}) fusion(f32[768,768]{1,0:T(8,128)S(1)} %get-tuple-element.188, f32[768]{0:T(1024)S(1)} %fusion.48, f32[768]{0:T(1024)S(1)} %broadcast_multiply_fusion, f32[768]{0:T(1024)S(1)} %copy-done.60, ...), kind=kOutput, calls=%fused_computation.57 | convolution fusion | flops 3628594944 | bytes 14171136 | tf_op jit(solution)/shard_map/ne,de->nd/dot_general | solution.py:54
  197.8 6.8 %convolution_convert_fusion = bf16[768,3072]{1,0:T(8,128)(2,1)} fusion(bf16[768,3072]{1,0:T(8,128)(2,1)S(1)} %copy-done.80, f32[768,768]{1,0:T(8,128)S(1)} %get-tuple-element.188, f32[768]{0:T(1024)S(1)} %copy-done.69, f32[768]{0:T(1024)S(1)} %copy-done.60, f32[768]{0:T(1024)S(1)} %fusion.48, f32[768]{0:T(1024)S(1)} %broadcast_multiply_fusion), kind=kOutput, calls=%fused_computation.26 | convolution fusion | flops 3629187072 | bytes 11808768 | tf_op jit(solution)/shard_map/nd,ne->de/dot_general | solution.py:50
  217.8 55.1 %attend_back.1 = (bf16[768,768]{1,0:T(8,128)(2,1)S(1)}, bf16[1664,768]{1,0:T(8,128)(2,1)}, bf16[1664,768]{1,0:T(8,128)(2,1)}) custom-call(bf16[768,768]{1,0:T(8,128)(2,1)S(1)} %get-tuple-element.110.q_ref, bf16[1664,768]{1,0:T(8,128)(2,1)} %copy-done.1, bf16[1664,768]{1,0:T(8,128)(2,1)} %fusion.9.v_ref, bf16[768,768]{1,0:T(8,128)(2,1)S(1)} %copy-done.6, ...), custom_call_target="tpu_custom_call" | custom-call | flops 23555211264 | bytes 16777216 | tf_op jit(solution)/shard_map/attend_back/pallas_call | solution.py:196
  272.9 2.8 slice.323
  279.6 2.3 fusion.21
  283.8 4.4 convolution_convert_fusion.1
  288.3 3.9 add_convert_fusion.4
  298.7 4.7 collective-permute-start.7
  303.7 3.0 fusion.24
  306.7 2.9 fusion.10
  312.4 2.3 pad_maximum_fusion
  314.7 4.1 copy-done.9
  318.8 2.7 dynamic-slice_bitcast_fusion
  322.3 2.7 reduce_sum.261
  343.3 6.5 %collective-permute-done.33 = bf16[1,192,512]{2,1,0:T(8,128)(2,1)S(1)} collective-permute-done((bf16[1,192,512]{2,1,0:T(8,128)(2,1)S(1)}, bf16[1,192,512]{2,1,0:T(8,128)(2,1)S(1)}, u32[]{:S(2)}, u32[]{:S(2)}) %collective-permute-start.33) | collective-permute-done | bytes 196640 | tf_op jit(solution)/shard_map/ppermute | solution.py:229
  350.7 8.1 %multiply_reduce_fusion.1 = (bf16[768]{0:T(1024)(128)(2,1)}, f32[768]{0:T(1024)}, bf16[768]{0:T(1024)(128)(2,1)}, f32[768,768]{1,0:T(8,128)}) fusion(f32[768,768]{1,0:T(8,128)S(1)} %copy-done.12, f32[768]{0:T(1024)S(1)} %copy-done.54, f32[768]{0:T(1024)S(1)} %copy-done.49, f32[768]{0:T(1024)S(1)} %copy-done.52, ...), kind=kOutput, calls=%fused_computation.58 | convolution fusion | flops 2737370880 | bytes 14171136 | tf_op jit(solution)/shard_map/ne,de->nd/dot_general | solution.py:54
  360.8 3.4 fusion.66
  372.6 3.4 fusion.12
  376.0 4.4 copy.78
  383.8 3.9 collective-permute-done.35
  387.8 2.8 add_convert_fusion.2
  398.8 5.5 fusion
  406.8 3.4 convolution_convert_fusion.3
  410.3 2.3 collective-permute-start.39
  412.6 66.8 %collective-permute-done.9 = bf16[1,448,768]{2,1,0:T(8,128)(2,1)S(1)} collective-permute-done((bf16[1,448,768]{2,1,0:T(8,128)(2,1)S(1)}, bf16[1,448,768]{2,1,0:T(8,128)(2,1)S(1)}, u32[]{:S(2)}, u32[]{:S(2)}) %collective-permute-start.9) | collective-permute-done | bytes 688160 | tf_op jit(solution)/shard_map/ppermute | solution.py:229
  484.4 2.7 collective-permute-done.10
  489.0 3.7 collective-permute-done.11
  492.8 3.7 collective-permute-start.12
  499.4 9.5 %collective-permute-done.17 = bf16[1,768,768]{2,1,0:T(8,128)(2,1)S(1)} collective-permute-done((bf16[1,768,768]{2,1,0:T(8,128)(2,1)S(1)}, bf16[1,768,768]{2,1,0:T(8,128)(2,1)S(1)}, u32[]{:S(2)}, u32[]{:S(2)}) %collective-permute-start.17) | collective-permute-done | bytes 1179680 | tf_op jit(solution)/shard_map/ppermute | solution.py:229
  509.7 2.9 collective-permute-start.13
  517.1 20.8 %collective-permute-done.18 = bf16[384,768]{1,0:T(8,128)(2,1)S(1)} collective-permute-done((bf16[384,768]{1,0:T(8,128)(2,1)S(1)}, bf16[384,768]{1,0:T(8,128)(2,1)S(1)}, u32[]{:S(2)}, u32[]{:S(2)}) %collective-permute-start.18) | collective-permute-done | bytes 589856 | tf_op jit(solution)/shard_map/ppermute | solution.py:229
  542.3 7.3 %collective-permute-done.19 = bf16[192,768]{1,0:T(8,128)(2,1)S(1)} collective-permute-done((bf16[192,768]{1,0:T(8,128)(2,1)S(1)}, bf16[192,768]{1,0:T(8,128)(2,1)S(1)}, u32[]{:S(2)}, u32[]{:S(2)}) %collective-permute-start.19) | collective-permute-done | bytes 294944 | tf_op jit(solution)/shard_map/ppermute | solution.py:229
  549.8 12.4 %collective-permute-done.27 = bf16[448,768]{1,0:T(8,128)(2,1)S(1)} collective-permute-done((bf16[448,768]{1,0:T(8,128)(2,1)S(1)}, bf16[448,768]{1,0:T(8,128)(2,1)S(1)}, u32[]{:S(2)}, u32[]{:S(2)}) %collective-permute-start.27) | collective-permute-done | bytes 688160 | tf_op jit(solution)/shard_map/ppermute | solution.py:229
  564.7 3.5 collective-permute-start.21
  568.2 15.2 %collective-permute-done.28 = bf16[224,768]{1,0:T(8,128)(2,1)S(1)} collective-permute-done((bf16[224,768]{1,0:T(8,128)(2,1)S(1)}, bf16[224,768]{1,0:T(8,128)(2,1)S(1)}, u32[]{:S(2)}, u32[]{:S(2)}) %collective-permute-start.28) | collective-permute-done | bytes 344096 | tf_op jit(solution)/shard_map/ppermute | solution.py:229
  583.5 3.0 collective-permute-done.21
  587.4 7.3 %collective-permute-done.29 = bf16[224,768]{1,0:T(8,128)(2,1)S(1)} collective-permute-done((bf16[224,768]{1,0:T(8,128)(2,1)S(1)}, bf16[224,768]{1,0:T(8,128)(2,1)S(1)}, u32[]{:S(2)}, u32[]{:S(2)}) %collective-permute-start.29) | collective-permute-done | bytes 344096 | tf_op jit(solution)/shard_map/ppermute | solution.py:229
  603.9 8.1 %collective-permute-done.30 = bf16[448,768]{1,0:T(8,128)(2,1)} collective-permute-done((bf16[448,768]{1,0:T(8,128)(2,1)}, bf16[448,768]{1,0:T(8,128)(2,1)}, u32[]{:S(2)}, u32[]{:S(2)}) %collective-permute-start.30) | collective-permute-done | bytes 688160 | tf_op jit(solution)/shard_map/ppermute | solution.py:229
  617.1 25.0 %collective-permute-done.31 = bf16[896,768]{1,0:T(8,128)(2,1)S(1)} collective-permute-done((bf16[896,768]{1,0:T(8,128)(2,1)S(1)}, bf16[896,768]{1,0:T(8,128)(2,1)S(1)}, u32[]{:S(2)}, u32[]{:S(2)}) %collective-permute-start.31) | collective-permute-done | bytes 1376288 | tf_op jit(solution)/shard_map/ppermute | solution.py:229
  (480 shorter events, 199.6 us)
Async XLA Ops:
  13.6 27.6 %copy-start.26 = (bf16[768,768]{1,0:T(8,128)(2,1)}, bf16[768,768]{1,0:T(8,128)(2,1)S(1)}, u32[]{:S(2)}) copy-start(bf16[768,768]{1,0:T(8,128)(2,1)S(1)} %add_convert_fusion.6) | copy-start | bytes 3538948
  17.8 56.8 %collective-permute-start.2 = (bf16[56,768]{1,0:T(8,128)(2,1)}, bf16[56,768]{1,0:T(8,128)(2,1)}, u32[]{:S(2)}, u32[]{:S(2)}) collective-permute-start(bf16[56,768]{1,0:T(8,128)(2,1)} %pad_maximum_fusion.23), channel_id=1, source_target_pairs={{0,1},{1,2},{2,3},{3,4},{4,5},{5,6},{6,7},{7,0},{8,9},{9,10},{10,1... | collective-permute-start | bytes 258056 | tf_op jit(solution)/shard_map/ppermute | solution.py:234
  27.8 48.1 %collective-permute-start.3 = (bf16[56,768]{1,0:T(8,128)(2,1)}, bf16[56,768]{1,0:T(8,128)(2,1)}, u32[]{:S(2)}, u32[]{:S(2)}) collective-permute-start(bf16[56,768]{1,0:T(8,128)(2,1)} %pad_maximum_fusion.24), channel_id=1, source_target_pairs={{0,7},{1,0},{2,1},{3,2},{4,3},{5,4},{6,5},{7,6},{8,15},{9,8},{10,9... | collective-permute-start | bytes 258056 | tf_op jit(solution)/shard_map/ppermute | solution.py:234
  35.3 44.4 %collective-permute-start = (bf16[392,768]{1,0:T(8,128)(2,1)}, bf16[392,768]{1,0:T(8,128)(2,1)}, u32[]{:S(2)}, u32[]{:S(2)}) collective-permute-start(bf16[392,768]{1,0:T(8,128)(2,1)} %pad_maximum_fusion.15), channel_id=1, source_target_pairs={{0,8},{8,16},{16,24},{24,0},{1,9},{9,17},{17,25},{25,1},{2,10},{10... | collective-permute-start | bytes 1806344 | tf_op jit(solution)/shard_map/ppermute | solution.py:234
  38.6 44.3 %collective-permute-start.1 = (bf16[392,768]{1,0:T(8,128)(2,1)}, bf16[392,768]{1,0:T(8,128)(2,1)}, u32[]{:S(2)}, u32[]{:S(2)}) collective-permute-start(bf16[392,768]{1,0:T(8,128)(2,1)} %pad_maximum_fusion.16), channel_id=1, source_target_pairs={{0,24},{8,0},{16,8},{24,16},{1,25},{9,1},{17,9},{25,17},{2,26},{10... | collective-permute-start | bytes 1806344 | tf_op jit(solution)/shard_map/ppermute | solution.py:234
  104.7 39.3 %copy-start.11 = (f32[768,768]{1,0:T(8,128)S(1)}, f32[768,768]{1,0:T(8,128)}, u32[]{:S(2)}) copy-start(f32[768,768]{1,0:T(8,128)} %copy-done.10) | copy-start | bytes 7077892
  104.7 39.3 %copy-start.70 = (f32[768]{0:T(1024)S(1)}, f32[768]{0:T(1024)}, u32[]{:S(2)}) copy-start(f32[768]{0:T(1024)} %convert_element_type.480) | copy-start | bytes 9220
  104.7 39.3 %copy-start.78 = (bf16[768,768]{1,0:T(8,128)(2,1)S(1)}, bf16[768,768]{1,0:T(8,128)(2,1)}, u32[]{:S(2)}) copy-start(bf16[768,768]{1,0:T(8,128)(2,1)} %param.47) | copy-start | bytes 3538948
  143.9 62.9 %copy-start.4 = (bf16[768,768]{1,0:T(8,128)(2,1)}, bf16[768,768]{1,0:T(8,128)(2,1)S(1)}, u32[]{:S(2)}) copy-start(bf16[768,768]{1,0:T(8,128)(2,1)S(1)} %get-tuple-element.86.o_ref) | copy-start | bytes 3538948
  145.2 59.4 %copy-start.21 = (f32[768,768]{1,0:T(8,128)}, f32[768,768]{1,0:T(8,128)S(1)}, u32[]{:S(2)}) copy-start(f32[768,768]{1,0:T(8,128)S(1)} %get-tuple-element.188) | copy-start | bytes 7077892
  147.6 28.1 %copy-start.15 = (f32[768,768]{1,0:T(8,128)S(1)}, f32[768,768]{1,0:T(8,128)}, u32[]{:S(2)}) copy-start(f32[768,768]{1,0:T(8,128)} %fusion.89) | copy-start | bytes 7077892
  272.9 30.7 %copy-start.2 = (bf16[768,768]{1,0:T(8,128)(2,1)}, bf16[768,768]{1,0:T(8,128)(2,1)S(1)}, u32[]{:S(2)}) copy-start(bf16[768,768]{1,0:T(8,128)(2,1)S(1)} %get-tuple-element.88) | copy-start | bytes 3538948
  294.9 44.2 %collective-permute-start.32 = (bf16[2,192,512]{2,1,0:T(8,128)(2,1)}, bf16[2,192,512]{2,1,0:T(8,128)(2,1)}, u32[]{:S(2)}, u32[]{:S(2)}) collective-permute-start(bf16[2,192,512]{2,1,0:T(8,128)(2,1)} %dynamic-slice_bitcast_fusion.6), channel_id=1, source_target_pairs={{0,8},{8,0},{16,24},{24,16},{1,9},{9,1},{17,25},{25,17},{2,10},{10... | collective-permute-start | bytes 1179656 | tf_op jit(solution)/shard_map/ppermute | solution.py:229
  298.6 37.2 %collective-permute-start.6 = (bf16[48,768]{1,0:T(8,128)(2,1)}, bf16[48,768]{1,0:T(8,128)(2,1)}, u32[]{:S(2)}, u32[]{:S(2)}) collective-permute-start(bf16[48,768]{1,0:T(8,128)(2,1)} %get-tuple-element.130), channel_id=1, source_target_pairs={{0,1},{1,2},{2,3},{3,4},{4,5},{5,6},{6,7},{7,0},{8,9},{9,10},{10,1... | collective-permute-start | bytes 221192 | tf_op jit(solution)/shard_map/ppermute | solution.py:234
  298.7 38.8 %collective-permute-start.7 = (bf16[48,768]{1,0:T(8,128)(2,1)}, bf16[48,768]{1,0:T(8,128)(2,1)}, u32[]{:S(2)}, u32[]{:S(2)}) collective-permute-start(bf16[48,768]{1,0:T(8,128)(2,1)} %get-tuple-element.131), channel_id=1, source_target_pairs={{0,7},{1,0},{2,1},{3,2},{4,3},{5,4},{6,5},{7,6},{8,15},{9,8},{10,9... | collective-permute-start | bytes 221192 | tf_op jit(solution)/shard_map/ppermute | solution.py:234
  303.4 47.2 %collective-permute-start.4 = (bf16[384,768]{1,0:T(8,128)(2,1)}, bf16[384,768]{1,0:T(8,128)(2,1)}, u32[]{:S(2)}, u32[]{:S(2)}) collective-permute-start(bf16[384,768]{1,0:T(8,128)(2,1)} %get-tuple-element.132), channel_id=1, source_target_pairs={{0,8},{8,16},{16,24},{24,0},{1,9},{9,17},{17,25},{25,1},{2,10},{10... | collective-permute-start | bytes 1769480 | tf_op jit(solution)/shard_map/ppermute | solution.py:234
  333.8 16.8 %collective-permute-start.5 = (bf16[384,768]{1,0:T(8,128)(2,1)}, bf16[384,768]{1,0:T(8,128)(2,1)}, u32[]{:S(2)}, u32[]{:S(2)}) collective-permute-start(bf16[384,768]{1,0:T(8,128)(2,1)} %get-tuple-element.133), channel_id=1, source_target_pairs={{0,24},{8,0},{16,8},{24,16},{1,25},{9,1},{17,9},{25,17},{2,26},{10... | collective-permute-start | bytes 1769480 | tf_op jit(solution)/shard_map/ppermute | solution.py:234
  335.9 63.0 %collective-permute-start.24 = (bf16[2,1792,768]{2,1,0:T(8,128)(2,1)}, bf16[2,1792,768]{2,1,0:T(8,128)(2,1)}, u32[]{:S(2)}, u32[]{:S(2)}) collective-permute-start(bf16[2,1792,768]{2,1,0:T(8,128)(2,1)} %dynamic-slice_bitcast_fusion), channel_id=1, source_target_pairs={{0,8},{8,0},{16,24},{24,16},{1,9},{9,1},{17,25},{25,17},{2,10},{10... | collective-permute-start | bytes 16515080 | tf_op jit(solution)/shard_map/ppermute | solution.py:229
  340.5 9.3 %collective-permute-start.33 = (bf16[1,192,512]{2,1,0:T(8,128)(2,1)S(1)}, bf16[1,192,512]{2,1,0:T(8,128)(2,1)S(1)}, u32[]{:S(2)}, u32[]{:S(2)}) collective-permute-start(bf16[1,192,512]{2,1,0:T(8,128)(2,1)S(1)} %constant_dynamic-slice_fusion), channel_id=1, source_target_pairs={{0,16},{8,24},{16,0},{24,8},{1,17},{9,25},{17,1},{25,9},{2,18},{10... | collective-permute-start | bytes 589832 | tf_op jit(solution)/shard_map/ppermute | solution.py:229
  350.6 31.8 %collective-permute-start.34 = (bf16[96,512]{1,0:T(8,128)(2,1)}, bf16[96,512]{1,0:T(8,128)(2,1)}, u32[]{:S(2)}, u32[]{:S(2)}) collective-permute-start(bf16[96,512]{1,0:T(8,128)(2,1)} %dynamic-slice_bitcast_fusion.12), channel_id=1, source_target_pairs={{0,1},{1,0},{2,3},{3,2},{4,5},{5,4},{6,7},{7,6},{8,9},{9,8},{10,11... | collective-permute-start | bytes 294920 | tf_op jit(solution)/shard_map/ppermute | solution.py:229
  383.5 4.2 collective-permute-start.35
  383.7 13.7 %collective-permute-start.8 = (bf16[2,448,768]{2,1,0:T(8,128)(2,1)S(1)}, bf16[2,448,768]{2,1,0:T(8,128)(2,1)S(1)}, u32[]{:S(2)}, u32[]{:S(2)}) collective-permute-start(bf16[2,448,768]{2,1,0:T(8,128)(2,1)S(1)} %dynamic-slice_bitcast_fusion.3), channel_id=1, source_target_pairs={{0,8},{8,0},{16,24},{24,16},{1,9},{9,1},{17,25},{25,17},{2,10},{10... | collective-permute-start | bytes 4128776 | tf_op jit(solution)/shard_map/ppermute | solution.py:229
  387.7 4.8 collective-permute-start.36
  392.5 4.8 collective-permute-start.37
  395.1 86.5 %collective-permute-start.16 = (bf16[2,768,768]{2,1,0:T(8,128)(2,1)}, bf16[2,768,768]{2,1,0:T(8,128)(2,1)}, u32[]{:S(2)}, u32[]{:S(2)}) collective-permute-start(bf16[2,768,768]{2,1,0:T(8,128)(2,1)} %dynamic-slice_bitcast_fusion.1), channel_id=1, source_target_pairs={{0,8},{8,0},{16,24},{24,16},{1,9},{9,1},{17,25},{25,17},{2,10},{10... | collective-permute-start | bytes 7077896 | tf_op jit(solution)/shard_map/ppermute | solution.py:229
  397.3 12.9 %collective-permute-start.38 = (bf16[48,512]{1,0:T(8,128)(2,1)S(1)}, bf16[48,512]{1,0:T(8,128)(2,1)S(1)}, u32[]{:S(2)}, u32[]{:S(2)}) collective-permute-start(bf16[48,512]{1,0:T(8,128)(2,1)S(1)} %pad_maximum_fusion.26), channel_id=1, source_target_pairs={{0,2},{1,3},{2,0},{3,1},{4,6},{5,7},{6,4},{7,5},{8,10},{9,11},{10,... | collective-permute-start | bytes 147464 | tf_op jit(solution)/shard_map/ppermute | solution.py:229
  404.6 91.9 %collective-permute-start.25 = (bf16[1,1792,768]{2,1,0:T(8,128)(2,1)S(1)}, bf16[1,1792,768]{2,1,0:T(8,128)(2,1)S(1)}, u32[]{:S(2)}, u32[]{:S(2)}) collective-permute-start(bf16[1,1792,768]{2,1,0:T(8,128)(2,1)S(1)} %constant_dynamic-slice_fusion.1), channel_id=1, source_target_pairs={{0,16},{8,24},{16,0},{24,8},{1,17},{9,25},{17,1},{25,9},{2,18},{10... | collective-permute-start | bytes 8257544 | tf_op jit(solution)/shard_map/ppermute | solution.py:229
  405.8 73.6 %collective-permute-start.9 = (bf16[1,448,768]{2,1,0:T(8,128)(2,1)S(1)}, bf16[1,448,768]{2,1,0:T(8,128)(2,1)S(1)}, u32[]{:S(2)}, u32[]{:S(2)}) collective-permute-start(bf16[1,448,768]{2,1,0:T(8,128)(2,1)S(1)} %constant_dynamic-slice_fusion.3), channel_id=1, source_target_pairs={{0,16},{8,24},{16,0},{24,8},{1,17},{9,25},{17,1},{25,9},{2,18},{10... | collective-permute-start | bytes 2064392 | tf_op jit(solution)/shard_map/ppermute | solution.py:229
  410.3 78.7 %collective-permute-start.39 = (bf16[96,512]{1,0:T(8,128)(2,1)S(1)}, bf16[96,512]{1,0:T(8,128)(2,1)S(1)}, u32[]{:S(2)}, u32[]{:S(2)}) collective-permute-start(bf16[96,512]{1,0:T(8,128)(2,1)S(1)} %pad_maximum_fusion.22), channel_id=1, source_target_pairs={{0,1},{1,0},{2,3},{3,2},{4,5},{5,4},{6,7},{7,6},{8,9},{9,8},{10,11... | collective-permute-start | bytes 294920 | tf_op jit(solution)/shard_map/ppermute | solution.py:229
  479.6 7.6 %collective-permute-start.10 = (bf16[224,768]{1,0:T(8,128)(2,1)S(1)}, bf16[224,768]{1,0:T(8,128)(2,1)S(1)}, u32[]{:S(2)}, u32[]{:S(2)}) collective-permute-start(bf16[224,768]{1,0:T(8,128)(2,1)S(1)} %dynamic-slice_bitcast_fusion.8), channel_id=1, source_target_pairs={{0,1},{1,0},{2,3},{3,2},{4,5},{5,4},{6,7},{7,6},{8,9},{9,8},{10,11... | collective-permute-start | bytes 1032200 | tf_op jit(solution)/shard_map/ppermute | solution.py:229
  484.0 24.9 %collective-permute-start.17 = (bf16[1,768,768]{2,1,0:T(8,128)(2,1)S(1)}, bf16[1,768,768]{2,1,0:T(8,128)(2,1)S(1)}, u32[]{:S(2)}, u32[]{:S(2)}) collective-permute-start(bf16[1,768,768]{2,1,0:T(8,128)(2,1)S(1)} %constant_dynamic-slice_fusion.2), channel_id=1, source_target_pairs={{0,16},{8,24},{16,0},{24,8},{1,17},{9,25},{17,1},{25,9},{2,18},{10... | collective-permute-start | bytes 3538952 | tf_op jit(solution)/shard_map/ppermute | solution.py:229
  487.3 5.5 collective-permute-start.11
  492.8 16.8 %collective-permute-start.12 = (bf16[56,768]{1,0:T(8,128)(2,1)S(1)}, bf16[56,768]{1,0:T(8,128)(2,1)S(1)}, u32[]{:S(2)}, u32[]{:S(2)}) collective-permute-start(bf16[56,768]{1,0:T(8,128)(2,1)S(1)} %dynamic-slice_bitcast_fusion.13), channel_id=1, source_target_pairs={{0,4},{1,5},{2,6},{3,7},{4,0},{5,1},{6,2},{7,3},{8,12},{9,13},{10,... | collective-permute-start | bytes 258056 | tf_op jit(solution)/shard_map/ppermute | solution.py:229
  497.5 42.2 %collective-permute-start.26 = (bf16[896,768]{1,0:T(8,128)(2,1)S(1)}, bf16[896,768]{1,0:T(8,128)(2,1)S(1)}, u32[]{:S(2)}, u32[]{:S(2)}) collective-permute-start(bf16[896,768]{1,0:T(8,128)(2,1)S(1)} %dynamic-slice_bitcast_fusion.2), channel_id=1, source_target_pairs={{0,1},{1,0},{2,3},{3,2},{4,5},{5,4},{6,7},{7,6},{8,9},{9,8},{10,11... | collective-permute-start | bytes 4128776 | tf_op jit(solution)/shard_map/ppermute | solution.py:229
  509.3 28.6 %collective-permute-start.18 = (bf16[384,768]{1,0:T(8,128)(2,1)S(1)}, bf16[384,768]{1,0:T(8,128)(2,1)S(1)}, u32[]{:S(2)}, u32[]{:S(2)}) collective-permute-start(bf16[384,768]{1,0:T(8,128)(2,1)S(1)} %dynamic-slice_bitcast_fusion.5), channel_id=1, source_target_pairs={{0,1},{1,0},{2,3},{3,2},{4,5},{5,4},{6,7},{7,6},{8,9},{9,8},{10,11... | collective-permute-start | bytes 1769480 | tf_op jit(solution)/shard_map/ppermute | solution.py:229
  509.7 5.7 collective-permute-start.13
  515.4 25.2 %collective-permute-start.14 = (bf16[112,768]{1,0:T(8,128)(2,1)S(1)}, bf16[112,768]{1,0:T(8,128)(2,1)S(1)}, u32[]{:S(2)}, u32[]{:S(2)}) collective-permute-start(bf16[112,768]{1,0:T(8,128)(2,1)S(1)} %pad_maximum_fusion.21), channel_id=1, source_target_pairs={{0,2},{1,3},{2,0},{3,1},{4,6},{5,7},{6,4},{7,5},{8,10},{9,11},{10,... | collective-permute-start | bytes 516104 | tf_op jit(solution)/shard_map/ppermute | solution.py:229
  538.0 11.6 %collective-permute-start.19 = (bf16[192,768]{1,0:T(8,128)(2,1)S(1)}, bf16[192,768]{1,0:T(8,128)(2,1)S(1)}, u32[]{:S(2)}, u32[]{:S(2)}) collective-permute-start(bf16[192,768]{1,0:T(8,128)(2,1)S(1)} %dynamic-slice_bitcast_fusion.9), channel_id=1, source_target_pairs={{0,2},{1,3},{2,0},{3,1},{4,6},{5,7},{6,4},{7,5},{8,10},{9,11},{10,... | collective-permute-start | bytes 884744 | tf_op jit(solution)/shard_map/ppermute | solution.py:229
  540.1 22.1 %collective-permute-start.27 = (bf16[448,768]{1,0:T(8,128)(2,1)S(1)}, bf16[448,768]{1,0:T(8,128)(2,1)S(1)}, u32[]{:S(2)}, u32[]{:S(2)}) collective-permute-start(bf16[448,768]{1,0:T(8,128)(2,1)S(1)} %dynamic-slice_bitcast_fusion.4), channel_id=1, source_target_pairs={{0,2},{1,3},{2,0},{3,1},{4,6},{5,7},{6,4},{7,5},{8,10},{9,11},{10,... | collective-permute-start | bytes 2064392 | tf_op jit(solution)/shard_map/ppermute | solution.py:229
  540.8 22.3 %collective-permute-start.15 = (bf16[224,768]{1,0:T(8,128)(2,1)S(1)}, bf16[224,768]{1,0:T(8,128)(2,1)S(1)}, u32[]{:S(2)}, u32[]{:S(2)}) collective-permute-start(bf16[224,768]{1,0:T(8,128)(2,1)S(1)} %pad_maximum_fusion.19), channel_id=1, source_target_pairs={{0,1},{1,0},{2,3},{3,2},{4,5},{5,4},{6,7},{7,6},{8,9},{9,8},{10,11... | collective-permute-start | bytes 1032200 | tf_op jit(solution)/shard_map/ppermute | solution.py:229
  549.7 14.9 %collective-permute-start.20 = (bf16[96,768]{1,0:T(8,128)(2,1)S(1)}, bf16[96,768]{1,0:T(8,128)(2,1)S(1)}, u32[]{:S(2)}, u32[]{:S(2)}) collective-permute-start(bf16[96,768]{1,0:T(8,128)(2,1)S(1)} %dynamic-slice_bitcast_fusion.11), channel_id=1, source_target_pairs={{0,4},{1,5},{2,6},{3,7},{4,0},{5,1},{6,2},{7,3},{8,12},{9,13},{10,... | collective-permute-start | bytes 442376 | tf_op jit(solution)/shard_map/ppermute | solution.py:229
  562.4 21.0 %collective-permute-start.28 = (bf16[224,768]{1,0:T(8,128)(2,1)S(1)}, bf16[224,768]{1,0:T(8,128)(2,1)S(1)}, u32[]{:S(2)}, u32[]{:S(2)}) collective-permute-start(bf16[224,768]{1,0:T(8,128)(2,1)S(1)} %dynamic-slice_bitcast_fusion.7), channel_id=1, source_target_pairs={{0,4},{1,5},{2,6},{3,7},{4,0},{5,1},{6,2},{7,3},{8,12},{9,13},{10,... | collective-permute-start | bytes 1032200 | tf_op jit(solution)/shard_map/ppermute | solution.py:229
  564.7 21.9 %collective-permute-start.21 = (bf16[96,768]{1,0:T(8,128)(2,1)S(1)}, bf16[96,768]{1,0:T(8,128)(2,1)S(1)}, u32[]{:S(2)}, u32[]{:S(2)}) collective-permute-start(bf16[96,768]{1,0:T(8,128)(2,1)S(1)} %fusion.41), channel_id=1, source_target_pairs={{0,4},{1,5},{2,6},{3,7},{4,0},{5,1},{6,2},{7,3},{8,12},{9,13},{10,... | collective-permute-start | bytes 442376 | tf_op jit(solution)/shard_map/ppermute | solution.py:229
  583.5 11.2 %collective-permute-start.29 = (bf16[224,768]{1,0:T(8,128)(2,1)S(1)}, bf16[224,768]{1,0:T(8,128)(2,1)S(1)}, u32[]{:S(2)}, u32[]{:S(2)}) collective-permute-start(bf16[224,768]{1,0:T(8,128)(2,1)S(1)} %fusion.33), channel_id=1, source_target_pairs={{0,4},{1,5},{2,6},{3,7},{4,0},{5,1},{6,2},{7,3},{8,12},{9,13},{10,... | collective-permute-start | bytes 1032200 | tf_op jit(solution)/shard_map/ppermute | solution.py:229
  587.4 14.1 %collective-permute-start.22 = (bf16[192,768]{1,0:T(8,128)(2,1)}, bf16[192,768]{1,0:T(8,128)(2,1)}, u32[]{:S(2)}, u32[]{:S(2)}) collective-permute-start(bf16[192,768]{1,0:T(8,128)(2,1)} %pad_maximum_fusion.20), channel_id=1, source_target_pairs={{0,2},{1,3},{2,0},{3,1},{4,6},{5,7},{6,4},{7,5},{8,10},{9,11},{10,... | collective-permute-start | bytes 884744 | tf_op jit(solution)/shard_map/ppermute | solution.py:229
  595.6 16.4 %collective-permute-start.30 = (bf16[448,768]{1,0:T(8,128)(2,1)}, bf16[448,768]{1,0:T(8,128)(2,1)}, u32[]{:S(2)}, u32[]{:S(2)}) collective-permute-start(bf16[448,768]{1,0:T(8,128)(2,1)} %pad_maximum_fusion.14), channel_id=1, source_target_pairs={{0,2},{1,3},{2,0},{3,1},{4,6},{5,7},{6,4},{7,5},{8,10},{9,11},{10,... | collective-permute-start | bytes 2064392 | tf_op jit(solution)/shard_map/ppermute | solution.py:229
  602.7 12.0 %collective-permute-start.23 = (bf16[384,768]{1,0:T(8,128)(2,1)S(1)}, bf16[384,768]{1,0:T(8,128)(2,1)S(1)}, u32[]{:S(2)}, u32[]{:S(2)}) collective-permute-start(bf16[384,768]{1,0:T(8,128)(2,1)S(1)} %pad_maximum_fusion.18), channel_id=1, source_target_pairs={{0,1},{1,0},{2,3},{3,2},{4,5},{5,4},{6,7},{7,6},{8,9},{9,8},{10,11... | collective-permute-start | bytes 1769480 | tf_op jit(solution)/shard_map/ppermute | solution.py:229
  613.4 28.7 %collective-permute-start.31 = (bf16[896,768]{1,0:T(8,128)(2,1)S(1)}, bf16[896,768]{1,0:T(8,128)(2,1)S(1)}, u32[]{:S(2)}, u32[]{:S(2)}) collective-permute-start(bf16[896,768]{1,0:T(8,128)(2,1)S(1)} %pad_maximum_fusion.11), channel_id=1, source_target_pairs={{0,1},{1,0},{2,3},{3,2},{4,5},{5,4},{6,7},{7,6},{8,9},{9,8},{10,11... | collective-permute-start | bytes 4128776 | tf_op jit(solution)/shard_map/ppermute | solution.py:229
  (84 other events, 401.6 us)

commit v2 on v1

v2 whole, which is shorter than its diff:
```python
import functools
import math

import jax
import jax.numpy as jnp
import numpy as np
from jax import lax
from jax.experimental import pallas as pl
from jax.experimental.pallas import tpu as pltpu
from jax.sharding import PartitionSpec as P

HEAD_WIDTH = 64
HALO = 2
EPS = 1e-06
NEG_FILL = -1e30
BLOCK = 256
LANES = 128
FF_BLOCK = 512
SCALE = HEAD_WIDTH**-0.5
LOG_SCALE = SCALE * math.log2(math.e)
F32 = jnp.float32
BF16 = jnp.bfloat16


def dot_last(a, b):
    return lax.dot_general(a, b, (((1,), (1,)), ((), ())), preferred_element_type=F32)


def dot_plain(a, b):
    return lax.dot_general(a, b, (((1,), (0,)), ((), ())), preferred_element_type=F32)


def one_head(pair, head):
    lane = lax.broadcasted_iota(jnp.int32, pair.shape, 1)
    keep = (lane < HEAD_WIDTH) if head == 0 else (lane >= HEAD_WIDTH)
    return jnp.where(keep, pair, jnp.zeros_like(pair))


def diagonal(size):
    rows = lax.broadcasted_iota(jnp.int32, (size, size), 0)
    return rows == lax.broadcasted_iota(jnp.int32, (size, size), 1)


def row_of(ref):
    return ref[...].astype(F32).reshape(1, -1)


def params(megabytes):
    return pltpu.CompilerParams(vmem_limit_bytes=megabytes << 20)


def cost(flops, moved):
    return pl.CostEstimate(flops=flops, bytes_accessed=moved, transcendentals=0)


def whole(shape):
    return pl.BlockSpec(shape, lambda *_: (0,) * len(shape))


def held(shape):
    return pl.BlockSpec(shape, lambda *_: (0,) * len(shape), pipeline_mode=pl.Buffered(1))


def embed_kernel(
    stamps_ref,
    count_ref,
    visible_ref,
    pixels_ref,
    w_ref,
    b_ref,
    gain_ref,
    shift_ref,
    wave_ref,
    stream_ref,
    normed_ref,
    high_ref,
    low_ref,
    tail_ref,
    head_ref,
    flags_ref,
    edge_ref,
    time_ref,
    col_ref,
    n_ref,
):
    at_row = pl.program_id(0)
    width = w_ref.shape[1]
    frames, tile_rows, tile_cols = visible_ref.shape
    line = frames * tile_cols
    band = HALO * line

    lane = lax.broadcasted_iota(jnp.int32, (1, width), 1)
    t_end, r_end = width // 4, width // 4 + width * 3 // 8
    t_mid, r_mid, c_mid = width // 8, t_end + width * 3 // 16, r_end + width * 3 // 16

    def waves(places):
        angles = places * wave_ref[...]
        is_sin = (lane < t_mid) | ((lane >= t_end) & (lane < r_mid)) | ((lane >= r_end) & (lane < c_mid))
        return jnp.where(is_sin, jnp.sin(angles), jnp.cos(angles))

    @pl.when(at_row == 0)
    def _():
        slot = lax.broadcasted_iota(jnp.int32, (8, 1), 0)
        stamps = jnp.zeros((8, 1), F32)
        for f in range(frames):
            stamps = jnp.where(slot == f, stamps_ref[f].astype(F32), stamps)
        time_ref[...] = jnp.where(lane < t_end, waves(stamps), 0.0)
        cols = lax.axis_index("col") * tile_cols + lax.broadcasted_iota(
            jnp.int32, (tile_cols, 1), 0
        )
        col_ref[...] = jnp.where(lane >= r_end, waves(cols.astype(F32)), 0.0)
        frame_at = lax.broadcasted_iota(jnp.int32, visible_ref.shape, 0)
        ok = ((frame_at < count_ref[0]) & (visible_ref[...] == 1)).astype(F32)
        pieces = [ok[f, r : r + 1, :] for r in range(tile_rows) for f in range(frames)]
        flat = jnp.concatenate(pieces, 1)
        flags_ref[...] = jnp.broadcast_to(flat, flags_ref.shape)
        edge_ref[...] = jnp.zeros_like(edge_ref)
        nothing = [jnp.zeros((8 - frames, tile_cols), F32)]
        stacked = jnp.concatenate(
            sum((pieces[r * frames : (r + 1) * frames] + nothing for r in range(tile_rows)), []), 0
        )
        slot = lax.broadcasted_iota(jnp.int32, (8, tile_cols), 0)
        col = lax.broadcasted_iota(jnp.int32, (8, tile_cols), 1)
        last = HALO * tile_rows
        chunk = 8 * tile_rows
        edge_ref[0, last, :, :chunk] = dot_last(
            (col == slot + tile_cols - HALO).astype(F32), stacked
        )
        edge_ref[1, last, :, :chunk] = dot_last((col == slot).astype(F32), stacked)

    places = (lax.axis_index("row") * tile_rows + at_row).astype(F32)
    row_part = jnp.where((lane >= t_end) & (lane < r_end), waves(jnp.full((1, 1), places)), 0.0)
    base = row_of(b_ref) + row_part
    stream = dot_plain(pixels_ref[...], w_ref[...])
    position = jnp.concatenate(
        [col_ref[...] + (time_ref[f : f + 1, :] + base) for f in range(frames)], 0
    )
    stream = stream + position
    stream_ref[...] = stream
    centre = stream - jnp.mean(stream, -1, keepdims=True)
    spread = jnp.mean(centre * centre, -1, keepdims=True)
    normed = centre * lax.rsqrt(spread + EPS) * row_of(gain_ref) + row_of(shift_ref)
    low = normed.astype(BF16)
    normed_ref[...] = low
    n_ref[...] = low.astype(F32)
    for j in range(HALO):
        target = j * tile_rows + at_row
        for f in range(frames):
            near = f * tile_cols + j
            far = near + tile_cols - HALO
            edge_ref[0, target, f : f + 1, :] = n_ref[far : far + 1, :]
            edge_ref[1, target, f : f + 1, :] = n_ref[near : near + 1, :]

    @pl.when(at_row < HALO)
    def _():
        low_ref[pl.ds(pl.multiple_of(at_row * line, line), line), :] = low

    @pl.when(at_row >= tile_rows - HALO)
    def _():
        start = (at_row - (tile_rows - HALO)) * line
        high_ref[pl.ds(pl.multiple_of(start, line), line), :] = low

    @pl.when(at_row == tile_rows - 1)
    def _():
        tail_ref[...] = edge_ref[0].reshape(tail_ref.shape).astype(BF16)
        head_ref[...] = edge_ref[1].reshape(head_ref.shape).astype(BF16)
        zeros = jnp.zeros((8, width - band), BF16)
        total = flags_ref.shape[1]
        low_ref[band : band + 8, :band] = flags_ref[:, :band].astype(BF16)
        low_ref[band : band + 8, band:] = zeros
        high_ref[band : band + 8, :band] = flags_ref[:, total - band :].astype(BF16)
        high_ref[band : band + 8, band:] = zeros


def embed(stamps, count, visible, pixels, w, b, gain, shift, wave):
    tokens, depth = pixels.shape
    width = w.shape[1]
    frames, tile_rows, tile_cols = visible.shape
    line = frames * tile_cols
    band = HALO * line
    side = HALO * tile_rows * 8
    smem = pl.BlockSpec(memory_space=pltpu.SMEM)
    block = pl.BlockSpec((line, width), lambda r: (r, 0))
    return pl.pallas_call(
        embed_kernel,
        grid=(tile_rows,),
        in_specs=[
            smem,
            smem,
            whole(visible.shape),
            pl.BlockSpec((line, depth), lambda r: (r, 0)),
            held(w.shape),
            whole((width,)),
            whole((width,)),
            whole((width,)),
            whole((1, width)),
        ],
        out_specs=[
            block,
            block,
            whole((band + 8, width)),
            whole((band + 8, width)),
            whole((side + 8, width)),
            whole((side + 8, width)),
            whole((8, tokens)),
        ],
        out_shape=[
            jax.ShapeDtypeStruct((tokens, width), F32),
            jax.ShapeDtypeStruct((tokens, width), BF16),
            jax.ShapeDtypeStruct((band + 8, width), BF16),
            jax.ShapeDtypeStruct((band + 8, width), BF16),
            jax.ShapeDtypeStruct((side + 8, width), BF16),
            jax.ShapeDtypeStruct((side + 8, width), BF16),
            jax.ShapeDtypeStruct((8, tokens), F32),
        ],
        scratch_shapes=[
            pltpu.VMEM((2, side // 8 + 1, 8, width), F32),
            pltpu.VMEM((8, width), F32),
            pltpu.VMEM((tile_cols, width), F32),
            pltpu.VMEM((line, width), F32),
        ],
        compiler_params=params(60),
        cost_estimate=cost(2 * tokens * depth * width, 10 << 20),
        name="embed",
    )(stamps, count, visible, pixels, w, b, gain, shift, wave)


def decode_back_kernel(
    cot_ref, w_pix_ref, w_dec_ref, dec_ref, out_ref, mlp_ref, sum_pix, sum_dec, sum_down
):
    @pl.when(pl.program_id(0) == 0)
    def _():
        sum_pix[...] = jnp.zeros_like(sum_pix)
        sum_dec[...] = jnp.zeros_like(sum_dec)
        sum_down[...] = jnp.zeros_like(sum_down)

    grad_dec = dot_last(cot_ref[...], w_pix_ref[...]).astype(BF16)
    dec_ref[...] = grad_dec
    grad_out = dot_last(grad_dec, w_dec_ref[...])
    out_ref[...] = grad_out
    low = grad_out.astype(BF16)
    mlp_ref[...] = low
    sum_pix[...] += jnp.sum(cot_ref[...].astype(F32), 0, keepdims=True)
    sum_dec[...] += jnp.sum(grad_dec.astype(F32), 0, keepdims=True)
    sum_down[...] += jnp.sum(low.astype(F32), 0, keepdims=True)


def decode_back(cot, w_pix, w_dec):
    tokens, pix = cot.shape
    width, dec = w_dec.shape

    def block(size):
        return pl.BlockSpec((BLOCK, size), lambda i: (i, 0))

    return pl.pallas_call(
        decode_back_kernel,
        grid=(tokens // BLOCK,),
        in_specs=[block(pix), held(w_pix.shape), held(w_dec.shape)],
        out_specs=[
            block(dec),
            block(width),
            block(width),
            whole((1, pix)),
            whole((1, dec)),
            whole((1, width)),
        ],
        out_shape=[
            jax.ShapeDtypeStruct((tokens, dec), BF16),
            jax.ShapeDtypeStruct((tokens, width), F32),
            jax.ShapeDtypeStruct((tokens, width), BF16),
            jax.ShapeDtypeStruct((1, pix), F32),
            jax.ShapeDtypeStruct((1, dec), F32),
            jax.ShapeDtypeStruct((1, width), F32),
        ],
        compiler_params=params(16),
        cost_estimate=cost(2 * tokens * dec * (pix + width), 10 << 20),
        name="decode_back",
    )(cot, w_pix, w_dec)


def own_qkv_kernel(x_ref, w_ref, bq_ref, bv_ref, q_ref, k_ref, v_ref):
    width = x_ref.shape[1]
    x = x_ref[...]
    q_ref[...] = (dot_plain(x, w_ref[:, :width]) + row_of(bq_ref)).astype(BF16)
    k_ref[...] = dot_plain(x, w_ref[:, width : 2 * width]).astype(BF16)
    v_ref[...] = (dot_plain(x, w_ref[:, 2 * width :]) + row_of(bv_ref)).astype(BF16)


def own_qkv(x, w, bq, bv):
    tokens, width = x.shape
    block = pl.BlockSpec((BLOCK, width), lambda i: (i, 0))
    return pl.pallas_call(
        own_qkv_kernel,
        grid=(tokens // BLOCK,),
        in_specs=[block, held(w.shape), whole((width,)), whole((width,))],
        out_specs=[block] * 3,
        out_shape=[jax.ShapeDtypeStruct((tokens, width), BF16)] * 3,
        compiler_params=params(16),
        cost_estimate=cost(6 * tokens * width * width, 8 << 20),
        name="own_qkv",
    )(x, w, bq, bv)


def strip_kv_kernel(
    reach_ref, upper_ref, lower_ref, left_ref, right_ref, flags_ref, w_ref, bv_ref,
    k_ref, v_ref, rows_ref, bias_ref,
):
    band = upper_ref.shape[0] - 8
    side = left_ref.shape[0] - 8
    tokens = flags_ref.shape[1]
    total = rows_ref.shape[0]
    at = pl.program_id(0)

    @pl.when(at == 0)
    def _():
        rows_ref[:band, :] = upper_ref[:band, :]
        rows_ref[band : 2 * band, :] = lower_ref[:band, :]
        rows_ref[2 * band : 2 * band + side, :] = left_ref[:side, :]
        rows_ref[2 * band + side : 2 * (band + side), :] = right_ref[:side, :]
        if total > 2 * (band + side):
            rows_ref[2 * (band + side) :, :] = jnp.zeros(
                (total - 2 * (band + side), rows_ref.shape[1]), BF16
            )
        reach = reach_ref[0]
        line = band // HALO
        where = lax.broadcasted_iota(jnp.int32, (1, band), 1) // line
        near = (reach >= where + 1).astype(F32)
        far = (reach >= HALO - where).astype(F32)
        upper_ok = upper_ref[band : band + 1, :band].astype(F32) * far
        lower_ok = lower_ref[band : band + 1, :band].astype(F32) * near
        chunk = side // HALO
        spare = total - 2 * band
        source = lax.broadcasted_iota(jnp.int32, (LANES, spare), 0)
        target = lax.broadcasted_iota(jnp.int32, (LANES, spare), 1)
        sides = jnp.zeros((8, spare), F32)
        for j in range(HALO):
            for part, ref, need in ((0, left_ref, HALO - j), (1, right_ref, j + 1)):
                place = (target == source + part * side + j * chunk) & (source < chunk)
                line_ok = jnp.broadcast_to(
                    ref[side : side + 8, :LANES].astype(F32)[j : j + 1], (8, LANES)
                )
                moved = dot_plain(line_ok.astype(BF16), place.astype(BF16))
                sides = sides + jnp.where(reach >= need, moved, 0.0)
        bias_ref[:, :tokens] = jnp.where(flags_ref[...] > 0.5, 0.0, NEG_FILL)
        bias_ref[:, tokens : tokens + band] = jnp.broadcast_to(
            jnp.where(upper_ok > 0.5, 0.0, NEG_FILL), (8, band)
        )
        bias_ref[:, tokens + band : tokens + 2 * band] = jnp.broadcast_to(
            jnp.where(lower_ok > 0.5, 0.0, NEG_FILL), (8, band)
        )
        bias_ref[:, tokens + 2 * band :] = jnp.where(sides > 0.5, 0.0, NEG_FILL)
        k_ref[...] = dot_plain(rows_ref[...], w_ref[...]).astype(BF16)

    @pl.when(at == 1)
    def _():
        v_ref[...] = (dot_plain(rows_ref[...], w_ref[...]) + row_of(bv_ref)).astype(BF16)


def strip_kv(reach, upper, lower, left, right, flags, w, bv):
    width = w.shape[0]
    tokens = flags.shape[1]
    keys = 2 * (upper.shape[0] - 8) + 2 * (left.shape[0] - 8)
    total = -(-(tokens + keys) // LANES) * LANES - tokens
    strip = jax.ShapeDtypeStruct((total, width), BF16)
    return pl.pallas_call(
        strip_kv_kernel,
        grid=(2,),
        in_specs=[
            pl.BlockSpec(memory_space=pltpu.SMEM),
            whole(upper.shape),
            whole(lower.shape),
            whole(left.shape),
            whole(right.shape),
            whole(flags.shape),
            pl.BlockSpec((width, width), lambda i: (0, i + 1)),
            whole((width,)),
        ],
        out_specs=[whole((total, width))] * 3 + [whole((8, tokens + total))],
        out_shape=[strip] * 3 + [jax.ShapeDtypeStruct((8, tokens + total), F32)],
        compiler_params=params(16),
        cost_estimate=cost(4 * total * width * width, 8 << 20),
        name="strip_kv",
    )(reach, upper, lower, left, right, flags, w, bv)


def attend_kernel(
    q_ref, k_ref, v_ref, ks_ref, vs_ref, bias_ref, out_ref, log_ref, s_ref, keys_ref, values_ref
):
    tokens = q_ref.shape[0]
    keys_ref[:tokens, :] = k_ref[...]
    keys_ref[tokens:, :] = ks_ref[...]
    values_ref[:tokens, :] = v_ref[...]
    values_ref[tokens:, :] = vs_ref[...]
    eye = diagonal(BLOCK)
    lane = lax.broadcasted_iota(jnp.int32, (BLOCK, LANES), 1)

    def step(i, carry):
        at = pl.multiple_of(i * BLOCK, BLOCK)
        q = q_ref[pl.ds(at, BLOCK), :]
        mixed = []
        for head in range(2):
            q_head = one_head(q, head)
            s_ref[head] = dot_last(q_head, keys_ref[...]) + bias_ref[0:1, :]
            own = dot_last(q_head, keys_ref[pl.ds(at, BLOCK), :])
            s_ref[head, :, pl.ds(at, BLOCK)] = jnp.where(
                eye, own, own + bias_ref[0:1, pl.ds(at, BLOCK)]
            )
            scores = s_ref[head]
            top = jnp.max(scores, axis=1, keepdims=True)
            weights = jnp.exp2(scores * LOG_SCALE - top * LOG_SCALE)
            total = jnp.sum(weights, axis=1, keepdims=True)
            mixed.append(dot_plain(weights.astype(BF16), values_ref[...]) / total)
            log_ref[0, head, pl.ds(at, BLOCK)] = (top * LOG_SCALE + jnp.log2(total))[:, 0]
        out_ref[pl.ds(at, BLOCK), :] = jnp.where(lane < HEAD_WIDTH, mixed[0], mixed[1]).astype(
            out_ref.dtype
        )
        return carry

    lax.fori_loop(0, tokens // BLOCK, step, 0)


def attend(q, k, v, ks, vs, bias):
    tokens, width = q.shape
    keys = tokens + ks.shape[0]
    pairs = width // LANES
    own = pl.BlockSpec((tokens, LANES), lambda p: (0, p))
    strip = pl.BlockSpec((keys - tokens, LANES), lambda p: (0, p))
    return pl.pallas_call(
        attend_kernel,
        grid=(pairs,),
        in_specs=[own, own, own, strip, strip, whole((8, keys))],
        out_specs=[own, pl.BlockSpec((1, 2, tokens), lambda p: (p, 0, 0))],
        out_shape=[
            jax.ShapeDtypeStruct((tokens, width), F32),
            jax.ShapeDtypeStruct((pairs, 2, tokens), F32),
        ],
        scratch_shapes=[
            pltpu.VMEM((2, BLOCK, keys), F32),
            pltpu.VMEM((keys, LANES), BF16),
            pltpu.VMEM((keys, LANES), BF16),
        ],
        compiler_params=params(24),
        cost_estimate=cost(16 * tokens * keys * width, 8 << 20),
        name="attend",
    )(q, k, v, ks, vs, bias)


def attend_back_kernel(
    q_ref, k_ref, v_ref, ks_ref, vs_ref, do_ref, o_ref, log_ref, bias_ref,
    dq_ref, dk_ref, dv_ref, dks_ref, dvs_ref, sum_q, sum_v,
    keys_ref, values_ref, kt_ref, dk_sum, dv_sum, mask_ref,
):
    tokens = q_ref.shape[0]
    keys_ref[:tokens, :] = k_ref[...]
    keys_ref[tokens:, :] = ks_ref[...]
    values_ref[:tokens, :] = v_ref[...]
    values_ref[tokens:, :] = vs_ref[...]
    kt_ref[...] = keys_ref[...].T

    @pl.when(pl.program_id(0) == 0)
    def _():
        mask_ref[...] = bias_ref[...].T[:, 0:1]

    eye = diagonal(BLOCK)
    dk_sum[...] = jnp.zeros_like(dk_sum)
    dv_sum[...] = jnp.zeros_like(dv_sum)

    def step(i, carry):
        at = pl.multiple_of(i * BLOCK, BLOCK)
        q = q_ref[pl.ds(at, BLOCK), :]
        do = do_ref[pl.ds(at, BLOCK), :]
        product = (do.astype(F32) * o_ref[pl.ds(at, BLOCK), :]).T
        parts = []
        for head in range(2):
            delta = jnp.sum(
                product[head * HEAD_WIDTH : (head + 1) * HEAD_WIDTH], axis=0, keepdims=True
            )
            q_head = one_head(q, head)
            do_head = one_head(do, head)
            log_total = log_ref[0, pl.ds(head, 1), pl.ds(at, BLOCK)]
            scores = dot_last(keys_ref[...], q_head) + mask_ref[...]
            weights = jnp.exp2(scores * LOG_SCALE - log_total)
            back = dot_last(values_ref[...], do_head)
            grad = (weights * (back - delta)).astype(BF16)
            own_scores = dot_last(keys_ref[pl.ds(at, BLOCK), :], q_head)
            own = jnp.where(
                eye & (mask_ref[pl.ds(at, BLOCK), :] < 0),
                jnp.exp2(own_scores * LOG_SCALE - log_total),
                0.0,
            )
            own_back = dot_last(values_ref[pl.ds(at, BLOCK), :], do_head)
            own_grad = (own * (own_back - delta)).astype(BF16)
            dv_sum[...] += dot_plain(weights.astype(BF16), do_head)
            dv_sum[pl.ds(at, BLOCK), :] += dot_plain(own.astype(BF16), do_head)
            dk_sum[...] += dot_plain(grad, q_head)
            dk_sum[pl.ds(at, BLOCK), :] += dot_plain(own_grad, q_head)
            parts.append(
                dot_plain(kt_ref[...], grad) + dot_plain(kt_ref[:, pl.ds(at, BLOCK)], own_grad)
            )
        joined = jnp.concatenate([parts[0][:HEAD_WIDTH], parts[1][HEAD_WIDTH:]], axis=0)
        dq_ref[pl.ds(at, BLOCK), :] = (joined.T * SCALE).astype(BF16)
        return carry

    lax.fori_loop(0, tokens // BLOCK, step, 0)
    dk = (dk_sum[...] * SCALE).astype(BF16)
    dv = dv_sum[...].astype(BF16)
    dk_ref[...] = dk[:tokens]
    dks_ref[...] = dk[tokens:]
    dv_ref[...] = dv[:tokens]
    dvs_ref[...] = dv[tokens:]
    sum_q[...] = jnp.sum(dq_ref[...].astype(F32), 0, keepdims=True)
    sum_v[...] = jnp.sum(dv.astype(F32), 0, keepdims=True)


def attend_back(q, k, v, ks, vs, do, o, log_total, bias, first, count, before, after):
    tokens, width = q.shape
    keys = tokens + ks.shape[0]
    own = pl.BlockSpec((tokens, LANES), lambda p: (0, p + first))
    strip = pl.BlockSpec((keys - tokens, LANES), lambda p: (0, p + first))
    line = pl.BlockSpec((1, LANES), lambda p: (0, p + first))
    return run(
        attend_back_kernel, "attend_back", (q, k, v, ks, vs, do, o, log_total, bias),
        [jax.ShapeDtypeStruct((tokens, width), BF16)] * 3
        + [jax.ShapeDtypeStruct((keys - tokens, width), BF16)] * 2
        + [jax.ShapeDtypeStruct((1, width), F32)] * 2,
        [
            own, own, own, strip, strip, own, own,
            pl.BlockSpec((1, 2, tokens), lambda p: (p + first, 0, 0)),
            whole((8, keys)),
        ],
        [own, own, own, strip, strip, line, line], grid=(count,), after=tuple(before) + tuple(after),
        aliases={9 + i: i for i in range(len(before))},
        estimate=cost(24 * tokens * keys * LANES * count, 3 * count << 20),
        scratch=[
            pltpu.VMEM((keys, LANES), BF16),
            pltpu.VMEM((keys, LANES), BF16),
            pltpu.VMEM((LANES, keys), BF16),
            pltpu.VMEM((keys, LANES), F32),
            pltpu.VMEM((keys, LANES), F32),
            pltpu.VMEM((keys, 1), F32),
        ],
    )


def dot_first(a, b):
    return lax.dot_general(a, b, (((0,), (0,)), ((), ())), preferred_element_type=F32)


def mlp_kernel(
    one_ref, att_ref, gout_ref, w_out_ref, b_out_ref, gain_ref, shift_ref, w_up_ref, b_up_ref,
    w_down_ref, b_down_ref, w_dec_ref, b_dec_ref, w_pix_ref, b_pix_ref,
    pix_ref, normed_ref, act_ref, gup_ref, low_ref, decoded_ref, attended_ref,
    gtwo_ref, gatt_ref, gattended_ref, sum_up, sum_out, sum_gain, sum_shift,
):
    @pl.when(pl.program_id(0) == 0)
    def _():
        for ref in (sum_up, sum_out, sum_gain, sum_shift):
            ref[...] = jnp.zeros_like(ref)

    ff = w_up_ref.shape[1]
    attended = att_ref[...].astype(BF16)
    attended_ref[...] = attended
    two = one_ref[...] + dot_plain(attended, w_out_ref[...]) + row_of(b_out_ref)
    centre = two - jnp.mean(two, -1, keepdims=True)
    inverse = lax.rsqrt(jnp.mean(centre * centre, -1, keepdims=True) + EPS)
    gain = row_of(gain_ref)
    normed = (centre * inverse * gain + row_of(shift_ref)).astype(BF16)
    normed_ref[...] = normed
    gout = gout_ref[...]
    gmlp = gout.astype(BF16)
    out = two + row_of(b_down_ref)
    gnormed = jnp.zeros_like(two)
    for at in range(0, ff, FF_BLOCK):
        cols = slice(at, at + FF_BLOCK)
        up = dot_plain(normed, w_up_ref[:, cols]) + b_up_ref[cols].astype(F32).reshape(1, -1)
        bell = 0.5 * (1.0 + lax.erf(up * math.sqrt(0.5)))
        act = (up * bell).astype(BF16)
        slope = bell + up * (jnp.exp2(up * up * (-0.5 * math.log2(math.e))) * (2 * math.pi) ** -0.5)
        act_ref[:, cols] = act
        out = out + dot_plain(act, w_down_ref[cols, :])
        gup = (dot_last(gmlp, w_down_ref[cols, :]) * slope).astype(BF16)
        gup_ref[:, cols] = gup
        sum_up[:, cols] += jnp.sum(gup.astype(F32), 0, keepdims=True)
        gnormed = gnormed + dot_last(gup, w_up_ref[:, cols])
    low = out.astype(BF16)
    low_ref[...] = low
    decoded = (dot_plain(low, w_dec_ref[...]) + row_of(b_dec_ref)).astype(BF16)
    decoded_ref[...] = decoded
    pix_ref[...] = (dot_plain(decoded, w_pix_ref[...]) + row_of(b_pix_ref)).astype(BF16)
    hat = centre * inverse
    sum_gain[...] += jnp.sum(gnormed * hat, 0, keepdims=True)
    sum_shift[...] += jnp.sum(gnormed, 0, keepdims=True)
    scaled = gnormed * gain
    back = inverse * (
        scaled
        - jnp.mean(scaled, -1, keepdims=True)
        - hat * jnp.mean(scaled * hat, -1, keepdims=True)
    )
    gtwo = gout + back
    gtwo_ref[...] = gtwo
    gatt = gtwo.astype(BF16)
    gatt_ref[...] = gatt
    sum_out[...] += jnp.sum(gatt.astype(F32), 0, keepdims=True)
    gattended_ref[...] = dot_last(gatt, w_out_ref[...]).astype(BF16)


def mlp(one, att, gout, w_out, b_out, gain, shift, w_up, b_up, w_down, b_down, w_dec, b_dec, w_pix, b_pix):
    tokens, width = one.shape
    ff, dec, pix = w_up.shape[1], w_dec.shape[1], w_pix.shape[1]

    def block(size):
        return pl.BlockSpec((BLOCK, size), lambda i: (i, 0))

    def out(size, kind=BF16):
        return jax.ShapeDtypeStruct((tokens, size), kind)

    def vector(size):
        return jax.ShapeDtypeStruct((1, size), F32)

    weights = [w_out, b_out, gain, shift, w_up, b_up, w_down, b_down, w_dec, b_dec, w_pix, b_pix]
    return pl.pallas_call(
        mlp_kernel,
        grid=(tokens // BLOCK,),
        in_specs=[block(width)] * 3 + [held(item.shape) for item in weights],
        out_specs=[
            block(pix), block(width), block(ff), block(ff), block(width), block(dec), block(width),
            block(width), block(width), block(width),
            whole((1, ff)), whole((1, width)), whole((1, width)), whole((1, width)),
        ],
        out_shape=[
            out(pix), out(width), out(ff), out(ff), out(width), out(dec), out(width),
            out(width, F32), out(width), out(width),
            vector(ff), vector(width), vector(width), vector(width),
        ],
        compiler_params=params(48),
        cost_estimate=cost(2 * tokens * width * (2 * width + 4 * ff + dec) + 2 * tokens * dec * pix, 40 << 20),
        name="mlp",
    )(one, att, gout, *weights)


def quarter_at(step, core):
    return 2 * (step % 2) + jnp.where(step < 2, 1 - core, core)


def lay_columns(ref, at, values, width):
    rows, cols = values.shape
    for i in range(cols // width):
        ref[0, at + i * rows : at + (i + 1) * rows, :] = values[:, i * width : (i + 1) * width]


def padded(rows):
    granule = 8 * lax.axis_size("col")
    return -(-rows // granule) * granule


def blank(ref, at):
    if at < ref.shape[1]:
        ref[0, at:, :] = jnp.zeros((ref.shape[1] - at, ref.shape[2]), BF16)


def pair_specs(rows, width):
    return [
        pl.BlockSpec((1, rows, width), lambda s, c: (jnp.minimum(s, 1), 0, 0)),
        pl.BlockSpec((1, rows, width), lambda s, c: (jnp.maximum(s - 2, 0), 0, 0)),
    ]


def grads_down_kernel(
    places, act_ref, gmlp_ref, decoded_ref, cot_ref, low_ref, gdec_ref, send_ref, keep_ref, lt_ref
):
    step = pl.program_id(0)

    @pl.when(step == 0)
    def _():
        lt_ref[...] = low_ref[...].T

    width = gmlp_ref.shape[1]
    part = width // 4
    rows = pl.ds(pl.multiple_of(quarter_at(step, places[0]) * part, part), part)
    down = dot_first(act_ref[...], gmlp_ref[...]).astype(BF16)
    pix = dot_first(decoded_ref[...], cot_ref[...]).astype(BF16)
    dec = dot_plain(lt_ref[rows, :], gdec_ref[...]).astype(BF16)
    at = down.shape[0] + pix.size // width
    cut, side = part * 2 // 3, dec.shape[1]
    rest = width - side
    for is_sent, ref in ((True, send_ref), (False, keep_ref)):

        @pl.when((step < 2) == is_sent)
        def _():
            ref[0, : down.shape[0], :] = down
            lay_columns(ref, down.shape[0], pix, width)
            ref[0, at : at + cut, :side] = dec[:cut]
            ref[0, at : at + part - cut, side:] = dec[cut:, :rest]
            ref[0, at + part - cut : at + cut, side:] = dec[cut:, rest:]
            blank(ref, at + cut)


def grads_down(places, act, gmlp, decoded, cot, low, gdec):
    tokens, ff = act.shape
    width, dec, pix = gmlp.shape[1], decoded.shape[1], cot.shape[1]
    rows = padded(ff // 4 + (dec // 4) * (pix // width) + dec // 4)
    return run(
        grads_down_kernel, "grads_down", (act, gmlp, decoded, cot, low, gdec),
        [jax.ShapeDtypeStruct((2, rows, width), BF16)] * 2,
        [
            pl.BlockSpec((tokens, ff // 4), lambda s, c: (0, quarter_at(s, c[0]))),
            held(gmlp.shape),
            pl.BlockSpec((tokens, dec // 4), lambda s, c: (0, quarter_at(s, c[0]))),
            held(cot.shape),
            held(low.shape),
            held(gdec.shape),
        ],
        pair_specs(rows, width), grid=(4,), places=places,
        estimate=cost(2 * tokens * (ff * width + dec * (pix + width)), 20 << 20),
        megabytes=32, scratch=[pltpu.VMEM((width, tokens), BF16)],
    )


def grads_up_kernel(
    places, normed_ref, gup_ref, att_ref, gatt_ref, send_ref, keep_ref, nt_ref, at_ref
):
    step = pl.program_id(0)

    @pl.when(step == 0)
    def _():
        nt_ref[...] = normed_ref[...].T
        at_ref[...] = att_ref[...].T

    width = normed_ref.shape[1]
    part = width // 4
    rows = pl.ds(pl.multiple_of(quarter_at(step, places[0]) * part, part), part)
    up = dot_plain(nt_ref[rows, :], gup_ref[...]).astype(BF16)
    out = dot_plain(at_ref[rows, :], gatt_ref[...]).astype(BF16)
    at = up.size // width
    for is_sent, ref in ((True, send_ref), (False, keep_ref)):

        @pl.when((step < 2) == is_sent)
        def _():
            lay_columns(ref, 0, up, width)
            ref[0, at : at + part, :] = out
            blank(ref, at + part)


def grads_up(places, normed, gup, attended, gatt, after):
    tokens, width = normed.shape
    ff = gup.shape[1]
    rows = padded(ff // 4 + width // 4)
    operands = (normed, gup, attended, gatt)
    return run(
        grads_up_kernel, "grads_up", operands, [jax.ShapeDtypeStruct((2, rows, width), BF16)] * 2,
        [held(item.shape) for item in operands], pair_specs(rows, width), grid=(4,), places=places,
        after=after, estimate=cost(2 * tokens * width * (ff + width), 16 << 20),
        scratch=[pltpu.VMEM((width, tokens), BF16)] * 2,
    )


def strip_back_kernel(dk_ref, dv_ref, w_ref, upper_ref, lower_ref, left_ref, right_ref):
    width = w_ref.shape[0]
    band, side = upper_ref.shape[0], left_ref.shape[0]
    back = (
        dot_last(dk_ref[...], w_ref[:, width : 2 * width]) + dot_last(dv_ref[...], w_ref[:, 2 * width :])
    ).astype(BF16)
    upper_ref[...] = back[:band]
    lower_ref[...] = back[band : 2 * band]
    left_ref[...] = back[2 * band : 2 * band + side]
    right_ref[...] = back[2 * band + side : 2 * (band + side)]


def strip_back(dk, dv, w, band, side, after):
    total, width = dk.shape
    sizes = (band, band, side, side)
    return run(
        strip_back_kernel, "strip_back", (dk, dv, w),
        [jax.ShapeDtypeStruct((rows, width), BF16) for rows in sizes],
        [whole(item.shape) for item in (dk, dv, w)], [whole((rows, width)) for rows in sizes],
        after=after, estimate=cost(4 * total * width * width, 8 << 20), megabytes=24,
    )


def grads_qkv_kernel(
    core_ref, normed_ref, rows_ref, dq_ref, dk_ref, dv_ref, dks_ref, dvs_ref,
    send_ref, keep_ref, nt_ref, st_ref,
):
    step = pl.program_id(0)

    @pl.when(step == 0)
    def _():
        nt_ref[...] = normed_ref[...].T
        st_ref[...] = rows_ref[...].T

    width = normed_ref.shape[1]
    part = width // 4
    rows = pl.ds(pl.multiple_of(quarter_at(step, core_ref[0]) * part, part), part)
    own, strip = nt_ref[rows, :], st_ref[rows, :]
    parts = (
        dot_plain(own, dq_ref[...]),
        dot_plain(own, dk_ref[...]) + dot_plain(strip, dks_ref[...]),
        dot_plain(own, dv_ref[...]) + dot_plain(strip, dvs_ref[...]),
    )
    for is_sent, ref in ((True, send_ref), (False, keep_ref)):

        @pl.when((step < 2) == is_sent)
        def _():
            for i, values in enumerate(parts):
                ref[0, i * part : (i + 1) * part, :] = values.astype(BF16)
            blank(ref, len(parts) * part)


def grads_qkv(places, normed, rows, dq, dk, dv, dks, dvs, after):
    tokens, width = normed.shape
    total = rows.shape[0]
    operands = (normed, rows, dq, dk, dv, dks, dvs)
    size = padded(3 * width // 4)
    return run(
        grads_qkv_kernel, "grads_qkv", operands, [jax.ShapeDtypeStruct((2, size, width), BF16)] * 2,
        [held(item.shape) for item in operands], pair_specs(size, width), grid=(4,), places=places,
        after=after, estimate=cost(2 * width * width * (3 * tokens + 2 * total), 20 << 20),
        scratch=[
            pltpu.VMEM((width, tokens), BF16),
            pltpu.VMEM((width, total), BF16),
        ],
    )


def embed_back_kernel(
    frames, stream_ref, dq_ref, dk_ref, dv_ref, w_ref, gtwo_ref, gain_ref, above_ref, below_ref, left_ref,
    right_ref, emb_ref, sum_patch, sum_gain, sum_shift, g_ref, side_ref,
):
    at_row = pl.program_id(0)
    width = stream_ref.shape[1]
    line = stream_ref.shape[0]
    tile_rows = left_ref.shape[0] // (8 * HALO)
    tile_cols = line // frames

    @pl.when(at_row == 0)
    def _():
        side_ref[0] = left_ref[...].astype(F32).reshape(side_ref.shape[1:])
        side_ref[1] = right_ref[...].astype(F32).reshape(side_ref.shape[1:])
        for ref in (sum_patch, sum_gain, sum_shift):
            ref[...] = jnp.zeros_like(ref)

    g_ref[...] = (
        dot_last(dq_ref[...], w_ref[:, :width])
        + dot_last(dk_ref[...], w_ref[:, width : 2 * width])
        + dot_last(dv_ref[...], w_ref[:, 2 * width :])
    )

    @pl.when(at_row < HALO)
    def _():
        g_ref[...] += above_ref[pl.ds(pl.multiple_of(at_row * line, line), line), :].astype(F32)

    @pl.when(at_row >= tile_rows - HALO)
    def _():
        start = (at_row - (tile_rows - HALO)) * line
        g_ref[...] += below_ref[pl.ds(pl.multiple_of(start, line), line), :].astype(F32)

    for j in range(HALO):
        source = j * tile_rows + at_row
        for f in range(frames):
            near = f * tile_cols + j
            far = near + tile_cols - HALO
            g_ref[near : near + 1, :] += side_ref[0, source, f : f + 1, :]
            g_ref[far : far + 1, :] += side_ref[1, source, f : f + 1, :]
    stream = stream_ref[...]
    grad = g_ref[...]
    centre = stream - jnp.mean(stream, -1, keepdims=True)
    inverse = lax.rsqrt(jnp.mean(centre * centre, -1, keepdims=True) + EPS)
    hat = centre * inverse
    sum_gain[...] += jnp.sum(grad * hat, 0, keepdims=True)
    sum_shift[...] += jnp.sum(grad, 0, keepdims=True)
    scaled = grad * row_of(gain_ref)
    one = gtwo_ref[...] + inverse * (
        scaled
        - jnp.mean(scaled, -1, keepdims=True)
        - hat * jnp.mean(scaled * hat, -1, keepdims=True)
    )
    sum_patch[...] += jnp.sum(one, 0, keepdims=True)
    emb_ref[...] = one.astype(BF16)


def embed_back(stream, dq, dk, dv, w, gtwo, gain, above, below, left, right, tile_rows, frames, hold):
    tokens, width = stream.shape
    line = tokens // tile_rows
    block = pl.BlockSpec((line, width), lambda r: (r, 0))
    vector = jax.ShapeDtypeStruct((1, width), F32)
    return run(
        functools.partial(embed_back_kernel, frames), "embed_back",
        (stream, dq, dk, dv, w, gtwo, gain, above, below, left, right),
        [jax.ShapeDtypeStruct((tokens, width), BF16)] + [vector] * 3,
        [
            block, block, block, block, held(w.shape), block, whole((width,)),
            whole(above.shape), whole(below.shape), whole(left.shape), whole(right.shape),
        ],
        [block] + [whole((1, width))] * 3, grid=(tile_rows,), hold=hold,
        estimate=cost(6 * tokens * width * width, 16 << 20),
        scratch=[pltpu.VMEM((line, width), F32), pltpu.VMEM((2, left.shape[0] // 8, 8, width), F32)],
    )


def lay_vectors(ref, at, vectors, quarter):
    width = ref.shape[2]
    ref[0, at:, :] = jnp.zeros((ref.shape[1] - at, width), BF16)
    lines = []
    for item in vectors:
        part = item.shape[1] // 4
        mine = jnp.zeros((1, part), F32)
        for q in range(4):
            mine = jnp.where(quarter == q, item[:, q * part : (q + 1) * part], mine)
        if part < width:
            mine = jnp.concatenate([mine, jnp.zeros((1, width - part), F32)], 1)
        lines.append(mine)
    pad = -(-len(lines) // 16) * 16 - len(lines)
    block = jnp.concatenate(lines + [jnp.zeros((pad, width), F32)], 0)
    high = block.astype(BF16)
    ref[0, at : at + block.shape[0], :] = high
    ref[0, at + block.shape[0] : at + 2 * block.shape[0], :] = (block - high.astype(F32)).astype(BF16)


def grads_patch_kernel(core_ref, pixels_ref, emb_ref, *refs):
    vectors, (send_ref, keep_ref) = refs[:-2], refs[-2:]
    step = pl.program_id(0)
    quarter = quarter_at(step, core_ref[0])
    patch = dot_first(pixels_ref[...], emb_ref[...]).astype(BF16)
    for is_sent, ref in ((True, send_ref), (False, keep_ref)):

        @pl.when((step < 2) == is_sent)
        def _():
            ref[0, : patch.shape[0], :] = patch
            lay_vectors(ref, patch.shape[0], [item[...] for item in vectors], quarter)


def grads_patch(places, pixels, emb, vectors, after):
    tokens, pix = pixels.shape
    width = emb.shape[1]
    rows = padded(pix // 4 + 64)
    return run(
        grads_patch_kernel, "grads_patch", (pixels, emb, *vectors),
        [jax.ShapeDtypeStruct((2, rows, width), BF16)] * 2,
        [
            pl.BlockSpec((tokens, pix // 4), lambda s, c: (0, quarter_at(s, c[0]))),
            held(emb.shape),
        ]
        + [whole(item.shape) for item in vectors],
        pair_specs(rows, width), grid=(4,), places=places, after=after,
        estimate=cost(2 * tokens * pix * width, 8 << 20),
    )


def pixel_back_kernel(emb_ref, w_ref, out_ref):
    out_ref[...] = dot_last(emb_ref[...], w_ref[...]).astype(BF16)


def pixel_back(emb, w, after):
    tokens, width = emb.shape
    pix = w.shape[0]
    return run(
        pixel_back_kernel, "pixel_back", (emb, w), jax.ShapeDtypeStruct((tokens, pix), BF16),
        [pl.BlockSpec((BLOCK, width), lambda i: (i, 0)), held(w.shape)],
        pl.BlockSpec((BLOCK, pix), lambda i: (i, 0)), grid=(tokens // BLOCK,), after=after,
        estimate=cost(2 * tokens * pix * width, 8 << 20),
    )


def swap(value, axis, stride):
    count = lax.axis_size(axis)
    return lax.ppermute(value, axis, [(i, i ^ stride) for i in range(count)])


def rotate(value, axis, steps):
    count = lax.axis_size(axis)
    return lax.ppermute(value, axis, [(i, (i + steps) % count) for i in range(count)])


def run(
    kernel, name, operands, out_shape, in_specs, out_specs, *, grid=(1,), places=None, after=(), hold=(),
    estimate=None, scratch=(), megabytes=28, aliases=None,
):
    scalars = () if places is None else (places,)
    count = len(scalars) + len(operands)
    extra = tuple(after) + tuple(hold)
    any_space = pl.BlockSpec(memory_space=pl.ANY)
    shapes = list(out_shape) if isinstance(out_shape, (list, tuple)) else [out_shape]
    specs = list(out_specs) if isinstance(out_specs, (list, tuple)) else [out_specs]
    own = len(shapes)

    def body(*refs):
        results = refs[count + len(extra) :]
        kernel(*refs[:count], *results[:own], *results[own + len(hold) :])

    at = count + len(after)
    aliases = dict(aliases or {})
    aliases.update({at + i: own + i for i in range(len(hold))})
    results = pl.pallas_call(
        body,
        grid_spec=pltpu.PrefetchScalarGridSpec(
            num_scalar_prefetch=len(scalars),
            grid=grid,
            in_specs=list(in_specs) + [any_space] * len(extra),
            out_specs=specs + [any_space] * len(hold),
            scratch_shapes=list(scratch),
        ),
        out_shape=shapes + [jax.ShapeDtypeStruct(item.shape, item.dtype) for item in hold],
        input_output_aliases=aliases,
        compiler_params=params(megabytes),
        cost_estimate=estimate,
        name=name,
    )(*scalars, *operands, *extra)
    return results[0] if len(results) == 1 else results


def add_across_kernel(places, keep_ref, came_ref, out_ref):
    out_ref[...] = (keep_ref[0].astype(F32) + came_ref[0].astype(F32)).astype(BF16)


def add_across(places, keep, came, after):
    rows, width = keep.shape[1:]
    block = pl.BlockSpec((1, rows // 2, width), lambda i, p: (1 - p[1], i, 0))
    return run(
        add_across_kernel, "add_across", (keep, came), jax.ShapeDtypeStruct((rows, width), BF16),
        [block, block], pl.BlockSpec((rows // 2, width), lambda i, p: (i, 0)),
        grid=(2,), places=places, after=after, estimate=cost(rows * width, 6 * rows * width),
        megabytes=16,
    )


def add_down_kernel(places, *refs):
    terms, (sent_ref, mine_ref) = refs[:-2], refs[-2:]
    total = sum(ref[...].reshape(sent_ref.shape).astype(F32) for ref in terms).astype(BF16)

    @pl.when(pl.program_id(0) == 0)
    def _():
        sent_ref[...] = total

    @pl.when(pl.program_id(0) == 1)
    def _():
        mine_ref[...] = total


def add_down(places, bit, terms, after, hold=()):
    rows, width = terms[-1].shape
    half = rows // 2

    def which(h, p):
        return jnp.where(h == 0, 1 - p[bit], p[bit])

    flat = pl.BlockSpec((half, width), lambda h, p: (which(h, p), 0))
    pair = pl.BlockSpec((1, half, width), lambda h, p: (p[1], which(h, p), 0))
    out = pl.BlockSpec((half, width), lambda h, p: (0, 0))
    return run(
        add_down_kernel, "add_down", terms, [jax.ShapeDtypeStruct((half, width), BF16)] * 2,
        [pair if item.ndim == 3 else flat for item in terms], [out, out],
        grid=(2,), places=places, after=after, hold=hold,
        estimate=cost(rows * width, 6 * rows * width), megabytes=16,
    )


def add_whole_kernel(a_ref, b_ref, out_ref):
    out_ref[...] = (a_ref[...].astype(F32) + b_ref[...].astype(F32)).astype(BF16)


def add_whole(a, b, after):
    return run(
        add_whole_kernel, "add_whole", (a, b), jax.ShapeDtypeStruct(a.shape, BF16),
        [whole(a.shape)] * 2, whole(a.shape), after=after, estimate=cost(a.size, 6 * a.size),
        megabytes=16,
    )


def join_kernel(bit, places, own_ref, other_ref, out_ref):
    rows = own_ref.shape[0]
    first = places[bit] == 0
    own, other = own_ref[...], other_ref[...]
    out_ref[:rows, :] = jnp.where(first, own, other)
    out_ref[rows:, :] = jnp.where(first, other, own)


def join(places, bit, own, other, after):
    rows, width = own.shape
    return run(
        functools.partial(join_kernel, bit), "join", (own, other),
        jax.ShapeDtypeStruct((2 * rows, width), BF16), [whole(own.shape)] * 2,
        whole((2 * rows, width)), places=places, after=after,
        estimate=cost(own.size, 8 * own.size), megabytes=16,
    )


def wide(full_ref, at, rows, cols, out_ref):
    width = full_ref.shape[1]
    for i in range(cols // width):
        out_ref[:, i * width : (i + 1) * width] = full_ref[at + i * rows : at + (i + 1) * rows, :]


def unfold_kernel(lay_out, ref, *refs):
    outs, full_ref = refs[:-1], refs[-1]
    full_ref[...] = ref[...].astype(F32)
    lay_out(full_ref, *outs)


def unfold(packed, lay_out, shapes):
    return run(
        functools.partial(unfold_kernel, lay_out), "unfold", (packed,),
        [jax.ShapeDtypeStruct(shape, F32) for shape in shapes], [whole(packed.shape)],
        [whole(shape) for shape in shapes], estimate=cost(packed.size, 10 * packed.size),
        megabytes=24, scratch=[pltpu.VMEM(packed.shape, F32)],
    )


def finish_kernel(bit, lay_out, places, own_ref, other_ref, *refs):
    outs, full_ref = refs[:-1], refs[-1]
    rows = own_ref.shape[0]
    first = places[bit] == 0
    own, other = own_ref[...].astype(F32), other_ref[...].astype(F32)
    full_ref[:rows, :] = jnp.where(first, own, other)
    full_ref[rows:, :] = jnp.where(first, other, own)
    lay_out(full_ref, *outs)


def finish(places, bit, own, other, lay_out, shapes, after):
    rows, width = own.shape
    return run(
        functools.partial(finish_kernel, bit, lay_out), "finish", (own, other),
        [jax.ShapeDtypeStruct(shape, F32) for shape in shapes], [whole(own.shape)] * 2,
        [whole(shape) for shape in shapes], places=places, after=after,
        estimate=cost(own.size, 16 * own.size), megabytes=16, scratch=[pltpu.VMEM((2 * rows, width), F32)],
    )


class Reduction:
    def __init__(self, order, places, pair, lay_out, shapes):
        send, self.keep = pair
        self.order, self.places = order, places
        self.lay_out, self.shapes = lay_out, shapes
        self.send = send
        bits = lax.axis_size("col").bit_length() - 1
        self.steps = ["across"] + [("down", i) for i in range(bits - 1)] + [("full", bits - 1)]
        self.steps += [("up", i) for i in reversed(range(bits - 1))] + ["end"]
        self.pending = None
        self.sent = self.result = None

    def after(self):
        return (self.order[-1].sent,) if self.order and self.order[-1] is not self else ()

    def advance(self, then=None):
        step = self.steps.pop(0)
        places, after = self.places, self.after()
        if step == "across":
            self.came = swap(self.send, "row", 1)
            self.sent = add_across(places, self.keep, self.came, after)
        else:
            if self.pending == "across":
                terms = (self.keep, self.came, swap(self.sent, "row", 2))
            else:
                terms = (self.mine, swap(self.sent, "col", 1 << self.pending[1]))
            if step == "end":
                bit = 2 + self.pending[1]
                result = finish(places, bit, *terms, self.lay_out, self.shapes, after)
                self.result = result if isinstance(result, (list, tuple)) else [result]
                self.sent = self.result[0]
            elif step[0] == "down":
                hold = () if then is None else (then.send,)
                self.sent, self.mine, *kept = add_down(places, 2 + step[1], terms, after, hold)
                if kept:
                    (then.send,) = kept
            elif self.pending[0] in ("down", "full"):
                self.sent = self.mine = add_whole(*terms, after)
            else:
                self.sent = self.mine = join(places, 2 + self.pending[1], *terms, after)
        self.pending = step
        self.order.append(self)


class Ready:
    def __init__(self, value):
        self.sent = value


def wave_numbers(width):
    def of(part):
        half = part // 2
        one = np.float32(1.0) / np.float32(10000.0) ** (
            np.arange(half, dtype=np.float32) / np.float32(half)
        )
        return [one, one]

    unit = width // 16
    return np.concatenate(of(4 * unit) + of(6 * unit) + of(6 * unit)).astype(np.float32)[None, :]


def per_device(
    pixels, timestamps, frame_count, visible, halo_reach, w_patch, b_patch, gain_one, shift_one,
    w_qkv, b_query, b_value, w_out, b_out, gain_two, shift_two, w_up, b_up, w_down, b_down,
    w_dec, b_dec, w_pix, b_pix, cotangent,
):
    tile_rows, tile_cols, frames, pix_width = pixels.shape
    model_width = w_patch.shape[1]
    tokens = tile_rows * tile_cols * frames
    ff = w_up.shape[1]
    grid_shape = (tile_rows, frames, tile_cols)
    side = tile_rows * 8 * HALO
    band = HALO * frames * tile_cols
    row_at, col_at = lax.axis_index("row"), lax.axis_index("col")
    col_bits = lax.axis_size("col").bit_length() - 1
    places = jnp.stack(
        [row_at % 2, row_at // 2] + [(col_at >> i) % 2 for i in range(col_bits)]
    ).astype(jnp.int32)

    flat_pixels = pixels.transpose(0, 2, 1, 3).reshape(tokens, pix_width)
    flat_cotangent = cotangent.transpose(0, 2, 1, 3).reshape(tokens, pix_width)
    stream_one, normed_one, high, low, tail, head, flags = embed(
        timestamps.reshape(-1), frame_count.reshape(-1), visible.transpose(2, 0, 1), flat_pixels,
        w_patch, b_patch, gain_one, shift_one, wave_numbers(model_width),
    )
    upper = rotate(high, "row", 1)
    lower = rotate(low, "row", -1)
    left = rotate(tail, "col", 1)
    right = rotate(head, "col", -1)
    query, key, value = own_qkv(normed_one, w_qkv, b_query, b_value)
    grad_dec, grad_stream, grad_mlp, sum_pix, sum_dec, sum_down = decode_back(
        flat_cotangent, w_pix, w_dec
    )
    strip_key, strip_value, strip_rows, bias = strip_kv(
        halo_reach.reshape(-1), upper, lower, left, right, flags, w_qkv, b_value
    )
    mixed, log_total = attend(query, key, value, strip_key, strip_value, bias)
    (
        pixel_out, normed_two, act, grad_pre, stream_low, decoded, attended,
        grad_two, grad_att, grad_attended, sum_up, sum_out, sum_gain_two, sum_shift_two,
    ) = mlp(
        stream_one, mixed, grad_stream, w_out, b_out, gain_two, shift_two,
        w_up, b_up, w_down, b_down, w_dec, b_dec, w_pix, b_pix,
    )
    fixed = (query, key, value, strip_key, strip_value)
    rest = (mixed, log_total, bias)
    pairs = model_width // LANES
    third = pairs // 3
    quarter = model_width // 4
    patch_rows, down_rows = pix_width // 4, ff // 4
    pix_rows, up_rows = w_dec.shape[1] // 4, quarter * (ff // model_width)
    dec_width = w_dec.shape[1]
    cut = quarter * 2 // 3
    order = []

    def lay_down(full, down_ref, pix_ref, dec_ref):
        down_ref[...] = full[:down_rows, :]
        wide(full, down_rows, pix_rows, pix_width, pix_ref)
        at, tall = down_rows + pix_rows * (pix_width // model_width), quarter - cut
        dec_ref[:cut, :] = full[at : at + cut, :dec_width]
        dec_ref[cut:, : model_width - dec_width] = full[at : at + tall, dec_width:]
        dec_ref[cut:, model_width - dec_width :] = full[at + tall : at + cut, dec_width:]

    def lay_up(full, up_ref, out_ref):
        wide(full, 0, quarter, ff, up_ref)
        out_ref[...] = full[up_rows : up_rows + quarter, :]

    def lay_middle(full, qkv_ref):
        wide(full, 0, quarter, 3 * model_width, qkv_ref)

    def lay_last(full, patch_ref, *refs):
        patch_ref[...] = full[:patch_rows, :]
        lines = -(-len(refs) // 16) * 16
        for i, ref in enumerate(refs):
            at = patch_rows + i
            size = ref.shape[1]
            ref[...] = full[at : at + 1, :size] + full[at + lines : at + lines + 1, :size]

    down = Reduction(
        order, places,
        grads_down(places, act, grad_mlp, decoded, flat_cotangent, stream_low, grad_dec), lay_down,
        [(down_rows, model_width), (pix_rows, pix_width), (quarter, dec_width)],
    )
    up = Reduction(
        order, places, grads_up(places, normed_two, grad_pre, attended, grad_att, (down.keep,)),
        lay_up, [(quarter, ff), (quarter, model_width)],
    )
    down.advance()
    back = attend_back(*fixed, grad_attended, *rest, 0, third, (), (down.sent, up.keep))
    back = attend_back(*fixed, grad_attended, *rest, third, third, back, ())
    order.append(Ready(back[0]))
    down.advance()
    up.advance()
    back = attend_back(
        *fixed, grad_attended, *rest, 2 * third, pairs - 2 * third, back, (up.sent, down.sent)
    )
    dq, dk, dv, dks, dvs, sum_query, sum_value = back
    order.append(Ready(dq))
    down.advance()
    upper_back, lower_back, left_back, right_back = strip_back(
        dks, dvs, w_qkv, band, side, (down.sent,)
    )
    from_right = rotate(left_back, "col", -1)
    from_left = rotate(right_back, "col", 1)
    from_below = rotate(upper_back, "row", -1)
    from_above = rotate(lower_back, "row", 1)
    middle = Reduction(
        order, places,
        grads_qkv(places, normed_one, strip_rows, dq, dk, dv, dks, dvs, (upper_back,)),
        lay_middle, [(quarter, 3 * model_width)],
    )
    grad_emb, sum_patch, sum_gain_one, sum_shift_one, down.sent = embed_back(
        stream_one, dq, dk, dv, w_qkv, grad_two, gain_one, from_above,
        from_below, from_left, from_right, tile_rows, frames, (down.sent,),
    )
    vectors = [
        sum_patch, sum_gain_one, sum_shift_one, sum_query, sum_value, sum_out, sum_gain_two,
        sum_shift_two, sum_up, sum_down, sum_dec, sum_pix,
    ]
    order.append(Ready(grad_emb))
    up.advance(middle)
    last = Reduction(
        order, places, grads_patch(places, flat_pixels, grad_emb, vectors, (up.sent,)),
        lay_last, [(patch_rows, model_width)] + [(1, item.shape[1] // 4) for item in vectors],
    )
    down.advance()
    middle.advance()
    last.advance()
    pixel_grad = pixel_back(grad_emb, w_patch, (last.sent,))
    order.append(Ready(pixel_grad))
    for each in (up, down, middle, last, up, down, middle, last, up, down, middle, last, up, down, middle, last, middle, last, last):
        if each.steps:
            each.advance()
    groups = (down, up, middle, last)
    while any(each.steps for each in groups):
        for each in groups:
            if each.steps:
                each.advance()
    share_down, share_pix, share_dec = down.result
    share_up, share_out = up.result
    (share_qkv,) = middle.result
    share_patch, *pieces = last.result
    pieces = [item.reshape(-1) for item in pieces]

    def to_scene(flat):
        return flat.reshape(grid_shape + (pix_width,)).transpose(0, 2, 1, 3)

    return (
        to_scene(pixel_out), to_scene(pixel_grad), share_patch, pieces[0], pieces[1], pieces[2],
        share_qkv, pieces[3], pieces[4], share_out, pieces[5], pieces[6], pieces[7], share_up,
        pieces[8], share_down, pieces[9], share_dec, pieces[10], share_pix, pieces[11],
    )


def solution(mesh):
    tiles = P("row", "col", None, None)
    return jax.shard_map(
        per_device,
        mesh=mesh,
        in_specs=(
            tiles,
            P("row", "col", None),
            P("row", "col"),
            P("row", "col", None),
            P("row", "col"),
        )
        + (P(),) * 19
        + (tiles,),
        out_specs=(
            tiles,
            tiles,
            P("row", None),
            P("row"),
            P("row"),
            P("row"),
            P("row", None),
            P("row"),
            P("row"),
            P("row", None),
            P("row"),
            P("row"),
            P("row"),
            P("row", None),
            P("row"),
            P("row", None),
            P("row"),
            P("row", None),
            P("row"),
            P("row", None),
            P("row"),
        ),
        check_vma=False,
    )
```

time: 654 us -> 411 us (0.63)
  Pallas kernels: 94.3 us -> 217 us
  matrix products: 116 us -> 0 us
  waiting for transfers between devices: 199 us -> 109 us
  other arithmetic: 82.6 us -> 1.2 us
  local copies, waits for them, and re-layouts: 105 us -> 27.8 us
    pallas_call x2 -> x44, Pallas kernels: 94.3 us -> 217 us  [the longest x38 127 us: run(): pl.pallas_call(body, grid_spec=pltpu.PrefetchScalarGridSpec(num_scalar_pr...]
    dot_general x24 -> x0, matrix products: 116 us -> none  [the longest x8 48.3 us: mat_low(): return jnp.dot(left_side, right_side, preferred_element_type=F32)]
    ppermute x32 -> x28, waiting for transfers between devices: 199 us -> 106 us  [swap(): return lax.ppermute(value, axis, [(i, i ^ stride) for i in range(count)])]
    convert_element_type x46 -> x0, other arithmetic: 38.5 us -> none  [the longest x20 14.1 us: add(): return (a.astype(F32) + b.astype(F32)).astype(BF16)]
    reshape x24 -> x0, local copies, waits for them, and re-layouts: 27 us -> none  [the longest x6 6.6 us: per_device(): item.astype(BF16).reshape(4, -1)]
    slice x32 -> x0, local copies, waits for them, and re-layouts: 23.9 us -> none  [the longest x4 3.87 us: per_device(): pieces.append(sums[at:at + item.size // 4])]
    concatenate x22 -> x0, other arithmetic: 19.6 us -> none  [the longest x4 6.94 us: with_flags(): jnp.concatenate([rows.reshape(-1, model_width), line.reshape(8, model_wid...]
    reduce_sum x9 -> x0, other arithmetic: 13.1 us -> none  [the longest x4 6.98 us: column_sum(): return jnp.sum(values, 0, dtype=F32)]
  transfers between devices with their start and end apart: 40 -> 36, of which waited for: 18 -> 14; matrix products, arithmetic and copies ran while one was open for 24% -> 0% of each run, Pallas kernels for 0% -> 30%
where the time goes in v2:
time: 411 us; the launch traced here: 404 us
  Pallas kernels  217 us (53%)
  waiting for transfers between devices  109 us (27%)
  starting transfers between devices  46.9 us (11%)
  local copies, waits for them, and re-layouts  27.8 us (7%)
    pallas_call x38, Pallas kernels, run(): pl.pallas_call(body, grid_spec=pltpu.PrefetchScalarGridSpec(num_scalar_pr...  127 us
    ppermute x28, waiting for transfers between devices, swap(): return lax.ppermute(value, axis, [(i, i ^ stride) for i in range(count)])  106 us
    pallas_call x1, Pallas kernels, attend(): pl.pallas_call(attend_kernel, grid=(pairs,), in_specs=[own, own, own, str...  38.6 us
    ppermute x28, starting transfers between devices, swap(): return lax.ppermute(value, axis, [(i, i ^ stride) for i in range(count)])  32.7 us
    pallas_call x1, Pallas kernels, mlp(): pl.pallas_call(mlp_kernel, grid=(tokens // BLOCK,), in_specs=[block(width...  32.6 us
    unnamed x142, local copies, waits for them, and re-layouts  27.7 us
    ppermute x8, starting transfers between devices, rotate(): lax.ppermute(value, axis, [(i, (i + steps) % count) for i in range(count)])  14.3 us
  transfers between devices with their start and end apart: 36, of which 14 were waited for; matrix products, arithmetic and copies ran while one was open for 0% of the time, Pallas kernels for 30%

profile of v2, /device:TPU:0, one launch (start us, length us, event | category | flops | bytes accessed | tf_op | source)
XLA Modules:
  0.0 404.5 jit_solution(17360155760545164649)
XLA Ops:
  1.3 8.1 %embed.1 = (f32[768,768]{1,0:T(8,128)}, bf16[768,768]{1,0:T(8,128)(2,1)}, bf16[392,768]{1,0:T(8,128)(2,1)}, bf16[392,768]{1,0:T(8,128)(2,1)}, bf16[72,768]{1,0:T...) custom-call(s32[6]{0:T(128)} %bitcast.48, s32[1]{0:T(128)} %bitcast.31.count_ref, s32[6,4,32]{2,1,0:T(4,128)} %bitcast.38, ...), custom_call_target="tpu_custom_call" | custom-call | flops 1811939328 | bytes 10485760 | tf_op jit(solution)/shard_map/embed/pallas_call | solution.py:184
  9.9 2.0 collective-permute-start.1
  11.9 2.3 collective-permute-start.2
  14.2 3.0 collective-permute-start.3
  19.3 3.3 own_qkv.1
  22.7 3.0 decode_back.1
  27.2 4.0 strip_kv.1
  32.4 38.6 %attend.1 = (f32[768,768]{1,0:T(8,128)S(1)}, f32[6,2,768]{2,1,0:T(2,128)S(1)}) custom-call(bf16[768,768]{1,0:T(8,128)(2,1)S(1)} %get-tuple-element.132.q_ref.refs_0_, bf16[768,768]{1,0:T(8,128)(2,1)S(1)} %get-tuple-element.133.k_ref.refs_1_, bf16[768,768]{1,0:T(8,128)(2,1)S(1)} %get-tuple-element.134.v_ref.refs_2_, ...), custom_call_target="tpu_custom_call" | custom-call | flops 15703474176 | bytes 8388608 | tf_op jit(solution)/shard_map/attend/pallas_call | solution.py:428
  72.5 32.6 %mlp.1 = (bf16[768,1536]{1,0:T(8,128)(2,1)}, bf16[768,768]{1,0:T(8,128)(2,1)S(1)}, bf16[768,3072]{1,0:T(8,128)(2,1)}, bf16[768,3072]{1,0:T(8,128)(2,1)}, bf16[76...) custom-call(f32[768,768]{1,0:T(8,128)} %get-tuple-element.130.one_re, ...), custom_call_target="tpu_custom_call" | custom-call | flops 18119393280 | bytes 41943040 | tf_op jit(solution)/shard_map/mlp/pallas_call | solution.py:621
  106.1 2.8 copy-done.47
  108.9 8.5 %grads_down.1 = (bf16[2,1152,768]{2,1,0:T(8,128)(2,1)S(1)}, bf16[2,1152,768]{2,1,0:T(8,128)(2,1)S(1)}) custom-call(s32[5]{0:T(128)S(1)} %stack.23.refs_0_, bf16[768,3072]{1,0:T(8,128)(2,1)S(1)} %copy-done.47, bf16[768,768]{1,0:T(8,128)(2,1)S(1)} %get-tuple-element.149.refs_2_, bf16[768,512]{1,0:T(8,128)(2,1)S(1)} %get-tuple-element.150.refs_3_, ...), custom_call_target="tpu_custom_call" | custom-call | flops 5435817984 | bytes 20971520 | tf_op jit(solution)/shard_map/grads_down/pallas_call | solution.py:993
  120.1 8.5 %grads_up.1 = (bf16[2,960,768]{2,1,0:T(8,128)(2,1)}, bf16[2,960,768]{2,1,0:T(8,128)(2,1)S(1)}) custom-call(s32[5]{0:T(128)S(1)} %stack.23.refs_0_, bf16[768,768]{1,0:T(8,128)(2,1)S(1)} %copy-done.49, bf16[768,3072]{1,0:T(8,128)(2,1)S(1)} %copy-done.38, bf16[768,768]{1,0:T(8,128)(2,1)S(1)} %copy-done.51, bf16[768,768]{1,0:T(8,128)(2,1)S(1)} %copy-done.52, ...), custom_call_target="tpu_custom_call" | custom-call | flops 4529848320 | bytes 16777216 | tf_op jit(solution)/shard_map/grads_up/pallas_call | solution.py:993
  129.2 2.0 add_across.4.refs_9_
  132.8 19.8 %attend_back.3 = (bf16[768,768]{1,0:T(8,128)(2,1)S(1)}, bf16[768,768]{1,0:T(8,128)(2,1)S(1)}, bf16[768,768]{1,0:T(8,128)(2,1)S(1)}, bf16[896,768]{1,0:T(8,128)(2...) custom-call(bf16[768,768]{1,0:T(8,128)(2,1)S(1)} %copy-done.54, ...), custom_call_target="tpu_custom_call" | custom-call | flops 7851737088 | bytes 6291456 | tf_op jit(solution)/shard_map/attend_back/pallas_call | solution.py:993
  154.9 19.3 %attend_back.4 = (bf16[768,768]{1,0:T(8,128)(2,1)S(1)}, bf16[768,768]{1,0:T(8,128)(2,1)S(1)}, bf16[768,768]{1,0:T(8,128)(2,1)S(1)}, bf16[896,768]{1,0:T(8,128)(2...) custom-call(bf16[768,768]{1,0:T(8,128)(2,1)S(1)} %copy-done.54, ...), custom_call_target="tpu_custom_call", output_to_operand_aliasing={{0}: (9, {}), {1}: (10, {}), {2}: (11, {}), {3}: (12, {}), ... | custom-call | flops 7851737088 | bytes 6291456 | tf_op jit(solution)/shard_map/attend_back/pallas_call | solution.py:993
  174.3 1.9 add_down.8
  177.5 1.8 add_across.5.refs_16_
  180.9 19.4 %attend_back.5 = (bf16[768,768]{1,0:T(8,128)(2,1)S(1)}, bf16[768,768]{1,0:T(8,128)(2,1)S(1)}, bf16[768,768]{1,0:T(8,128)(2,1)S(1)}, bf16[896,768]{1,0:T(8,128)(2...) custom-call(bf16[768,768]{1,0:T(8,128)(2,1)S(1)} %copy-done.55, ...), custom_call_target="tpu_custom_call", output_to_operand_aliasing={{0}: (9, {}), {1}: (10, {}), {2}: (11, {}), {3}: (12, {}), ... | custom-call | flops 7851737088 | bytes 6291456 | tf_op jit(solution)/shard_map/attend_back/pallas_call | solution.py:993
  203.6 2.3 strip_back.1
  207.0 1.7 collective-permute-start.9
  209.6 3.8 collective-permute-start.11
  214.8 7.9 %grads_qkv.1 = (bf16[2,576,768]{2,1,0:T(8,128)(2,1)S(1)}, bf16[2,576,768]{2,1,0:T(8,128)(2,1)S(1)}) custom-call(s32[5]{0:T(128)S(1)} %stack.23.refs_0_, bf16[768,768]{1,0:T(8,128)(2,1)S(1)} %copy-done.37, bf16[896,768]{1,0:T(8,128)(2,1)S(1)} %copy-done.40, bf16[768,768]{1,0:T(8,128)(2,1)S(1)} %get-tuple-element.176.refs_3_.refs_1_, ...), custom_call_target="tpu_custom_call" | custom-call | flops 4831838208 | bytes 20971520 | tf_op jit(solution)/shard_map/grads_qkv/pallas_call | solution.py:993
  222.7 2.2 collective-permute-done.8.refs_7_
  227.7 7.8 %embed_back.1 = (bf16[768,768]{1,0:T(8,128)(2,1)S(1)}, f32[1,768]{1,0:T(1,128)S(1)}, f32[1,768]{1,0:T(1,128)S(1)}, f32[1,768]{1,0:T(1,128)S(1)}, bf16[288,768]{1,0:T(8,128)(2,1)S(1)}) custom-call(f32[768,768]{1,0:T(8,128)S(1)} %copy-done.5, bf16[768,768]{1,0:T(8,128)(2,1)S(1)} %get-tuple-element.176.refs_3_.refs_1_, ...), custom_call_target="tpu_custom_call", output_to_operand_aliasing={{4}: (11, {})} | custom-call | flops 2717908992 | bytes 16777216 | tf_op jit(solution)/shard_map/embed_back/pallas_call | solution.py:993
  235.5 1.7 add_down.10
  238.1 4.1 %grads_patch.1 = (bf16[2,448,768]{2,1,0:T(8,128)(2,1)S(1)}, bf16[2,448,768]{2,1,0:T(8,128)(2,1)S(1)}) custom-call(s32[5]{0:T(128)S(1)} %stack.23.refs_0_, bf16[768,1536]{1,0:T(8,128)(2,1)S(1)} %bitcast.37, bf16[768,768]{1,0:T(8,128)(2,1)S(1)} %get-tuple-element.188.refs_4_.refs_2_.refs_0_, f32[1,768]{1,0:T(1,128)S(1)} %get-tuple-element.189.refs_3_, ...), custom_call_target="tpu_custom_call" | custom-call | flops 1811939328 | bytes 8388608 | tf_op jit(solution)/shard_map/grads_patch/pallas_call | solution.py:993
  244.4 10.4 %collective-permute-done.15.refs_1_ = bf16[288,768]{1,0:T(8,128)(2,1)S(1)} collective-permute-done((bf16[288,768]{1,0:T(8,128)(2,1)S(1)}, bf16[288,768]{1,0:T(8,128)(2,1)S(1)}, u32[]{:S(2)}, u32[]{:S(2)}) %collective-permute-start.15) | collective-permute-done | bytes 442400 | tf_op jit(solution)/shard_map/ppermute | solution.py:966
  257.3 2.6 collective-permute-start.18
  261.6 3.4 pixel_back.1.refs_3_
  265.0 1.7 copy-done.2
  267.6 11.6 %collective-permute-done.18.refs_1_ = bf16[288,768]{1,0:T(8,128)(2,1)S(1)} collective-permute-done((bf16[288,768]{1,0:T(8,128)(2,1)S(1)}, bf16[288,768]{1,0:T(8,128)(2,1)S(1)}, u32[]{:S(2)}, u32[]{:S(2)}) %collective-permute-start.18) | collective-permute-done | bytes 442400 | tf_op jit(solution)/shard_map/ppermute | solution.py:966
  282.6 9.2 %collective-permute-done.16.refs_3_ = bf16[448,768]{1,0:T(8,128)(2,1)S(1)} collective-permute-done((bf16[448,768]{1,0:T(8,128)(2,1)S(1)}, bf16[448,768]{1,0:T(8,128)(2,1)S(1)}, u32[]{:S(2)}, u32[]{:S(2)}) %collective-permute-start.16) | collective-permute-done | bytes 688160 | tf_op jit(solution)/shard_map/ppermute | solution.py:966
  292.9 5.4 %collective-permute-done.23.refs_1_ = bf16[240,768]{1,0:T(8,128)(2,1)S(1)} collective-permute-done((bf16[240,768]{1,0:T(8,128)(2,1)S(1)}, bf16[240,768]{1,0:T(8,128)(2,1)S(1)}, u32[]{:S(2)}, u32[]{:S(2)}) %collective-permute-start.23) | collective-permute-done | bytes 368672 | tf_op jit(solution)/shard_map/ppermute | solution.py:966
  299.0 2.3 collective-permute-start.26
  301.3 3.1 collective-permute-start.27
  304.9 26.4 %collective-permute-done.21.refs_2_ = bf16[288,768]{1,0:T(8,128)(2,1)S(1)} collective-permute-done((bf16[288,768]{1,0:T(8,128)(2,1)S(1)}, bf16[288,768]{1,0:T(8,128)(2,1)S(1)}, u32[]{:S(2)}, u32[]{:S(2)}) %collective-permute-start.21) | collective-permute-done | bytes 442400 | tf_op jit(solution)/shard_map/ppermute | solution.py:966
  332.1 4.8 %collective-permute-done.20.refs_2_ = bf16[224,768]{1,0:T(8,128)(2,1)S(1)} collective-permute-done((bf16[224,768]{1,0:T(8,128)(2,1)S(1)}, bf16[224,768]{1,0:T(8,128)(2,1)S(1)}, u32[]{:S(2)}, u32[]{:S(2)}) %collective-permute-start.20) | collective-permute-done | bytes 344096 | tf_op jit(solution)/shard_map/ppermute | solution.py:966
  341.3 2.5 finish.4
  343.8 9.4 %collective-permute-done.25.refs_1_ = bf16[144,768]{1,0:T(8,128)(2,1)S(1)} collective-permute-done((bf16[144,768]{1,0:T(8,128)(2,1)S(1)}, bf16[144,768]{1,0:T(8,128)(2,1)S(1)}, u32[]{:S(2)}, u32[]{:S(2)}) %collective-permute-start.25) | collective-permute-done | bytes 221216 | tf_op jit(solution)/shard_map/ppermute | solution.py:966
  354.9 4.4 %collective-permute-start.29 = (bf16[144,768]{1,0:T(8,128)(2,1)S(1)}, bf16[144,768]{1,0:T(8,128)(2,1)S(1)}, u32[]{:S(2)}, u32[]{:S(2)}) collective-permute-start(bf16[144,768]{1,0:T(8,128)(2,1)S(1)} %add_whole.12.refs_2_.refs_0_), channel_id=1, source_target_pairs={{0,4},{1,5},{2,6},{3,7},{4,0},{5,1},{6,2},{7,3},{8,12},{9,13},{10,... | collective-permute-start | bytes 663560 | tf_op jit(solution)/shard_map/ppermute | solution.py:966
  360.5 1.9 collective-permute-start.28
  362.4 8.0 %collective-permute-done.29.refs_1_ = bf16[144,768]{1,0:T(8,128)(2,1)S(1)} collective-permute-done((bf16[144,768]{1,0:T(8,128)(2,1)S(1)}, bf16[144,768]{1,0:T(8,128)(2,1)S(1)}, u32[]{:S(2)}, u32[]{:S(2)}) %collective-permute-start.29) | collective-permute-done | bytes 221216 | tf_op jit(solution)/shard_map/ppermute | solution.py:966
  370.6 1.7 collective-permute-done.28.refs_1_
  372.7 5.6 %collective-permute-done.32.refs_2_ = bf16[144,768]{1,0:T(8,128)(2,1)S(1)} collective-permute-done((bf16[144,768]{1,0:T(8,128)(2,1)S(1)}, bf16[144,768]{1,0:T(8,128)(2,1)S(1)}, u32[]{:S(2)}, u32[]{:S(2)}) %collective-permute-start.32) | collective-permute-done | bytes 221216 | tf_op jit(solution)/shard_map/ppermute | solution.py:966
  381.6 12.4 %collective-permute-done.33.refs_2_ = bf16[224,768]{1,0:T(8,128)(2,1)S(1)} collective-permute-done((bf16[224,768]{1,0:T(8,128)(2,1)S(1)}, bf16[224,768]{1,0:T(8,128)(2,1)S(1)}, u32[]{:S(2)}, u32[]{:S(2)}) %collective-permute-start.33) | collective-permute-done | bytes 344096 | tf_op jit(solution)/shard_map/ppermute | solution.py:966
  394.0 1.7 finish.5
  397.0 2.4 finish.6
  402.3 2.0 finish.7
  (213 shorter events, 56.1 us)
Async XLA Ops:
  1.3 16.7 %copy-start = (bf16[768,2304]{1,0:T(8,128)(2,1)S(1)}, bf16[768,2304]{1,0:T(8,128)(2,1)}, u32[]{:S(2)}) copy-start(bf16[768,2304]{1,0:T(8,128)(2,1)} %refs_4_.1) | copy-start | bytes 10616836
  9.4 17.7 %collective-permute-start = (bf16[392,768]{1,0:T(8,128)(2,1)}, bf16[392,768]{1,0:T(8,128)(2,1)}, u32[]{:S(2)}, u32[]{:S(2)}) collective-permute-start(bf16[392,768]{1,0:T(8,128)(2,1)} %get-tuple-element.135), channel_id=1, source_target_pairs={{0,8},{8,16},{16,24},{24,0},{1,9},{9,17},{17,25},{25,1},{2,10},{10... | collective-permute-start | bytes 1806344 | tf_op jit(solution)/shard_map/ppermute | solution.py:971
  9.9 17.2 %collective-permute-start.1 = (bf16[392,768]{1,0:T(8,128)(2,1)}, bf16[392,768]{1,0:T(8,128)(2,1)}, u32[]{:S(2)}, u32[]{:S(2)}) collective-permute-start(bf16[392,768]{1,0:T(8,128)(2,1)} %get-tuple-element.136), channel_id=1, source_target_pairs={{0,24},{8,0},{16,8},{24,16},{1,25},{9,1},{17,9},{25,17},{2,26},{10... | collective-permute-start | bytes 1806344 | tf_op jit(solution)/shard_map/ppermute | solution.py:971
  11.9 15.2 %collective-permute-start.2 = (bf16[72,768]{1,0:T(8,128)(2,1)}, bf16[72,768]{1,0:T(8,128)(2,1)}, u32[]{:S(2)}, u32[]{:S(2)}) collective-permute-start(bf16[72,768]{1,0:T(8,128)(2,1)} %get-tuple-element.137), channel_id=1, source_target_pairs={{0,1},{1,2},{2,3},{3,4},{4,5},{5,6},{6,7},{7,0},{8,9},{9,10},{10,1... | collective-permute-start | bytes 331784 | tf_op jit(solution)/shard_map/ppermute | solution.py:971
  14.2 12.9 %collective-permute-start.3 = (bf16[72,768]{1,0:T(8,128)(2,1)}, bf16[72,768]{1,0:T(8,128)(2,1)}, u32[]{:S(2)}, u32[]{:S(2)}) collective-permute-start(bf16[72,768]{1,0:T(8,128)(2,1)} %get-tuple-element.138), channel_id=1, source_target_pairs={{0,7},{1,0},{2,1},{3,2},{4,3},{5,4},{6,5},{7,6},{8,15},{9,8},{10,9... | collective-permute-start | bytes 331784 | tf_op jit(solution)/shard_map/ppermute | solution.py:971
  32.3 38.8 %copy-start.41 = (bf16[896,768]{1,0:T(8,128)(2,1)}, bf16[896,768]{1,0:T(8,128)(2,1)S(1)}, u32[]{:S(2)}) copy-start(bf16[896,768]{1,0:T(8,128)(2,1)S(1)} %get-tuple-element.140.ks_ref.refs_3_) | copy-start | bytes 4128772
  32.3 38.8 %copy-start.44 = (bf16[896,768]{1,0:T(8,128)(2,1)}, bf16[896,768]{1,0:T(8,128)(2,1)S(1)}, u32[]{:S(2)}) copy-start(bf16[896,768]{1,0:T(8,128)(2,1)S(1)} %get-tuple-element.141.vs_ref.refs_4_) | copy-start | bytes 4128772
  32.3 38.8 %copy-start.66 = (f32[8,1664]{1,0:T(8,128)}, f32[8,1664]{1,0:T(8,128)S(1)}, u32[]{:S(2)}) copy-start(f32[8,1664]{1,0:T(8,128)S(1)} %get-tuple-element.142.bias_ref.refs_8_) | copy-start | bytes 159748
  32.3 40.2 %copy-start.22 = (bf16[3072]{0:T(1024)(128)(2,1)S(1)}, bf16[3072]{0:T(1024)(128)(2,1)}, u32[]{:S(2)}) copy-start(bf16[3072]{0:T(1024)(128)(2,1)} %b_up_ref.1) | copy-start | bytes 18436
  32.3 40.2 %copy-start.23 = (bf16[1536]{0:T(1024)(128)(2,1)S(1)}, bf16[1536]{0:T(1024)(128)(2,1)}, u32[]{:S(2)}) copy-start(bf16[1536]{0:T(1024)(128)(2,1)} %b_pix_ref.1) | copy-start | bytes 9220
  32.3 40.2 %copy-start.26 = (bf16[768]{0:T(1024)(128)(2,1)S(1)}, bf16[768]{0:T(1024)(128)(2,1)}, u32[]{:S(2)}) copy-start(bf16[768]{0:T(1024)(128)(2,1)} %b_out_ref.1) | copy-start | bytes 4612
  32.3 40.1 %copy-start.27 = (bf16[768]{0:T(1024)(128)(2,1)S(1)}, bf16[768]{0:T(1024)(128)(2,1)}, u32[]{:S(2)}) copy-start(bf16[768]{0:T(1024)(128)(2,1)} %gain_ref.3) | copy-start | bytes 4612
  32.3 40.1 %copy-start.28 = (bf16[768]{0:T(1024)(128)(2,1)S(1)}, bf16[768]{0:T(1024)(128)(2,1)}, u32[]{:S(2)}) copy-start(bf16[768]{0:T(1024)(128)(2,1)} %shift_ref.3) | copy-start | bytes 4612
  32.3 40.1 %copy-start.29 = (bf16[768]{0:T(1024)(128)(2,1)S(1)}, bf16[768]{0:T(1024)(128)(2,1)}, u32[]{:S(2)}) copy-start(bf16[768]{0:T(1024)(128)(2,1)} %b_down_ref.1) | copy-start | bytes 4612
  32.4 40.1 %copy-start.30 = (bf16[512]{0:T(512)(128)(2,1)S(1)}, bf16[512]{0:T(512)(128)(2,1)}, u32[]{:S(2)}) copy-start(bf16[512]{0:T(512)(128)(2,1)} %b_dec_ref.1) | copy-start | bytes 3076
  117.4 11.7 %collective-permute-start.4 = (bf16[2,1152,768]{2,1,0:T(8,128)(2,1)S(1)}, bf16[2,1152,768]{2,1,0:T(8,128)(2,1)S(1)}, u32[]{:S(2)}, u32[]{:S(2)}) collective-permute-start(bf16[2,1152,768]{2,1,0:T(8,128)(2,1)S(1)} %get-tuple-element.154), channel_id=1, source_target_pairs={{0,8},{8,0},{16,24},{24,16},{1,9},{9,1},{17,25},{25,17},{2,10},{10... | collective-permute-start | bytes 10616840 | tf_op jit(solution)/shard_map/ppermute | solution.py:966
  128.6 48.9 %collective-permute-start.5 = (bf16[2,960,768]{2,1,0:T(8,128)(2,1)}, bf16[2,960,768]{2,1,0:T(8,128)(2,1)S(1)}, u32[]{:S(2)}, u32[]{:S(2)}) collective-permute-start(bf16[2,960,768]{2,1,0:T(8,128)(2,1)} %get-tuple-element.174), channel_id=1, source_target_pairs={{0,8},{8,0},{16,24},{24,16},{1,9},{9,1},{17,25},{25,17},{2,10},{10... | collective-permute-start | bytes 8847368 | tf_op jit(solution)/shard_map/ppermute | solution.py:966
  131.1 43.1 %collective-permute-start.6 = (bf16[1152,768]{1,0:T(8,128)(2,1)}, bf16[1152,768]{1,0:T(8,128)(2,1)S(1)}, u32[]{:S(2)}, u32[]{:S(2)}) collective-permute-start(bf16[1152,768]{1,0:T(8,128)(2,1)} %add_across.4.refs_9_), channel_id=1, source_target_pairs={{0,16},{8,24},{16,0},{24,8},{1,17},{9,25},{17,1},{25,9},{2,18},{10... | collective-permute-start | bytes 5308424 | tf_op jit(solution)/shard_map/ppermute | solution.py:966
  176.3 25.1 %collective-permute-start.7 = (bf16[576,768]{1,0:T(8,128)(2,1)S(1)}, bf16[576,768]{1,0:T(8,128)(2,1)S(1)}, u32[]{:S(2)}, u32[]{:S(2)}) collective-permute-start(bf16[576,768]{1,0:T(8,128)(2,1)S(1)} %get-tuple-element.175.refs_3_.refs_17_), channel_id=1, source_target_pairs={{0,1},{1,0},{2,3},{3,2},{4,5},{5,4},{6,7},{7,6},{8,9},{9,8},{10,11... | collective-permute-start | bytes 2654216 | tf_op jit(solution)/shard_map/ppermute | solution.py:966
  179.4 56.1 %collective-permute-start.12 = (bf16[960,768]{1,0:T(8,128)(2,1)}, bf16[960,768]{1,0:T(8,128)(2,1)S(1)}, u32[]{:S(2)}, u32[]{:S(2)}) collective-permute-start(bf16[960,768]{1,0:T(8,128)(2,1)} %add_across.5.refs_16_), channel_id=1, source_target_pairs={{0,16},{8,24},{16,0},{24,8},{1,17},{9,25},{17,1},{25,9},{2,18},{10... | collective-permute-start | bytes 4423688 | tf_op jit(solution)/shard_map/ppermute | solution.py:966
  180.9 21.5 %copy-start.1 = (bf16[768,2304]{1,0:T(8,128)(2,1)S(1)}, bf16[768,2304]{1,0:T(8,128)(2,1)}, u32[]{:S(2)}) copy-start(bf16[768,2304]{1,0:T(8,128)(2,1)} %refs_4_.1) | copy-start | bytes 10616836
  207.0 17.9 %collective-permute-start.8 = (bf16[384,768]{1,0:T(8,128)(2,1)S(1)}, bf16[384,768]{1,0:T(8,128)(2,1)S(1)}, u32[]{:S(2)}, u32[]{:S(2)}) collective-permute-start(bf16[384,768]{1,0:T(8,128)(2,1)S(1)} %get-tuple-element.184), channel_id=1, source_target_pairs={{0,8},{8,16},{16,24},{24,0},{1,9},{9,17},{17,25},{25,1},{2,10},{10... | collective-permute-start | bytes 1769480 | tf_op jit(solution)/shard_map/ppermute | solution.py:971
  207.0 18.2 %collective-permute-start.9 = (bf16[384,768]{1,0:T(8,128)(2,1)S(1)}, bf16[384,768]{1,0:T(8,128)(2,1)S(1)}, u32[]{:S(2)}, u32[]{:S(2)}) collective-permute-start(bf16[384,768]{1,0:T(8,128)(2,1)S(1)} %get-tuple-element.185.refs_8_), channel_id=1, source_target_pairs={{0,24},{8,0},{16,8},{24,16},{1,25},{9,1},{17,9},{25,17},{2,26},{10... | collective-permute-start | bytes 1769480 | tf_op jit(solution)/shard_map/ppermute | solution.py:971
  208.7 14.0 %collective-permute-start.10 = (bf16[64,768]{1,0:T(8,128)(2,1)S(1)}, bf16[64,768]{1,0:T(8,128)(2,1)S(1)}, u32[]{:S(2)}, u32[]{:S(2)}) collective-permute-start(bf16[64,768]{1,0:T(8,128)(2,1)S(1)} %get-tuple-element.186), channel_id=1, source_target_pairs={{0,1},{1,2},{2,3},{3,4},{4,5},{5,6},{6,7},{7,0},{8,9},{9,10},{10,1... | collective-permute-start | bytes 294920 | tf_op jit(solution)/shard_map/ppermute | solution.py:971
  209.6 13.1 %collective-permute-start.11 = (bf16[64,768]{1,0:T(8,128)(2,1)S(1)}, bf16[64,768]{1,0:T(8,128)(2,1)S(1)}, u32[]{:S(2)}, u32[]{:S(2)}) collective-permute-start(bf16[64,768]{1,0:T(8,128)(2,1)S(1)} %get-tuple-element.187), channel_id=1, source_target_pairs={{0,7},{1,0},{2,1},{3,2},{4,3},{5,4},{6,5},{7,6},{8,15},{9,8},{10,9... | collective-permute-start | bytes 294920 | tf_op jit(solution)/shard_map/ppermute | solution.py:971
  237.2 17.7 %collective-permute-start.14 = (bf16[2,576,768]{2,1,0:T(8,128)(2,1)S(1)}, bf16[2,576,768]{2,1,0:T(8,128)(2,1)S(1)}, u32[]{:S(2)}, u32[]{:S(2)}) collective-permute-start(bf16[2,576,768]{2,1,0:T(8,128)(2,1)S(1)} %get-tuple-element.207), channel_id=1, source_target_pairs={{0,8},{8,0},{16,24},{24,16},{1,9},{9,1},{17,25},{25,17},{2,10},{10... | collective-permute-start | bytes 5308424 | tf_op jit(solution)/shard_map/ppermute | solution.py:966
  242.2 17.7 %collective-permute-start.13 = (bf16[2,448,768]{2,1,0:T(8,128)(2,1)S(1)}, bf16[2,448,768]{2,1,0:T(8,128)(2,1)S(1)}, u32[]{:S(2)}, u32[]{:S(2)}) collective-permute-start(bf16[2,448,768]{2,1,0:T(8,128)(2,1)S(1)} %get-tuple-element.205), channel_id=1, source_target_pairs={{0,8},{8,0},{16,24},{24,16},{1,9},{9,1},{17,25},{25,17},{2,10},{10... | collective-permute-start | bytes 4128776 | tf_op jit(solution)/shard_map/ppermute | solution.py:966
  242.3 12.6 %collective-permute-start.15 = (bf16[288,768]{1,0:T(8,128)(2,1)S(1)}, bf16[288,768]{1,0:T(8,128)(2,1)S(1)}, u32[]{:S(2)}, u32[]{:S(2)}) collective-permute-start(bf16[288,768]{1,0:T(8,128)(2,1)S(1)} %get-tuple-element.209), channel_id=1, source_target_pairs={{0,2},{1,3},{2,0},{3,1},{4,6},{5,7},{6,4},{7,5},{8,10},{9,11},{10,... | collective-permute-start | bytes 1327112 | tf_op jit(solution)/shard_map/ppermute | solution.py:966
  243.9 21.1 %collective-permute-start.19 = (bf16[480,768]{1,0:T(8,128)(2,1)S(1)}, bf16[480,768]{1,0:T(8,128)(2,1)S(1)}, u32[]{:S(2)}, u32[]{:S(2)}) collective-permute-start(bf16[480,768]{1,0:T(8,128)(2,1)S(1)} %get-tuple-element.203.refs_15_.refs_2_), channel_id=1, source_target_pairs={{0,1},{1,0},{2,3},{3,2},{4,5},{5,4},{6,7},{7,6},{8,9},{9,8},{10,11... | collective-permute-start | bytes 2211848 | tf_op jit(solution)/shard_map/ppermute | solution.py:966
  255.8 25.6 %collective-permute-start.17 = (bf16[576,768]{1,0:T(8,128)(2,1)S(1)}, bf16[576,768]{1,0:T(8,128)(2,1)S(1)}, u32[]{:S(2)}, u32[]{:S(2)}) collective-permute-start(bf16[576,768]{1,0:T(8,128)(2,1)S(1)} %add_across.6.refs_3_), channel_id=1, source_target_pairs={{0,16},{8,24},{16,0},{24,8},{1,17},{9,25},{17,1},{25,9},{2,18},{10... | collective-permute-start | bytes 2654216 | tf_op jit(solution)/shard_map/ppermute | solution.py:966
  257.3 21.8 %collective-permute-start.18 = (bf16[288,768]{1,0:T(8,128)(2,1)S(1)}, bf16[288,768]{1,0:T(8,128)(2,1)S(1)}, u32[]{:S(2)}, u32[]{:S(2)}) collective-permute-start(bf16[288,768]{1,0:T(8,128)(2,1)S(1)} %add_whole.8.refs_3_.refs_0_), channel_id=1, source_target_pairs={{0,4},{1,5},{2,6},{3,7},{4,0},{5,1},{6,2},{7,3},{8,12},{9,13},{10,... | collective-permute-start | bytes 1327112 | tf_op jit(solution)/shard_map/ppermute | solution.py:966
  260.7 31.1 %collective-permute-start.16 = (bf16[448,768]{1,0:T(8,128)(2,1)S(1)}, bf16[448,768]{1,0:T(8,128)(2,1)S(1)}, u32[]{:S(2)}, u32[]{:S(2)}) collective-permute-start(bf16[448,768]{1,0:T(8,128)(2,1)S(1)} %add_across.7.refs_2_), channel_id=1, source_target_pairs={{0,16},{8,24},{16,0},{24,8},{1,17},{9,25},{17,1},{25,9},{2,18},{10... | collective-permute-start | bytes 2064392 | tf_op jit(solution)/shard_map/ppermute | solution.py:966
  279.3 19.1 %collective-permute-start.22 = (bf16[288,768]{1,0:T(8,128)(2,1)S(1)}, bf16[288,768]{1,0:T(8,128)(2,1)S(1)}, u32[]{:S(2)}, u32[]{:S(2)}) collective-permute-start(bf16[288,768]{1,0:T(8,128)(2,1)S(1)} %add_whole.9.refs_4_.refs_1_), channel_id=1, source_target_pairs={{0,2},{1,3},{2,0},{3,1},{4,6},{5,7},{6,4},{7,5},{8,10},{9,11},{10,... | collective-permute-start | bytes 1327112 | tf_op jit(solution)/shard_map/ppermute | solution.py:966
  280.0 18.2 %collective-permute-start.23 = (bf16[240,768]{1,0:T(8,128)(2,1)S(1)}, bf16[240,768]{1,0:T(8,128)(2,1)S(1)}, u32[]{:S(2)}, u32[]{:S(2)}) collective-permute-start(bf16[240,768]{1,0:T(8,128)(2,1)S(1)} %get-tuple-element.211.refs_2_), channel_id=1, source_target_pairs={{0,2},{1,3},{2,0},{3,1},{4,6},{5,7},{6,4},{7,5},{8,10},{9,11},{10,... | collective-permute-start | bytes 1105928 | tf_op jit(solution)/shard_map/ppermute | solution.py:966
  299.0 42.3 %collective-permute-start.26 = (bf16[576,768]{1,0:T(8,128)(2,1)S(1)}, bf16[576,768]{1,0:T(8,128)(2,1)S(1)}, u32[]{:S(2)}, u32[]{:S(2)}) collective-permute-start(bf16[576,768]{1,0:T(8,128)(2,1)S(1)} %join.4.refs_3_.refs_1_), channel_id=1, source_target_pairs={{0,1},{1,0},{2,3},{3,2},{4,5},{5,4},{6,7},{7,6},{8,9},{9,8},{10,11... | collective-permute-start | bytes 2654216 | tf_op jit(solution)/shard_map/ppermute | solution.py:966
  301.3 30.0 %collective-permute-start.21 = (bf16[288,768]{1,0:T(8,128)(2,1)S(1)}, bf16[288,768]{1,0:T(8,128)(2,1)S(1)}, u32[]{:S(2)}, u32[]{:S(2)}) collective-permute-start(bf16[288,768]{1,0:T(8,128)(2,1)S(1)} %get-tuple-element.212.refs_4_), channel_id=1, source_target_pairs={{0,1},{1,0},{2,3},{3,2},{4,5},{5,4},{6,7},{7,6},{8,9},{9,8},{10,11... | collective-permute-start | bytes 1327112 | tf_op jit(solution)/shard_map/ppermute | solution.py:966
  301.3 36.3 %collective-permute-start.27 = (bf16[240,768]{1,0:T(8,128)(2,1)S(1)}, bf16[240,768]{1,0:T(8,128)(2,1)S(1)}, u32[]{:S(2)}, u32[]{:S(2)}) collective-permute-start(bf16[240,768]{1,0:T(8,128)(2,1)S(1)} %add_whole.10.refs_3_.refs_0_), channel_id=1, source_target_pairs={{0,4},{1,5},{2,6},{3,7},{4,0},{5,1},{6,2},{7,3},{8,12},{9,13},{10,... | collective-permute-start | bytes 1105928 | tf_op jit(solution)/shard_map/ppermute | solution.py:966
  304.4 32.4 %collective-permute-start.20 = (bf16[224,768]{1,0:T(8,128)(2,1)S(1)}, bf16[224,768]{1,0:T(8,128)(2,1)S(1)}, u32[]{:S(2)}, u32[]{:S(2)}) collective-permute-start(bf16[224,768]{1,0:T(8,128)(2,1)S(1)} %get-tuple-element.214.refs_2_), channel_id=1, source_target_pairs={{0,1},{1,0},{2,3},{3,2},{4,5},{5,4},{6,7},{7,6},{8,9},{9,8},{10,11... | collective-permute-start | bytes 1032200 | tf_op jit(solution)/shard_map/ppermute | solution.py:966
  337.7 21.6 %collective-permute-start.30 = (bf16[240,768]{1,0:T(8,128)(2,1)S(1)}, bf16[240,768]{1,0:T(8,128)(2,1)S(1)}, u32[]{:S(2)}, u32[]{:S(2)}) collective-permute-start(bf16[240,768]{1,0:T(8,128)(2,1)S(1)} %add_whole.11.refs_3_.refs_1_), channel_id=1, source_target_pairs={{0,2},{1,3},{2,0},{3,1},{4,6},{5,7},{6,4},{7,5},{8,10},{9,11},{10,... | collective-permute-start | bytes 1105928 | tf_op jit(solution)/shard_map/ppermute | solution.py:966
  339.3 13.9 %collective-permute-start.25 = (bf16[144,768]{1,0:T(8,128)(2,1)S(1)}, bf16[144,768]{1,0:T(8,128)(2,1)S(1)}, u32[]{:S(2)}, u32[]{:S(2)}) collective-permute-start(bf16[144,768]{1,0:T(8,128)(2,1)S(1)} %get-tuple-element.217.refs_3_), channel_id=1, source_target_pairs={{0,2},{1,3},{2,0},{3,1},{4,6},{5,7},{6,4},{7,5},{8,10},{9,11},{10,... | collective-permute-start | bytes 663560 | tf_op jit(solution)/shard_map/ppermute | solution.py:966
  339.8 19.4 %collective-permute-start.24 = (bf16[112,768]{1,0:T(8,128)(2,1)S(1)}, bf16[112,768]{1,0:T(8,128)(2,1)S(1)}, u32[]{:S(2)}, u32[]{:S(2)}) collective-permute-start(bf16[112,768]{1,0:T(8,128)(2,1)S(1)} %get-tuple-element.219.refs_2_), channel_id=1, source_target_pairs={{0,2},{1,3},{2,0},{3,1},{4,6},{5,7},{6,4},{7,5},{8,10},{9,11},{10,... | collective-permute-start | bytes 516104 | tf_op jit(solution)/shard_map/ppermute | solution.py:966
  354.9 15.5 %collective-permute-start.29 = (bf16[144,768]{1,0:T(8,128)(2,1)S(1)}, bf16[144,768]{1,0:T(8,128)(2,1)S(1)}, u32[]{:S(2)}, u32[]{:S(2)}) collective-permute-start(bf16[144,768]{1,0:T(8,128)(2,1)S(1)} %add_whole.12.refs_2_.refs_0_), channel_id=1, source_target_pairs={{0,4},{1,5},{2,6},{3,7},{4,0},{5,1},{6,2},{7,3},{8,12},{9,13},{10,... | collective-permute-start | bytes 663560 | tf_op jit(solution)/shard_map/ppermute | solution.py:966
  359.9 35.8 %collective-permute-start.35 = (bf16[480,768]{1,0:T(8,128)(2,1)S(1)}, bf16[480,768]{1,0:T(8,128)(2,1)S(1)}, u32[]{:S(2)}, u32[]{:S(2)}) collective-permute-start(bf16[480,768]{1,0:T(8,128)(2,1)S(1)} %join.5.refs_2_.refs_1_), channel_id=1, source_target_pairs={{0,1},{1,0},{2,3},{3,2},{4,5},{5,4},{6,7},{7,6},{8,9},{9,8},{10,11... | collective-permute-start | bytes 2211848 | tf_op jit(solution)/shard_map/ppermute | solution.py:966
  360.5 11.8 %collective-permute-start.28 = (bf16[112,768]{1,0:T(8,128)(2,1)S(1)}, bf16[112,768]{1,0:T(8,128)(2,1)S(1)}, u32[]{:S(2)}, u32[]{:S(2)}) collective-permute-start(bf16[112,768]{1,0:T(8,128)(2,1)S(1)} %add_whole.13.refs_3_.refs_0_), channel_id=1, source_target_pairs={{0,4},{1,5},{2,6},{3,7},{4,0},{5,1},{6,2},{7,3},{8,12},{9,13},{10,... | collective-permute-start | bytes 516104 | tf_op jit(solution)/shard_map/ppermute | solution.py:966
  370.5 7.8 %collective-permute-start.32 = (bf16[144,768]{1,0:T(8,128)(2,1)S(1)}, bf16[144,768]{1,0:T(8,128)(2,1)S(1)}, u32[]{:S(2)}, u32[]{:S(2)}) collective-permute-start(bf16[144,768]{1,0:T(8,128)(2,1)S(1)} %add_whole.14.refs_2_.refs_1_), channel_id=1, source_target_pairs={{0,2},{1,3},{2,0},{3,1},{4,6},{5,7},{6,4},{7,5},{8,10},{9,11},{10,... | collective-permute-start | bytes 663560 | tf_op jit(solution)/shard_map/ppermute | solution.py:966
  372.3 7.8 %collective-permute-start.31 = (bf16[112,768]{1,0:T(8,128)(2,1)S(1)}, bf16[112,768]{1,0:T(8,128)(2,1)S(1)}, u32[]{:S(2)}, u32[]{:S(2)}) collective-permute-start(bf16[112,768]{1,0:T(8,128)(2,1)S(1)} %add_whole.15.refs_3_.refs_1_), channel_id=1, source_target_pairs={{0,2},{1,3},{2,0},{3,1},{4,6},{5,7},{6,4},{7,5},{8,10},{9,11},{10,... | collective-permute-start | bytes 516104 | tf_op jit(solution)/shard_map/ppermute | solution.py:966
  378.9 21.8 %collective-permute-start.34 = (bf16[288,768]{1,0:T(8,128)(2,1)S(1)}, bf16[288,768]{1,0:T(8,128)(2,1)S(1)}, u32[]{:S(2)}, u32[]{:S(2)}) collective-permute-start(bf16[288,768]{1,0:T(8,128)(2,1)S(1)} %join.6.refs_3_.refs_1_), channel_id=1, source_target_pairs={{0,1},{1,0},{2,3},{3,2},{4,5},{5,4},{6,7},{7,6},{8,9},{9,8},{10,11... | collective-permute-start | bytes 1327112 | tf_op jit(solution)/shard_map/ppermute | solution.py:966
  380.7 13.3 %collective-permute-start.33 = (bf16[224,768]{1,0:T(8,128)(2,1)S(1)}, bf16[224,768]{1,0:T(8,128)(2,1)S(1)}, u32[]{:S(2)}, u32[]{:S(2)}) collective-permute-start(bf16[224,768]{1,0:T(8,128)(2,1)S(1)} %join.7.refs_1_), channel_id=1, source_target_pairs={{0,1},{1,0},{2,3},{3,2},{4,5},{5,4},{6,7},{7,6},{8,9},{9,8},{10,11... | collective-permute-start | bytes 1032200 | tf_op jit(solution)/shard_map/ppermute | solution.py:966
  (59 other events, 298.2 us)
